TPU v7x, 256 devices: a whole 4x4x8 slice. The times are simulated.
256 devices in a mesh: site: 4 (over x), chan: 32 (over z, y), grp: 2 (over core).
Axes of the slice: x: 4, y: 4, z: 8, core: 2. Of those that a mesh axis runs over, the one named last changes fastest.
Arguments:
- voltages: bfloat16 [2, 65536, 3072], P(None, 'chan', ('site', 'grp')), may hold values from -6 to 6
- taps: float32 [8, 32], replicated, may hold values from -0.375 to 0.375
- sections: int32 [4, 2], replicated, may hold values from 0 to 768, as said below
- tile_list: int32 [2, 68, 2], replicated, may hold values from 0 to 15, as said below
Outputs:
- visibility: float32 [4, 32, 136, 2, 128, 128], P('site', 'chan', 'grp')
Inputs may be any that keep to these rules, and one draw needn't show every extreme that they name: `sections`: the live counts sum to 2048; each is at least 128 and at most 768, one site has exactly 768; each first live column plus its count is at most 768. `tile_list`: every pair (p, q) with 0 <= p <= q < 16 stands exactly once in the whole list.
All inputs are finite; a program needn't handle non-finite values.
Results may differ from a plain program's by a relative error of at most 0.0033.
Values may be sent and summed in bfloat16 or wider, within the bound.
No kernel may reach another device: no remote copies, remote signals or barrier semaphores. Data moves between devices by JAX's collectives and lax.ppermute only.
A program may use at most 128 MiB of HBM per device.

v0:
```python
import jax
import jax.numpy as jnp
from jax import lax
from jax.sharding import PartitionSpec as P

NIN = 2048
PANEL = 128


slots_per_turn = 8


def from_behind(value, axis, steps):
    count = lax.axis_size(axis)
    leading, last = (max(0, -steps), min(count, count - steps))
    return lax.ppermute(value, axis, [(source, source + steps) for source in range(leading, last)])


def dft_table(chan_count):
    positions = jnp.arange(chan_count, dtype=jnp.int32)
    products = positions[:, None] * positions[None, :] % chan_count
    phases = products.astype(jnp.float32) * (2.0 * jnp.pi / chan_count)
    cosine_part = jnp.cos(phases)
    sine_part = jnp.sin(phases)
    from_real = jnp.stack([cosine_part, -sine_part], axis=1)
    from_imag = jnp.stack([sine_part, cosine_part], axis=1)
    return jnp.stack([from_real, from_imag], axis=0)


def filter_frames(history, taps, transform, frames):
    tap_count = taps.shape[0]
    filtered = jnp.zeros(
        (history.shape[0], frames, history.shape[2], history.shape[3]), jnp.float32
    )
    for tap_index in range(tap_count):
        first_frame = tap_count - 1 - tap_index
        filtered = (
            filtered
            + taps[tap_index][None, None, :, None] * history[:, first_frame : first_frame + frames]
        )
    spectra = jnp.einsum("qfkr,qkpm->pmfr", filtered, transform, precision=lax.Precision.HIGHEST)
    return spectra.astype(jnp.bfloat16)


def compact_inputs(spectra, sections, half_cols):
    site_total = sections.shape[0]
    row_width = site_total * half_cols
    group_total = spectra.shape[3] // row_width
    section_cols = group_total * half_cols
    counts = sections[:, 0]
    starts = sections[:, 1]
    offsets = jnp.cumsum(counts) - counts
    lead = spectra.shape[:3]
    buffer = jnp.zeros(lead + (NIN + section_cols,), spectra.dtype)
    blank = jnp.zeros(lead + (section_cols,), spectra.dtype)
    for site_id in range(site_total):
        pieces = [
            spectra[
                ..., g * row_width + site_id * half_cols : g * row_width + (site_id + 1) * half_cols
            ]
            for g in range(group_total)
        ]
        padded = jnp.concatenate(pieces + [blank], axis=3)
        live = lax.dynamic_slice_in_dim(padded, starts[site_id], section_cols, 3)
        buffer = lax.dynamic_update_slice_in_dim(buffer, live, offsets[site_id], 3)
    return buffer[..., :NIN]


def correlate(compact, slot_pairs):
    chan_local = compact.shape[1]
    slot_total = slot_pairs.shape[0]
    turns = -(-slot_total // slots_per_turn)
    filler = jnp.broadcast_to(slot_pairs[:1], (turns * slots_per_turn - slot_total, 2))
    grouped = jnp.concatenate([slot_pairs, filler], axis=0).reshape(turns, slots_per_turn, 2)

    def one_turn(turn_pairs):
        values = []
        for slot_index in range(slots_per_turn):
            left_panel = lax.dynamic_slice_in_dim(
                compact, turn_pairs[slot_index, 0] * PANEL, PANEL, 3
            )
            right_panel = lax.dynamic_slice_in_dim(
                compact, turn_pairs[slot_index, 1] * PANEL, PANEL, 3
            )
            gram_block = jnp.einsum(
                "qcfu,rcfv->cqruv", left_panel, right_panel, preferred_element_type=jnp.float32
            )
            real_part = gram_block[:, 0, 0] + gram_block[:, 1, 1]
            imag_part = gram_block[:, 1, 0] - gram_block[:, 0, 1]
            values.append(jnp.stack([real_part, imag_part], axis=1))
        return jnp.stack(values, axis=0)

    tile_values = lax.map(one_turn, grouped)
    tile_values = tile_values.reshape(turns * slots_per_turn, chan_local, 2, PANEL, PANEL)[
        :slot_total
    ]
    return jnp.moveaxis(tile_values, 0, 1)


def per_device(voltages, taps, sections, tile_list):
    tap_count, chan_count = taps.shape
    local_frames = voltages.shape[1] // chan_count
    half_cols = voltages.shape[2]
    signal = voltages.reshape(2, local_frames, chan_count, half_cols)
    last_frames = signal[:, local_frames - (tap_count - 1) :]
    earlier = from_behind(last_frames, "chan", 1)
    history = jnp.concatenate([earlier, signal], axis=1).astype(jnp.float32)
    spectra = filter_frames(history, taps, dft_table(chan_count), local_frames)
    blocked = lax.all_to_all(
        lax.all_to_all(spectra, "chan", split_axis=1, concat_axis=2, tiled=True),
        "site",
        split_axis=2,
        concat_axis=3,
        tiled=True,
    )
    gathered = lax.all_gather(blocked, "grp", axis=3, tiled=True)
    own_pairs = lax.dynamic_index_in_dim(tile_list, lax.axis_index("grp"), 0, keepdims=False)
    tile_values = correlate(compact_inputs(gathered, sections, half_cols), own_pairs)
    block_frames = gathered.shape[2]
    return (tile_values / block_frames)[None]


def solution(mesh):
    in_specs = (P(None, "chan", ("site", "grp")), P(), P(), P())
    out_specs = P("site", "chan", "grp", None, None, None)
    return jax.shard_map(
        per_device, mesh=mesh, in_specs=in_specs, out_specs=out_specs, check_vma=False
    )
```

profile of v0, /device:TPU:1, one launch (start us, length us, event | category | flops | bytes accessed | tf_op | source)
XLA Modules:
  0.0 554.3 jit_solution(6160222560364801349)
XLA Ops:
  7.6 4.0 collective-permute-start
  12.8 5.5 collective-permute-done
  18.4 5.8 %maximum_convert_fusion = f32[2,71,32,384]{3,2,0,1:T(8,128)} fusion(bf16[2,7,32,384]{3,2,0,1:T(8,128)(2,1)S(1)} %collective-permute-done, bf16[2,64,32,384]{3,2,1,0:T(8,128)(2,1)} %bitcast.398), kind=kLoop, calls=%fused_computation.120 | loop fusion | flops 6979584 | bytes 10469376 | tf_op jit(solution)/shard_map/convert_element_type | solution.py:107
  24.2 22.5 %bitcast_convert_fusion = bf16[2,32,64,384]{3,1,2,0:T(8,128)(2,1)} fusion(f32[2,71,32,384]{3,2,0,1:T(8,128)} %maximum_convert_fusion, f32[32]{0:T(128)S(1)} %get-tuple-element.94, f32[32]{0:T(128)S(1)} %get-tuple-element.95, f32[32]{0:T(128)S(1)} %get-tuple-element.89, f32[32]{0:T(128)S(1)} %get-tuple-element.90, f32[32]{0:T(128)S(1)} %get-tuple-element.91, ...), kind=kOutput, calls=%fused_computation.119 | convolution fusion | flops 1233129472 | bytes 53494784 | tf_op jit(solution)/shard_map/qfkr,qkpm->pmfr/dot_general | solution.py:41
  46.6 3.0 copy.101
  49.6 83.2 %all_to_all.30 = bf16[2,32,64,384]{3,2,0,1:T(8,128)(2,1)S(1)} all-to-all(bf16[2,32,64,384]{3,2,0,1:T(8,128)(2,1)S(1)} %copy.101), channel_id=1, replica_groups=mesh['site'=4,'chan'=32,'grp'=2] {'chan'}, dimensions={1} | all-to-all | bytes 6291456 | tf_op jit(solution)/shard_map/all_to_all | solution.py:110
  133.3 30.1 %copy.103 = bf16[2,1,2048,384]{3,0,1,2:T(2,128)(2,1)S(1)} copy(bf16[2,1,2048,384]{3,2,0,1:T(8,128)(2,1)S(1)} %bitcast.394) | data formatting | bytes 6291456 | tf_op jit(solution)/shard_map/all_to_all | solution.py:110
  163.4 37.6 %all_to_all.31 = bf16[2,1,2048,384]{3,0,1,2:T(2,128)(2,1)S(1)} all-to-all(bf16[2,1,2048,384]{3,0,1,2:T(2,128)(2,1)S(1)} %copy.103), channel_id=1, replica_groups=mesh['site'=4,'chan'=32,'grp'=2] {'site'}, dimensions={2} | all-to-all | bytes 6291456 | tf_op jit(solution)/shard_map/all_to_all | solution.py:109
  201.0 2.1 copy.104
  203.1 4.7 copy.105
  225.1 6.2 %all-gather.2.cloned.1.call-done = bf16[2,1,512,3072]{2,3,0,1:T(8,128)(2,1)} async-done(((bf16[2,1,512,1536]{2,3,0,1:T(8,128)(2,1)}), bf16[2,1,512,3072]{2,3,0,1:T(8,128)(2,1)}) %all-gather.2.cloned.1.call-update) | async-done | bytes 6291472 | tf_op jit(solution)/shard_map/all_gather | solution.py:116
  231.3 4.8 fusion.113
  236.1 2.3 copy.110
  238.4 2.3 copy.111
  240.7 2.3 copy.108
  243.0 2.3 copy.109
  249.2 2.5 fusion.95
  251.8 3.8 fusion.97
  255.5 3.8 fusion.99
  259.3 2.9 broadcast_in_dim.26
  262.2 15.1 %dynamic_update_slice.16 = bf16[2,1,512,2816]{3,2,0,1:T(8,128)(2,1)} dynamic-update-slice(bf16[2,1,512,2816]{3,2,0,1:T(8,128)(2,1)} %broadcast_in_dim.26, bf16[2,1,512,768]{3,2,0,1:T(8,128)(2,1)} %fusion.99, s32[]{:T(128)} %constant.61.clone.1, s32[]{:T(128)} %constant.61.clone.1, s32[]{:T(128)} %constant.61.clone.1, s32[]{:T(128)S(6)} %select_n.107) | dynamic-update-slice | bytes 3145732 | tf_op jit(solution)/shard_map/dynamic_update_slice | solution.py:65
  277.4 16.9 %dynamic_update_slice.17 = bf16[2,1,512,2816]{3,2,0,1:T(8,128)(2,1)} dynamic-update-slice(bf16[2,1,512,2816]{3,2,0,1:T(8,128)(2,1)} %dynamic_update_slice.16, bf16[2,1,512,768]{3,2,0,1:T(8,128)(2,1)} %fusion.97, s32[]{:T(128)} %constant.61.clone.1, s32[]{:T(128)} %constant.61.clone.1, s32[]{:T(128)} %constant.61.clone.1, s32[]{:T(128)S(6)} %select_n.109) | dynamic-update-slice | bytes 3145732 | tf_op jit(solution)/shard_map/dynamic_update_slice | solution.py:65
  294.2 16.1 %dynamic_update_slice.18 = bf16[2,1,512,2816]{3,2,0,1:T(8,128)(2,1)} dynamic-update-slice(bf16[2,1,512,2816]{3,2,0,1:T(8,128)(2,1)} %dynamic_update_slice.17, bf16[2,1,512,768]{3,2,0,1:T(8,128)(2,1)S(1)} %fusion.95, s32[]{:T(128)} %constant.61.clone.1, s32[]{:T(128)} %constant.61.clone.1, s32[]{:T(128)} %constant.61.clone.1, s32[]{:T(128)S(6)} %select_n.111) | dynamic-update-slice | bytes 3145732 | tf_op jit(solution)/shard_map/dynamic_update_slice | solution.py:65
  311.6 14.5 %dynamic_update_slice.19 = bf16[2,1,512,2816]{3,2,0,1:T(8,128)(2,1)} dynamic-update-slice(bf16[2,1,512,2816]{3,2,0,1:T(8,128)(2,1)} %dynamic_update_slice.18, bf16[2,1,512,768]{3,2,0,1:T(8,128)(2,1)S(1)} %fusion.93, s32[]{:T(128)} %constant.61.clone.1, s32[]{:T(128)} %constant.61.clone.1, s32[]{:T(128)} %constant.61.clone.1, s32[]{:T(128)S(6)} %select_n.113) | dynamic-update-slice | bytes 3145732 | tf_op jit(solution)/shard_map/dynamic_update_slice | solution.py:65
  326.1 4.9 slice.355
  331.0 207.6 %while.10 = (s32[]{:T(128)}, f32[9,8,1,2,128,128]{5,4,3,1,0,2:T(8,128)}, s32[9,8,2]{1,0,2:T(8,128)S(1)}, bf16[2,1,512,2048]{3,2,0,1:T(8,128)(2,1)}, s32[]{:T(128)}, /*index=5*/s32[1,1]{0,1:T(1,128)}, s32[]{:T(128)}, s32[]{:T(128)}) while((s32[]{:T(128)}, f32[9,8,1,2,128,128]{5,4,3,1,0,2:T(8,128)}, s32[9,8,2]{1,0,2:T(8,128)S(1)}, ...), condition=%wide.region_2.3_spmd, body=%wide.region_1.2_spmd.sunk | while | flops 537395200 | bytes 15730297 | solution.py:93
  338.1 1.3 convolution_bitcast_fusion.18
  340.8 1.4 convolution_bitcast_fusion.19
  343.4 1.3 convolution_bitcast_fusion.20
  346.1 1.3 convolution_bitcast_fusion.21
  361.2 1.3 convolution_bitcast_fusion.18
  366.4 1.3 convolution_bitcast_fusion.20
  369.1 1.3 convolution_bitcast_fusion.21
  386.9 1.3 convolution_bitcast_fusion.19
  392.1 1.3 convolution_bitcast_fusion.21
  397.4 1.3 convolution_bitcast_fusion.23
  412.5 1.3 convolution_bitcast_fusion.20
  415.2 1.3 convolution_bitcast_fusion.21
  420.4 1.3 convolution_bitcast_fusion.23
  435.5 1.3 convolution_bitcast_fusion.20
  438.2 1.3 convolution_bitcast_fusion.21
  456.0 1.3 convolution_bitcast_fusion.19
  481.6 1.3 convolution_bitcast_fusion.20
  486.9 1.3 convolution_bitcast_fusion.22
  522.6 1.3 convolution_bitcast_fusion.18
  525.2 1.3 convolution_bitcast_fusion.19
  530.5 1.3 convolution_bitcast_fusion.21
  538.6 8.9 %fusion.65 = f32[1,1,68,2,128,128]{5,4,3,2,1,0:T(8,128)} fusion(f32[72,1,2,128,128]{4,3,2,0,1:T(8,128)} %bitcast.396), kind=kLoop, calls=%fused_computation.101 | loop fusion | flops 2228224 | bytes 17825792 | tf_op jit(solution)/shard_map/div | solution.py:120
  (277 shorter events, 97.6 us)
Async XLA Ops:
  6.5 212.9 %copy-start = (s32[2,68,2]{1,2,0:T(2,128)S(1)}, s32[2,68,2]{1,2,0:T(2,128)}, u32[]{:S(2)}) copy-start(s32[2,68,2]{1,2,0:T(2,128)} %param.9) | copy-start | bytes 3268
  6.5 224.8 %all-gather.2.cloned.1.call-start = ((), (), s32[]{:S(2)}) async-start(), calls=%async_computation.2 | async-start | bytes 9437184 | tf_op jit(solution)/shard_map/all_gather | solution.py:116
  7.6 10.8 %collective-permute-start = (bf16[2,7,32,384]{3,2,0,1:T(8,128)(2,1)S(1)}, bf16[2,7,32,384]{3,2,0,1:T(8,128)(2,1)S(1)}, u32[]{:S(2)}, u32[]{:S(2)}) collective-permute-start(bf16[2,7,32,384]{3,2,0,1:T(8,128)(2,1)S(1)} %copy.140), channel_id=1, source_target_pairs={{0,2},{2,4},{4,6},{6,8},{8,10},{10,12},{12,14},{14,16},{16,18},{18... | collective-permute-start | bytes 1032200 | tf_op jit(solution)/shard_map/ppermute | solution.py:16
  203.1 4.7 copy-start.3
  203.1 10.6 %slice-start = ((s32[4,2]{0,1:T(2,128)}), s32[4,1]{0,1:T(1,128)S(1)}, s32[]{:S(2)}) async-start(s32[4,2]{0,1:T(2,128)} %param.8), calls=%async_computation.3 | async-start | bytes 1024 | tf_op jit(solution)/shard_map/slice | solution.py:50
  262.2 48.1 %copy-start.2 = (bf16[2,1,512,384]{3,2,0,1:T(8,128)(2,1)S(1)}, bf16[2,1,512,384]{3,2,0,1:T(8,128)(2,1)}, u32[]{:S(2)}) copy-start(bf16[2,1,512,384]{3,2,0,1:T(8,128)(2,1)} %copy.113) | copy-start | bytes 2359300
  538.6 8.9 %copy-start.1 = (s32[2,68,2]{1,2,0:T(2,128)S(1)}, s32[2,68,2]{1,2,0:T(2,128)}, u32[]{:S(2)}) copy-start(s32[2,68,2]{1,2,0:T(2,128)} %param.9) | copy-start | bytes 3268
Sparse Core Ops, SparseCore 0:
  207.9 23.4 all-gather.1
where the time goes:
time: 560 us; the launch traced here: 554 us
  local copies, waits for them, and re-layouts  151 us (27%)
  blocking collectives  121 us (22%)
  matrix products  117 us (21%)
  loops' own time  92.2 us (16%)
  between operations  28.9 us (5%)
  other arithmetic  28.5 us (5%)
  waiting for transfers between devices  11.7 us (2%)
    dot_general x72, matrix products, one_turn(): jnp.einsum('qcfu,rcfv->cqruv', left_panel, right_panel, preferred_element...  94.2 us
    another operation x1, loops' own time, correlate(): tile_values = lax.map(one_turn, grouped)  92.2 us
    all_to_all x1, blocking collectives, per_device(): lax.all_to_all(spectra, 'chan', split_axis=1, concat_axis=2, tiled=True)  83.2 us
    dynamic_update_slice x4, local copies, waits for them, and re-layouts, compact_inputs(): buffer = lax.dynamic_update_slice_in_dim(buffer, live, offsets[site_id], 3)  62.7 us
    all_to_all x1, blocking collectives, per_device(): lax.all_to_all(lax.all_to_all(spectra, 'chan', split_axis=1, concat_axis=...  37.6 us
    all_to_all x2, local copies, waits for them, and re-layouts, per_device(): lax.all_to_all(spectra, 'chan', split_axis=1, concat_axis=2, tiled=True)  30.5 us
    dot_general x1, matrix products, filter_frames(): jnp.einsum('qfkr,qkpm->pmfr', filtered, transform, precision=lax.Precisio...  22.5 us
    slice x9, local copies, waits for them, and re-layouts, compact_inputs(): spectra[..., g * row_width + site_id * half_cols:g * row_width + (site_id...  17.9 us
  transfers between devices with their start and end apart: 2, of which 2 were waited for; matrix products, arithmetic and copies ran while one was open for 1% of the time, Pallas kernels for 0%

commit v1 on v0

v1 whole, which is shorter than its diff:
```python
import functools

import jax
import jax.numpy as jnp
import numpy as np
from jax import lax
from jax.experimental import pallas as pl
from jax.experimental.pallas import tpu as pltpu
from jax.sharding import PartitionSpec as P


NIN = 2048
PANEL = 128
PANELS = NIN // PANEL
NCHAN = 32
N_SITE = 4
LOCAL = 64
BLOCKS = 8
FB = LOCAL * BLOCKS
CAP = 768
HALF = 384
TSLOT = 68
TIMES = 4
ROUNDS = 8
SINGLE = 8
PER_STEP = 4
STRIP = 16
GROUP = 8


def trig_rows():
    k = np.arange(NCHAN)
    rows = [np.cos(2.0 * np.pi * (m * k % NCHAN) / NCHAN) for m in range(17)]
    rows += [np.sin(2.0 * np.pi * (m * k % NCHAN) / NCHAN) for m in range(1, 16)]
    return np.tile(np.stack(rows), (1, 2 * GROUP)).astype(np.float32)


def tap_rows(taps):
    flipped = taps[::-1]
    rows = [jnp.pad(flipped, ((j + 1, GROUP - 1 - j), (0, 0))) for j in range(GROUP)]
    return jnp.stack(rows).reshape(GROUP, 2 * GROUP * NCHAN)


def filter_body(slot_of, has_halo, trig_ref, tap_ref, before_ref, now_ref, *rest):
    out_ref, high_ref, low_ref = rest[-3:]

    @pl.when(pl.program_id(0) == 0)
    def _():
        full = (trig_ref[...][:, None, :] * tap_ref[...][None]).reshape(
            NCHAN * GROUP, 2 * GROUP * NCHAN
        )
        high = full.astype(jnp.bfloat16)
        high_ref[...] = high
        low_ref[...] = (full - high.astype(jnp.float32)).astype(jnp.bfloat16)

    step = GROUP * NCHAN
    products = []
    for sub in range(STRIP // GROUP):
        pair = []
        for part in range(2):
            now = now_ref[part]
            if sub == 0:
                before = before_ref[part]
                if has_halo:
                    before = jnp.where(pl.program_id(0) == 0, rest[0][part], before)
                frames = jnp.concatenate([before, now[:step]], axis=0)
            else:
                frames = now
            pair.append(
                jnp.dot(high_ref[...], frames, preferred_element_type=jnp.float32)
                + jnp.dot(low_ref[...], frames, preferred_element_type=jnp.float32)
            )
        products.append(pair)

    def rows(part, index):
        return jnp.concatenate(
            [pair[part][index * GROUP : (index + 1) * GROUP] for pair in products], axis=0
        )

    for m in range(17):
        cos_re, cos_im = rows(0, m), rows(1, m)
        if m in (0, 16):
            out_ref[slot_of(m), 0] = cos_re.astype(jnp.bfloat16)
            out_ref[slot_of(m), 1] = cos_im.astype(jnp.bfloat16)
        else:
            sin_re, sin_im = rows(0, 16 + m), rows(1, 16 + m)
            out_ref[slot_of(m), 0] = (cos_re + sin_im).astype(jnp.bfloat16)
            out_ref[slot_of(m), 1] = (cos_im - sin_re).astype(jnp.bfloat16)
            out_ref[slot_of(NCHAN - m), 0] = (cos_re - sin_im).astype(jnp.bfloat16)
            out_ref[slot_of(NCHAN - m), 1] = (cos_im + sin_re).astype(jnp.bfloat16)


def filter_call(trig, tap_table, voltages, halo, begin, strips, slot_of):
    rows = STRIP * NCHAN
    half_rows = GROUP * NCHAN
    in_specs = [
        pl.BlockSpec((NCHAN, 2 * GROUP * NCHAN), lambda i: (0, 0)),
        pl.BlockSpec((GROUP, 2 * GROUP * NCHAN), lambda i: (0, 0)),
        pl.BlockSpec((2, half_rows, HALF), lambda i: (0, jnp.maximum(2 * (i + begin) - 1, 0), 0)),
        pl.BlockSpec((2, rows, HALF), lambda i: (0, i + begin, 0)),
    ]
    args = [trig, tap_table, voltages, voltages]
    if halo is not None:
        in_specs.append(pl.BlockSpec((2, half_rows, HALF), lambda i: (0, 0, 0)))
        args.append(halo)
    return pl.pallas_call(
        functools.partial(filter_body, slot_of, halo is not None),
        out_shape=jax.ShapeDtypeStruct((NCHAN, 2, STRIP * strips, HALF), jnp.bfloat16),
        grid_spec=pltpu.PrefetchScalarGridSpec(
            num_scalar_prefetch=0,
            grid=(strips,),
            in_specs=in_specs,
            out_specs=pl.BlockSpec((NCHAN, 2, STRIP, HALF), lambda i: (0, 0, i, 0)),
            scratch_shapes=[
                pltpu.VMEM((NCHAN * GROUP, 2 * GROUP * NCHAN), jnp.bfloat16),
                pltpu.VMEM((NCHAN * GROUP, 2 * GROUP * NCHAN), jnp.bfloat16),
            ],
        ),
        compiler_params=pltpu.CompilerParams(vmem_limit_bytes=16 << 20),
        cost_estimate=pl.CostEstimate(
            flops=strips * 2 * 2 * 2 * 2 * 256 * 512 * HALF,
            bytes_accessed=strips * 4 * rows * HALF * 2,
            transcendentals=0,
        ),
    )(*args)


def correlate_body(tiles, sections, place_ref, *refs):
    out_ref, raw_late, raw_soon, lanes, turned, held, in_sems, out_sems = refs[-8:]
    blocks = HALF // PANEL
    frames = BLOCKS * raw_late.shape[4]
    turn, group = place_ref[0], place_ref[1]

    copies = [[], []]
    for index, source in enumerate(refs[: 2 * TIMES]):
        which, step = index // TIMES, index % TIMES
        half = group if which == 0 else 1 - group
        copies[0].append(
            pltpu.make_async_copy(source, raw_late.at[half, step], in_sems.at[0, which, step])
        )
    for index, source in enumerate(refs[2 * TIMES : 2 * TIMES + 2 * ROUNDS]):
        which, step = index // ROUNDS, index % ROUNDS
        half = group if which == 0 else 1 - group
        if step >= SINGLE:
            source = source.at[pl.ds(TIMES, TIMES)]
        copies[1].append(
            pltpu.make_async_copy(
                source, raw_soon.at[half, step % N_SITE, step // N_SITE], in_sems.at[1, which, step]
            )
        )
    for copy in copies[1] + copies[0]:
        copy.start()

    counts = [sections[2 * s] for s in range(N_SITE)]
    starts = [sections[2 * s + 1] for s in range(N_SITE)]
    offsets = [jnp.int32(0)]
    for s in range(N_SITE - 1):
        offsets.append(offsets[-1] + counts[s])

    def pick(values, s):
        got = values[0]
        for index in range(1, N_SITE):
            got = jnp.where(s == index, values[index], got)
        return got

    def fill(chunk, panel):
        low = panel * PANEL
        high = low + PANEL - 1
        s_low = jnp.int32(0)
        s_high = jnp.int32(0)
        for s in range(1, N_SITE):
            s_low = s_low + (low >= offsets[s]).astype(jnp.int32)
            s_high = s_high + (high >= offsets[s]).astype(jnp.int32)
        bound = jnp.where(s_low == s_high, PANEL, pick(offsets, s_high) - low)
        lane = lax.broadcasted_iota(jnp.int32, (frames, PANEL), 1)

        def piece(s, block, part):
            block = jnp.clip(block, 0, 2 * blocks - 1)
            half = block // blocks
            at = pl.multiple_of((block - half * blocks) * PANEL, PANEL)
            slot = (turn - s + N_SITE) % N_SITE
            if chunk == 0:
                value = raw_late[half, :, pl.ds(2 * slot, 2), part, :, pl.ds(at, PANEL)]
            else:
                value = raw_soon[half, slot, :, :, part, :, pl.ds(at, PANEL)]
            return value.reshape(frames, PANEL)

        def window(s, part):
            at = low + pick(starts, s) - pick(offsets, s)
            block, shift = at >> 7, at & 127
            mixed = jnp.where(lane >= shift, piece(s, block, part), piece(s, block + 1, part))
            return pltpu.roll(mixed, (PANEL - shift) & 127, 1)

        def put(part, value):
            span = slice(chunk * frames, (chunk + 1) * frames)
            lanes[panel, span, part * PANEL : (part + 1) * PANEL] = value
            turned[panel, part * PANEL : (part + 1) * PANEL, span] = value.T

        @pl.when(s_low == s_high)
        def _():
            for part in range(2):
                put(part, window(s_low, part))

        @pl.when(s_low != s_high)
        def _():
            for part in range(2):
                put(part, jnp.where(lane < bound, window(s_low, part), window(s_high, part)))

    def repeat(count, action):
        def step(index, carry):
            action(index)
            return carry

        lax.fori_loop(0, count, step, 0)

    for chunk in (1, 0):
        for copy in copies[chunk]:
            copy.wait()
        repeat(PANELS, functools.partial(fill, chunk))

    scale = 1.0 / FB

    def result(at):
        return pltpu.make_async_copy(held.at[at], out_ref.at[0, 0, at], out_sems.at[at])

    def multiply(index):
        base = (group * TSLOT + index * PER_STEP) * 2
        for slot in range(PER_STEP):
            left = turned[tiles[base + 2 * slot]]
            right = lanes[tiles[base + 2 * slot + 1]]
            gram = jnp.dot(left, right, preferred_element_type=jnp.float32)
            at = index * PER_STEP + slot
            held[at, 0] = (gram[:PANEL, :PANEL] + gram[PANEL:, PANEL:]) * scale
            held[at, 1] = (gram[PANEL:, :PANEL] - gram[:PANEL, PANEL:]) * scale
        for slot in range(PER_STEP):
            result(index * PER_STEP + slot).start()

    repeat(TSLOT // PER_STEP, multiply)
    repeat(TSLOT, lambda at: result(at).wait())


def correlate_call(tiles, sections, place, pieces):
    count = pieces[0].shape[2]
    resident = pl.BlockSpec(memory_space=pltpu.HBM)
    return pl.pallas_call(
        correlate_body,
        name="correlate",
        out_shape=jax.ShapeDtypeStruct((1, 1, TSLOT, 2, PANEL, PANEL), jnp.float32),
        grid_spec=pltpu.PrefetchScalarGridSpec(
            num_scalar_prefetch=3,
            grid=(),
            in_specs=[resident] * len(pieces),
            out_specs=resident,
            scratch_shapes=[
                pltpu.VMEM((2, TIMES, ROUNDS, 2, count, HALF), jnp.bfloat16),
                pltpu.VMEM((2, N_SITE, 2, TIMES, 2, count, HALF), jnp.bfloat16),
                pltpu.VMEM((PANELS, FB, 2 * PANEL), jnp.bfloat16),
                pltpu.VMEM((PANELS, 2 * PANEL, FB), jnp.bfloat16),
                pltpu.VMEM((TSLOT, 2, PANEL, PANEL), jnp.float32),
                pltpu.SemaphoreType.DMA((2, 2, ROUNDS)),
                pltpu.SemaphoreType.DMA((TSLOT,)),
            ],
        ),
        compiler_params=pltpu.CompilerParams(vmem_limit_bytes=32 << 20),
        cost_estimate=pl.CostEstimate(
            flops=TSLOT * 2 * 256 * 256 * FB,
            bytes_accessed=TSLOT * 2 * PANEL * PANEL * 4 + 4 * FB * N_SITE * CAP,
            transcendentals=0,
        ),
    )(tiles, sections, place, *pieces)


def move_blocks(keys, sources, shapes, moves):
    def body(key_ref, *refs):
        ins, outs, sems = refs[: len(sources)], refs[len(sources) : -1], refs[-1]

        def at(ref, index):
            where = tuple(key_ref[i[0]] if isinstance(i, tuple) else i for i in index)
            return ref.at[where] if where else ref

        copies = [
            pltpu.make_async_copy(at(ins[i], i_at), at(outs[o], o_at), sems.at[number])
            for number, (i, i_at, o, o_at) in enumerate(moves)
        ]
        for copy in copies:
            copy.start()
        for copy in copies:
            copy.wait()

    return pl.pallas_call(
        body,
        out_shape=[jax.ShapeDtypeStruct(shape, jnp.bfloat16) for shape in shapes],
        grid_spec=pltpu.PrefetchScalarGridSpec(
            num_scalar_prefetch=1,
            grid=(),
            in_specs=[pl.BlockSpec(memory_space=pl.ANY)] * len(sources),
            out_specs=[pl.BlockSpec(memory_space=pl.ANY)] * len(shapes),
            scratch_shapes=[pltpu.SemaphoreType.DMA((len(moves),))],
        ),
        compiler_params=pltpu.CompilerParams(vmem_limit_bytes=1 << 20),
    )(keys, *sources)


def from_behind(value, axis):
    count = lax.axis_size(axis)
    return lax.ppermute(value, axis, [(source, source + 1) for source in range(count - 1)])


def across(turn, flip):
    pairs = []
    for site in range(N_SITE):
        for z in range(8):
            goal = 2 * ((z // 2 + site + turn) % N_SITE) + ((z % 2) ^ flip)
            for y in range(TIMES):
                pairs.append((site * NCHAN + z * TIMES + y, z // 2 * NCHAN + goal * TIMES + y))
    return pairs


def along(step):
    return [(z * TIMES + y, z * TIMES + (y + step) % TIMES) for z in range(8) for y in range(TIMES)]


def swap(piece):
    return lax.ppermute(piece, "grp", [(0, 1), (1, 0)])


def correlator(voltages, taps, sections, tile_list):
    halo = from_behind(voltages[:, -GROUP * NCHAN :], "chan")
    trig = jnp.asarray(trig_rows())
    tap_table = tap_rows(taps)
    site, chan, group = (lax.axis_index(name) for name in ("site", "chan", "grp"))
    z, y = chan // TIMES, chan % TIMES
    place = jnp.stack([(z // 2 - site) % N_SITE, group])
    tiles, section_list = tile_list.reshape(-1), sections.reshape(-1)
    strips = LOCAL // STRIP // 2
    rounds = [(turn, flip) for flip in range(2) for turn in range(N_SITE)]
    goals = [2 * ((z // 2 + site + turn) % N_SITE) + ((z % 2) ^ flip) for turn, flip in rounds]
    keys = jnp.stack(goals + [(y + step) % TIMES for step in range(TIMES)])
    joint = ("site", "chan")
    block = (2, STRIP * strips, HALF)

    soon = filter_call(
        trig, tap_table, voltages, None, strips, strips, lambda m: m % TIMES * 8 + m // TIMES
    ).reshape((TIMES, 8) + block)
    held = []
    for step in range(TIMES):
        piece = lax.dynamic_index_in_dim(soon, (y + step) % TIMES, 0, keepdims=False)
        if step:
            piece = lax.ppermute(piece, "chan", along(step))
        held.append(piece)

    late = filter_call(trig, tap_table, voltages, halo, 0, strips, lambda m: m)
    late = late.reshape((8, TIMES) + block)
    late_got, soon_own = [None] * ROUNDS, [None] * ROUNDS
    for index in range(SINGLE):
        piece = lax.dynamic_index_in_dim(late, goals[index], 0, keepdims=False)
        late_got[index] = lax.ppermute(piece, joint, across(*rounds[index]))

    moves, shapes = [], []
    for index in list(range(SINGLE, ROUNDS)) + list(range(SINGLE)):
        both = index >= SINGLE
        if both:
            moves += [(TIMES, ((index,), part), len(shapes), (part,)) for part in range(TIMES)]
        moves += [
            (step, ((index,),), len(shapes), (TIMES * both + step,)) for step in range(TIMES)
        ]
        shapes.append((TIMES * (1 + both),) + block)
    ready = move_blocks(keys, held, shapes, moves)
    for number, piece in enumerate(ready):
        index = (number + SINGLE) % ROUNDS
        soon_own[index] = lax.ppermute(piece, joint, across(*rounds[index]))
        if index >= SINGLE:
            late_got[index] = soon_own[index]

    moves = [
        (index, ((ROUNDS + step,),), step, (index % N_SITE * 2 + index // N_SITE,))
        for step in range(TIMES)
        for index in range(ROUNDS)
    ]
    shapes = [(ROUNDS,) + block] * TIMES
    late_own = list(move_blocks(keys, late_got, shapes, moves))
    for step in range(1, TIMES):
        late_own[step] = lax.ppermute(late_own[step], "chan", along(step))

    pieces = []
    for own in (late_own, soon_own):
        pieces += own + [swap(piece) for piece in own]
    return correlate_call(tiles, section_list, place, pieces)


def solution(mesh):
    in_specs = (P(None, "chan", ("site", "grp")), P(), P(), P())
    out_specs = P("site", "chan", "grp", None, None, None)
    return jax.shard_map(
        correlator, mesh=mesh, in_specs=in_specs, out_specs=out_specs, check_vma=False
    )
```

time: 560 us -> 181 us (0.32)
  the two profiles are of different devices: /device:TPU:1 before, /device:TPU:13 now
where the time goes in v1:
time: 181 us; the launch traced here: 180 us
  starting transfers between devices  90.4 us (50%)
  Pallas kernels  35 us (19%)
  local copies, waits for them, and re-layouts  30 us (17%)
  waiting for transfers between devices  23.9 us (13%)
    ppermute x8, starting transfers between devices, correlator(): late_got[index] = lax.ppermute(piece, joint, across(*rounds[index]))  30.4 us
    ppermute x8, starting transfers between devices, correlator(): soon_own[index] = lax.ppermute(piece, joint, across(*rounds[index]))  25.1 us
    unnamed x74, local copies, waits for them, and re-layouts  24.5 us
    pallas_call x1, Pallas kernels, correlate_call(): pl.pallas_call(correlate_body, name='correlate', out_shape=jax.ShapeDtype...  22.8 us
    ppermute x12, starting transfers between devices, swap(): return lax.ppermute(piece, 'grp', [(0, 1), (1, 0)])  20.4 us
    ppermute x8, waiting for transfers between devices, correlator(): soon_own[index] = lax.ppermute(piece, joint, across(*rounds[index]))  10.5 us
    ppermute x3, waiting for transfers between devices, correlator(): late_own[step] = lax.ppermute(late_own[step], 'chan', along(step))  9.99 us
    ppermute x3, starting transfers between devices, correlator(): late_own[step] = lax.ppermute(late_own[step], 'chan', along(step))  7.08 us
  transfers between devices with their start and end apart: 35, of which 7 were waited for; matrix products, arithmetic and copies ran while one was open for 2% of the time, Pallas kernels for 7%

profile of v1, /device:TPU:13, one launch (start us, length us, event | category | flops | bytes accessed | tf_op | source)
XLA Modules:
  0.0 179.9 jit_solution(9799864506846074606)
XLA Ops:
  0.0 1.8 slice.3
  1.8 3.2 %collective-permute-start = (bf16[2,256,384]{2,1,0:T(8,128)(2,1)}, bf16[2,256,384]{2,1,0:T(8,128)(2,1)}, u32[]{:S(2)}, u32[]{:S(2)}) collective-permute-start(bf16[2,256,384]{2,1,0:T(8,128)(2,1)} %slice.3), channel_id=1, source_target_pairs={{0,2},{2,4},{4,6},{6,8},{8,10},{10,12},{12,14},{14,16},{16,18},{18... | collective-permute-start | bytes 1179656 | tf_op jit(solution)/shard_map/ppermute | solution.py:306
  6.5 1.9 %copy-done = bf16[2,2048,384]{2,1,0:T(8,128)(2,1)S(1)} copy-done((bf16[2,2048,384]{2,1,0:T(8,128)(2,1)S(1)}, bf16[2,2048,384]{2,1,0:T(8,128)(2,1)}, u32[]{:S(2)}) %copy-start) | copy-done | bytes 3145752
  9.2 3.1 %shard_map.57 = bf16[32,2,32,384]{3,2,1,0:T(8,128)(2,1)S(1)} custom-call(f32[32,512]{1,0:T(8,128)S(1)} %copy-done.2, f32[8,512]{1,0:T(8,128)S(1)} %stack.99.tap_ref, bf16[2,2048,384]{2,1,0:T(8,128)(2,1)S(1)} %copy-done, bf16[2,2048,384]{2,1,0:T(8,128)(2,1)S(1)} %copy-done), custom_call_target="tpu_custom_call" | custom-call | flops 1610612736 | bytes 3145728 | tf_op jit(solution)/shard_map/pallas_call | solution.py:106
  12.3 1.1 dynamic-slice_bitcast_fusion
  14.2 1.4 collective-permute-start.17
  15.6 1.9 %collective-permute-start.16 = (bf16[8,2,32,384]{3,2,1,0:T(8,128)(2,1)}, bf16[8,2,32,384]{3,2,1,0:T(8,128)(2,1)}, u32[]{:S(2)}, u32[]{:S(2)}) collective-permute-start(bf16[8,2,32,384]{3,2,1,0:T(8,128)(2,1)} %get-tuple-element.31), channel_id=1, source_target_pairs={{0,2},{2,4},{4,6},{6,0},{8,10},{10,12},{12,14},{14,8},{16,18},{18,... | collective-permute-start | bytes 1179656 | tf_op jit(solution)/shard_map/ppermute | solution.py:349
  18.3 3.9 %shard_map.55 = bf16[32,2,32,384]{3,2,1,0:T(8,128)(2,1)S(1)} custom-call(f32[32,512]{1,0:T(8,128)S(1)} %copy-done.3, f32[8,512]{1,0:T(8,128)S(1)} %stack.99.tap_ref, bf16[2,2048,384]{2,1,0:T(8,128)(2,1)S(1)} %copy-done.1, bf16[2,2048,384]{2,1,0:T(8,128)(2,1)S(1)} %copy-done.1, bf16[2,256,384]{2,1,0:T(8,128)(2,1)} %collective-permute-done.rest_0_), custom_call_target="tpu_custom_call" | custom-call | flops 1610612736 | bytes 3145728 | tf_op jit(solution)/shard_map/pallas_call | solution.py:106
  23.2 5.5 %collective-permute-start.8 = (bf16[4,2,32,384]{3,2,1,0:T(8,128)(2,1)S(1)}, bf16[4,2,32,384]{3,2,1,0:T(8,128)(2,1)S(1)}, u32[]{:S(2)}, u32[]{:S(2)}) collective-permute-start(bf16[4,2,32,384]{3,2,1,0:T(8,128)(2,1)S(1)} %get-tuple-element.33), channel_id=1, source_target_pairs={{0,56},{2,58},{4,60},{6,62},{8,48},{10,50},{12,52},{14,54},{16,72}... | collective-permute-start | bytes 589832 | tf_op jit(solution)/shard_map/ppermute | solution.py:357
  29.4 4.9 %collective-permute-start.6 = (bf16[4,2,32,384]{3,2,1,0:T(8,128)(2,1)S(1)}, bf16[4,2,32,384]{3,2,1,0:T(8,128)(2,1)S(1)}, u32[]{:S(2)}, u32[]{:S(2)}) collective-permute-start(bf16[4,2,32,384]{3,2,1,0:T(8,128)(2,1)S(1)} %get-tuple-element.35), channel_id=1, source_target_pairs={{0,24},{2,26},{4,28},{6,30},{8,16},{10,18},{12,20},{14,22},{16,104... | collective-permute-start | bytes 589832 | tf_op jit(solution)/shard_map/ppermute | solution.py:357
  34.3 4.6 %collective-permute-start.5 = (bf16[4,2,32,384]{3,2,1,0:T(8,128)(2,1)}, bf16[4,2,32,384]{3,2,1,0:T(8,128)(2,1)S(1)}, u32[]{:S(2)}, u32[]{:S(2)}) collective-permute-start(bf16[4,2,32,384]{3,2,1,0:T(8,128)(2,1)} %get-tuple-element.36), channel_id=1, source_target_pairs={{0,8},{2,10},{4,12},{6,14},{8,0},{10,2},{12,4},{14,6},{16,88},{18,... | collective-permute-start | bytes 589832 | tf_op jit(solution)/shard_map/ppermute | solution.py:357
  39.0 2.3 %collective-permute-start.4 = (bf16[4,2,32,384]{3,2,1,0:T(8,128)(2,1)}, bf16[4,2,32,384]{3,2,1,0:T(8,128)(2,1)S(1)}, u32[]{:S(2)}, u32[]{:S(2)}) collective-permute-start(bf16[4,2,32,384]{3,2,1,0:T(8,128)(2,1)} %get-tuple-element.37), channel_id=1, source_target_pairs={{0,48},{2,50},{4,52},{6,54},{8,56},{10,58},{12,60},{14,62},{16,64}... | collective-permute-start | bytes 589832 | tf_op jit(solution)/shard_map/ppermute | solution.py:357
  41.3 4.3 %collective-permute-start.3 = (bf16[4,2,32,384]{3,2,1,0:T(8,128)(2,1)}, bf16[4,2,32,384]{3,2,1,0:T(8,128)(2,1)S(1)}, u32[]{:S(2)}, u32[]{:S(2)}) collective-permute-start(bf16[4,2,32,384]{3,2,1,0:T(8,128)(2,1)} %get-tuple-element.38), channel_id=1, source_target_pairs={{0,32},{2,34},{4,36},{6,38},{8,40},{10,42},{12,44},{14,46},{16,112... | collective-permute-start | bytes 589832 | tf_op jit(solution)/shard_map/ppermute | solution.py:357
  45.6 2.3 %collective-permute-done.7.refs_6_ = bf16[4,2,32,384]{3,2,1,0:T(8,128)(2,1)S(1)} collective-permute-done((bf16[4,2,32,384]{3,2,1,0:T(8,128)(2,1)S(1)}, bf16[4,2,32,384]{3,2,1,0:T(8,128)(2,1)S(1)}, u32[]{:S(2)}, u32[]{:S(2)}) %collective-permute-start.7) | collective-permute-done | bytes 196640 | tf_op jit(solution)/shard_map/ppermute | solution.py:357
  47.9 6.2 %collective-permute-start.2 = (bf16[4,2,32,384]{3,2,1,0:T(8,128)(2,1)S(1)}, bf16[4,2,32,384]{3,2,1,0:T(8,128)(2,1)S(1)}, u32[]{:S(2)}, u32[]{:S(2)}) collective-permute-start(bf16[4,2,32,384]{3,2,1,0:T(8,128)(2,1)S(1)} %get-tuple-element.39), channel_id=1, source_target_pairs={{0,16},{2,18},{4,20},{6,22},{8,24},{10,26},{12,28},{14,30},{16,96}... | collective-permute-start | bytes 589832 | tf_op jit(solution)/shard_map/ppermute | solution.py:357
  54.1 1.9 %collective-permute-start.1 = (bf16[4,2,32,384]{3,2,1,0:T(8,128)(2,1)S(1)}, bf16[4,2,32,384]{3,2,1,0:T(8,128)(2,1)S(1)}, u32[]{:S(2)}, u32[]{:S(2)}) collective-permute-start(bf16[4,2,32,384]{3,2,1,0:T(8,128)(2,1)S(1)} %get-tuple-element.40), channel_id=1, source_target_pairs={{0,0},{2,2},{4,4},{6,6},{8,8},{10,10},{12,12},{14,14},{16,80},{18,... | collective-permute-start | bytes 589832 | tf_op jit(solution)/shard_map/ppermute | solution.py:357
  56.1 2.3 %shard_map.58 = (bf16[4,2,32,384]{3,2,1,0:T(8,128)(2,1)S(1)}, bf16[4,2,32,384]{3,2,1,0:T(8,128)(2,1)S(1)}, bf16[4,2,32,384]{3,2,1,0:T(8,128)(2,1)S(1)}, bf16[4,2...) custom-call(s32[12]{0:T(128)S(1)} %stack.90.key_ref, ...), custom_call_target="tpu_custom_call" | custom-call | tf_op jit(solution)/shard_map/pallas_call | solution.py:290
  58.5 4.9 %collective-permute-start.19 = (bf16[4,2,32,384]{3,2,1,0:T(8,128)(2,1)S(1)}, bf16[4,2,32,384]{3,2,1,0:T(8,128)(2,1)S(1)}, u32[]{:S(2)}, u32[]{:S(2)}) collective-permute-start(bf16[4,2,32,384]{3,2,1,0:T(8,128)(2,1)S(1)} %get-tuple-element.21), channel_id=1, source_target_pairs={{0,0},{2,2},{4,4},{6,6},{8,8},{10,10},{12,12},{14,14},{16,80},{18,... | collective-permute-start | bytes 589832 | tf_op jit(solution)/shard_map/ppermute | solution.py:371
  63.3 1.9 %collective-permute-start.20 = (bf16[4,2,32,384]{3,2,1,0:T(8,128)(2,1)S(1)}, bf16[4,2,32,384]{3,2,1,0:T(8,128)(2,1)S(1)}, u32[]{:S(2)}, u32[]{:S(2)}) collective-permute-start(bf16[4,2,32,384]{3,2,1,0:T(8,128)(2,1)S(1)} %get-tuple-element.22), channel_id=1, source_target_pairs={{0,16},{2,18},{4,20},{6,22},{8,24},{10,26},{12,28},{14,30},{16,96}... | collective-permute-start | bytes 589832 | tf_op jit(solution)/shard_map/ppermute | solution.py:371
  65.3 2.7 %collective-permute-start.21 = (bf16[4,2,32,384]{3,2,1,0:T(8,128)(2,1)S(1)}, bf16[4,2,32,384]{3,2,1,0:T(8,128)(2,1)S(1)}, u32[]{:S(2)}, u32[]{:S(2)}) collective-permute-start(bf16[4,2,32,384]{3,2,1,0:T(8,128)(2,1)S(1)} %get-tuple-element.23), channel_id=1, source_target_pairs={{0,32},{2,34},{4,36},{6,38},{8,40},{10,42},{12,44},{14,46},{16,112... | collective-permute-start | bytes 589832 | tf_op jit(solution)/shard_map/ppermute | solution.py:371
  68.0 10.8 %collective-permute-start.22 = (bf16[4,2,32,384]{3,2,1,0:T(8,128)(2,1)S(1)}, bf16[4,2,32,384]{3,2,1,0:T(8,128)(2,1)S(1)}, u32[]{:S(2)}, u32[]{:S(2)}) collective-permute-start(bf16[4,2,32,384]{3,2,1,0:T(8,128)(2,1)S(1)} %get-tuple-element.24), channel_id=1, source_target_pairs={{0,48},{2,50},{4,52},{6,54},{8,56},{10,58},{12,60},{14,62},{16,64}... | collective-permute-start | bytes 589832 | tf_op jit(solution)/shard_map/ppermute | solution.py:371
  78.8 1.9 %collective-permute-start.23 = (bf16[4,2,32,384]{3,2,1,0:T(8,128)(2,1)S(1)}, bf16[4,2,32,384]{3,2,1,0:T(8,128)(2,1)S(1)}, u32[]{:S(2)}, u32[]{:S(2)}) collective-permute-start(bf16[4,2,32,384]{3,2,1,0:T(8,128)(2,1)S(1)} %get-tuple-element.25), channel_id=1, source_target_pairs={{0,8},{2,10},{4,12},{6,14},{8,0},{10,2},{12,4},{14,6},{16,88},{18,... | collective-permute-start | bytes 589832 | tf_op jit(solution)/shard_map/ppermute | solution.py:371
  80.7 1.7 collective-permute-start.24
  82.4 7.1 %collective-permute-done.20.refs_9_ = bf16[4,2,32,384]{3,2,1,0:T(8,128)(2,1)S(1)} collective-permute-done((bf16[4,2,32,384]{3,2,1,0:T(8,128)(2,1)S(1)}, bf16[4,2,32,384]{3,2,1,0:T(8,128)(2,1)S(1)}, u32[]{:S(2)}, u32[]{:S(2)}) %collective-permute-start.20) | collective-permute-done | bytes 196640 | tf_op jit(solution)/shard_map/ppermute | solution.py:371
  89.5 1.3 collective-permute-start.26
  90.8 13.8 %collective-permute-start.27 = (bf16[4,2,32,384]{3,2,1,0:T(8,128)(2,1)S(1)}, bf16[4,2,32,384]{3,2,1,0:T(8,128)(2,1)S(1)}, u32[]{:S(2)}, u32[]{:S(2)}) collective-permute-start(bf16[4,2,32,384]{3,2,1,0:T(8,128)(2,1)S(1)} %collective-permute-done.19.refs_8_), channel_id=1, source_target_pairs={{0,1},{1,0},{2,3},{3,2},{4,5},{5,4},{6,7},{7,6},{8,9},{9,8},{10,11... | collective-permute-start | bytes 589832 | tf_op jit(solution)/shard_map/ppermute | solution.py:324
  104.8 2.9 %shard_map.56 = (bf16[8,2,32,384]{3,2,1,0:T(8,128)(2,1)S(1)}, bf16[8,2,32,384]{3,2,1,0:T(8,128)(2,1)S(1)}, bf16[8,2,32,384]{3,2,1,0:T(8,128)(2,1)S(1)}, bf16[8,2,32,384]{3,2,1,0:T(8,128)(2,1)S(1)}) custom-call(s32[12]{0:T(128)S(1)} %stack.90.key_ref, bf16[4,2,32,384]{3,2,1,0:T(8,128)(2,1)S(1)} %collective-permute-done.1.refs_0_, ...), custom_call_target="tpu_custom_call" | custom-call | tf_op jit(solution)/shard_map/pallas_call | solution.py:290
  107.7 1.5 collective-permute-done.24.refs_13_
  109.7 1.9 %collective-permute-start.30 = (bf16[4,2,32,384]{3,2,1,0:T(8,128)(2,1)S(1)}, bf16[4,2,32,384]{3,2,1,0:T(8,128)(2,1)S(1)}, u32[]{:S(2)}, u32[]{:S(2)}) collective-permute-start(bf16[4,2,32,384]{3,2,1,0:T(8,128)(2,1)S(1)} %collective-permute-done.22.refs_11_), channel_id=1, source_target_pairs={{0,1},{1,0},{2,3},{3,2},{4,5},{5,4},{6,7},{7,6},{8,9},{9,8},{10,11... | collective-permute-start | bytes 589832 | tf_op jit(solution)/shard_map/ppermute | solution.py:324
  111.6 1.8 %collective-permute-done.26.refs_15_ = bf16[4,2,32,384]{3,2,1,0:T(8,128)(2,1)} collective-permute-done((bf16[4,2,32,384]{3,2,1,0:T(8,128)(2,1)S(1)}, bf16[4,2,32,384]{3,2,1,0:T(8,128)(2,1)}, u32[]{:S(2)}, u32[]{:S(2)}) %collective-permute-start.26) | collective-permute-done | bytes 196640 | tf_op jit(solution)/shard_map/ppermute | solution.py:371
  113.4 5.3 %collective-permute-start.9 = (bf16[8,2,32,384]{3,2,1,0:T(8,128)(2,1)S(1)}, bf16[8,2,32,384]{3,2,1,0:T(8,128)(2,1)S(1)}, u32[]{:S(2)}, u32[]{:S(2)}) collective-permute-start(bf16[8,2,32,384]{3,2,1,0:T(8,128)(2,1)S(1)} %get-tuple-element.18), channel_id=1, source_target_pairs={{0,2},{2,4},{4,6},{6,0},{8,10},{10,12},{12,14},{14,8},{16,18},{18,... | collective-permute-start | bytes 1179656 | tf_op jit(solution)/shard_map/ppermute | solution.py:383
  120.1 1.8 %collective-permute-start.11 = (bf16[8,2,32,384]{3,2,1,0:T(8,128)(2,1)S(1)}, bf16[8,2,32,384]{3,2,1,0:T(8,128)(2,1)S(1)}, u32[]{:S(2)}, u32[]{:S(2)}) collective-permute-start(bf16[8,2,32,384]{3,2,1,0:T(8,128)(2,1)S(1)} %get-tuple-element.20), channel_id=1, source_target_pairs={{0,6},{2,0},{4,2},{6,4},{8,14},{10,8},{12,10},{14,12},{16,22},{18,... | collective-permute-start | bytes 1179656 | tf_op jit(solution)/shard_map/ppermute | solution.py:383
  122.5 1.0 collective-permute-start.31
  127.4 7.7 %collective-permute-done.9.refs_1_ = bf16[8,2,32,384]{3,2,1,0:T(8,128)(2,1)S(1)} collective-permute-done((bf16[8,2,32,384]{3,2,1,0:T(8,128)(2,1)S(1)}, bf16[8,2,32,384]{3,2,1,0:T(8,128)(2,1)S(1)}, u32[]{:S(2)}, u32[]{:S(2)}) %collective-permute-start.9) | collective-permute-done | bytes 393248 | tf_op jit(solution)/shard_map/ppermute | solution.py:383
  135.2 1.3 collective-permute-start.13
  136.5 2.3 %collective-permute-done.11.refs_3_ = bf16[8,2,32,384]{3,2,1,0:T(8,128)(2,1)S(1)} collective-permute-done((bf16[8,2,32,384]{3,2,1,0:T(8,128)(2,1)S(1)}, bf16[8,2,32,384]{3,2,1,0:T(8,128)(2,1)S(1)}, u32[]{:S(2)}, u32[]{:S(2)}) %collective-permute-start.11) | collective-permute-done | bytes 393248 | tf_op jit(solution)/shard_map/ppermute | solution.py:383
  138.7 1.3 collective-permute-start.15
  141.3 1.1 collective-permute-done.34.refs_23_
  144.0 0.9 copy-done.7
  145.0 0.9 copy-done.9
  145.9 0.9 copy-done.11
  146.8 0.9 copy-done.13
  148.7 0.9 copy-done.17
  149.6 0.9 copy-done.19
  150.5 0.9 copy-done.21
  151.4 0.9 copy-done.23
  152.4 0.9 copy-done.25
  157.0 22.8 %correlate.1 = f32[1,1,68,2,128,128]{5,4,3,2,1,0:T(8,128)} custom-call(s32[272]{0:T(512)S(1)} %reshape.29.tiles, s32[8]{0:T(128)S(1)} %reshape.30.sections, s32[2]{0:T(128)S(1)} %pad_add_fusion.place_ref, bf16[8,2,32,384]{3,2,1,0:T(8,128)(2,1)S(1)} %get-tuple-element.17.refs_0_, bf16[8,2,32,384]{3,2,1,0:T(8,128)(2,1)S(1)} %collective-permute-done.9.refs_1_, ...), custom_call_target="tpu_custom_call" | custom-call | flops 4563402752 | bytes 15204352 | tf_op jit(solution)/shard_map/correlate/pallas_call | solution.py:245
  (119 shorter events, 19.8 us)
Async XLA Ops:
  1.8 15.7 %collective-permute-start = (bf16[2,256,384]{2,1,0:T(8,128)(2,1)}, bf16[2,256,384]{2,1,0:T(8,128)(2,1)}, u32[]{:S(2)}, u32[]{:S(2)}) collective-permute-start(bf16[2,256,384]{2,1,0:T(8,128)(2,1)} %slice.3), channel_id=1, source_target_pairs={{0,2},{2,4},{4,6},{6,8},{8,10},{10,12},{12,14},{14,16},{16,18},{18... | collective-permute-start | bytes 1179656 | tf_op jit(solution)/shard_map/ppermute | solution.py:306
  6.4 1.9 %copy-start = (bf16[2,2048,384]{2,1,0:T(8,128)(2,1)S(1)}, bf16[2,2048,384]{2,1,0:T(8,128)(2,1)}, u32[]{:S(2)}) copy-start(bf16[2,2048,384]{2,1,0:T(8,128)(2,1)} %now_ref.3) | copy-start | bytes 9437188
  12.3 5.2 %copy-start.1 = (bf16[2,2048,384]{2,1,0:T(8,128)(2,1)S(1)}, bf16[2,2048,384]{2,1,0:T(8,128)(2,1)}, u32[]{:S(2)}) copy-start(bf16[2,2048,384]{2,1,0:T(8,128)(2,1)} %now_ref.3) | copy-start | bytes 9437188
  13.4 16.1 %collective-permute-start.18 = (bf16[8,2,32,384]{3,2,1,0:T(8,128)(2,1)}, bf16[8,2,32,384]{3,2,1,0:T(8,128)(2,1)}, u32[]{:S(2)}, u32[]{:S(2)}) collective-permute-start(bf16[8,2,32,384]{3,2,1,0:T(8,128)(2,1)} %get-tuple-element.29), channel_id=1, source_target_pairs={{0,6},{2,0},{4,2},{6,4},{8,14},{10,8},{12,10},{14,12},{16,22},{18,... | collective-permute-start | bytes 1179656 | tf_op jit(solution)/shard_map/ppermute | solution.py:349
  14.2 20.1 %collective-permute-start.17 = (bf16[8,2,32,384]{3,2,1,0:T(8,128)(2,1)}, bf16[8,2,32,384]{3,2,1,0:T(8,128)(2,1)}, u32[]{:S(2)}, u32[]{:S(2)}) collective-permute-start(bf16[8,2,32,384]{3,2,1,0:T(8,128)(2,1)} %get-tuple-element.30), channel_id=1, source_target_pairs={{0,4},{2,6},{4,0},{6,2},{8,12},{10,14},{12,8},{14,10},{16,20},{18,... | collective-permute-start | bytes 1179656 | tf_op jit(solution)/shard_map/ppermute | solution.py:349
  15.6 23.4 %collective-permute-start.16 = (bf16[8,2,32,384]{3,2,1,0:T(8,128)(2,1)}, bf16[8,2,32,384]{3,2,1,0:T(8,128)(2,1)}, u32[]{:S(2)}, u32[]{:S(2)}) collective-permute-start(bf16[8,2,32,384]{3,2,1,0:T(8,128)(2,1)} %get-tuple-element.31), channel_id=1, source_target_pairs={{0,2},{2,4},{4,6},{6,0},{8,10},{10,12},{12,14},{14,8},{16,18},{18,... | collective-permute-start | bytes 1179656 | tf_op jit(solution)/shard_map/ppermute | solution.py:349
  23.2 18.1 %collective-permute-start.8 = (bf16[4,2,32,384]{3,2,1,0:T(8,128)(2,1)S(1)}, bf16[4,2,32,384]{3,2,1,0:T(8,128)(2,1)S(1)}, u32[]{:S(2)}, u32[]{:S(2)}) collective-permute-start(bf16[4,2,32,384]{3,2,1,0:T(8,128)(2,1)S(1)} %get-tuple-element.33), channel_id=1, source_target_pairs={{0,56},{2,58},{4,60},{6,62},{8,48},{10,50},{12,52},{14,54},{16,72}... | collective-permute-start | bytes 589832 | tf_op jit(solution)/shard_map/ppermute | solution.py:357
  28.7 19.2 %collective-permute-start.7 = (bf16[4,2,32,384]{3,2,1,0:T(8,128)(2,1)S(1)}, bf16[4,2,32,384]{3,2,1,0:T(8,128)(2,1)S(1)}, u32[]{:S(2)}, u32[]{:S(2)}) collective-permute-start(bf16[4,2,32,384]{3,2,1,0:T(8,128)(2,1)S(1)} %get-tuple-element.34), channel_id=1, source_target_pairs={{0,40},{2,42},{4,44},{6,46},{8,32},{10,34},{12,36},{14,38},{16,120... | collective-permute-start | bytes 589832 | tf_op jit(solution)/shard_map/ppermute | solution.py:357
  29.4 24.6 %collective-permute-start.6 = (bf16[4,2,32,384]{3,2,1,0:T(8,128)(2,1)S(1)}, bf16[4,2,32,384]{3,2,1,0:T(8,128)(2,1)S(1)}, u32[]{:S(2)}, u32[]{:S(2)}) collective-permute-start(bf16[4,2,32,384]{3,2,1,0:T(8,128)(2,1)S(1)} %get-tuple-element.35), channel_id=1, source_target_pairs={{0,24},{2,26},{4,28},{6,30},{8,16},{10,18},{12,20},{14,22},{16,104... | collective-permute-start | bytes 589832 | tf_op jit(solution)/shard_map/ppermute | solution.py:357
  34.3 24.1 %collective-permute-start.5 = (bf16[4,2,32,384]{3,2,1,0:T(8,128)(2,1)}, bf16[4,2,32,384]{3,2,1,0:T(8,128)(2,1)S(1)}, u32[]{:S(2)}, u32[]{:S(2)}) collective-permute-start(bf16[4,2,32,384]{3,2,1,0:T(8,128)(2,1)} %get-tuple-element.36), channel_id=1, source_target_pairs={{0,8},{2,10},{4,12},{6,14},{8,0},{10,2},{12,4},{14,6},{16,88},{18,... | collective-permute-start | bytes 589832 | tf_op jit(solution)/shard_map/ppermute | solution.py:357
  39.0 24.4 %collective-permute-start.4 = (bf16[4,2,32,384]{3,2,1,0:T(8,128)(2,1)}, bf16[4,2,32,384]{3,2,1,0:T(8,128)(2,1)S(1)}, u32[]{:S(2)}, u32[]{:S(2)}) collective-permute-start(bf16[4,2,32,384]{3,2,1,0:T(8,128)(2,1)} %get-tuple-element.37), channel_id=1, source_target_pairs={{0,48},{2,50},{4,52},{6,54},{8,56},{10,58},{12,60},{14,62},{16,64}... | collective-permute-start | bytes 589832 | tf_op jit(solution)/shard_map/ppermute | solution.py:357
  41.3 24.0 %collective-permute-start.3 = (bf16[4,2,32,384]{3,2,1,0:T(8,128)(2,1)}, bf16[4,2,32,384]{3,2,1,0:T(8,128)(2,1)S(1)}, u32[]{:S(2)}, u32[]{:S(2)}) collective-permute-start(bf16[4,2,32,384]{3,2,1,0:T(8,128)(2,1)} %get-tuple-element.38), channel_id=1, source_target_pairs={{0,32},{2,34},{4,36},{6,38},{8,40},{10,42},{12,44},{14,46},{16,112... | collective-permute-start | bytes 589832 | tf_op jit(solution)/shard_map/ppermute | solution.py:357
  47.9 20.1 %collective-permute-start.2 = (bf16[4,2,32,384]{3,2,1,0:T(8,128)(2,1)S(1)}, bf16[4,2,32,384]{3,2,1,0:T(8,128)(2,1)S(1)}, u32[]{:S(2)}, u32[]{:S(2)}) collective-permute-start(bf16[4,2,32,384]{3,2,1,0:T(8,128)(2,1)S(1)} %get-tuple-element.39), channel_id=1, source_target_pairs={{0,16},{2,18},{4,20},{6,22},{8,24},{10,26},{12,28},{14,30},{16,96}... | collective-permute-start | bytes 589832 | tf_op jit(solution)/shard_map/ppermute | solution.py:357
  54.1 24.7 %collective-permute-start.1 = (bf16[4,2,32,384]{3,2,1,0:T(8,128)(2,1)S(1)}, bf16[4,2,32,384]{3,2,1,0:T(8,128)(2,1)S(1)}, u32[]{:S(2)}, u32[]{:S(2)}) collective-permute-start(bf16[4,2,32,384]{3,2,1,0:T(8,128)(2,1)S(1)} %get-tuple-element.40), channel_id=1, source_target_pairs={{0,0},{2,2},{4,4},{6,6},{8,8},{10,10},{12,12},{14,14},{16,80},{18,... | collective-permute-start | bytes 589832 | tf_op jit(solution)/shard_map/ppermute | solution.py:357
  56.1 84.7 %copy-start.35 = (s32[4,2]{0,1:T(2,128)S(1)}, s32[4,2]{0,1:T(2,128)}, u32[]{:S(2)}) copy-start(s32[4,2]{0,1:T(2,128)} %param.7) | copy-start | bytes 100
  56.1 84.9 %copy-start.34 = (s32[2,68,2]{1,2,0:T(2,128)S(1)}, s32[2,68,2]{1,2,0:T(2,128)}, u32[]{:S(2)}) copy-start(s32[2,68,2]{1,2,0:T(2,128)} %param.8) | copy-start | bytes 3268
  58.5 22.2 %collective-permute-start.19 = (bf16[4,2,32,384]{3,2,1,0:T(8,128)(2,1)S(1)}, bf16[4,2,32,384]{3,2,1,0:T(8,128)(2,1)S(1)}, u32[]{:S(2)}, u32[]{:S(2)}) collective-permute-start(bf16[4,2,32,384]{3,2,1,0:T(8,128)(2,1)S(1)} %get-tuple-element.21), channel_id=1, source_target_pairs={{0,0},{2,2},{4,4},{6,6},{8,8},{10,10},{12,12},{14,14},{16,80},{18,... | collective-permute-start | bytes 589832 | tf_op jit(solution)/shard_map/ppermute | solution.py:371
  63.3 26.1 %collective-permute-start.20 = (bf16[4,2,32,384]{3,2,1,0:T(8,128)(2,1)S(1)}, bf16[4,2,32,384]{3,2,1,0:T(8,128)(2,1)S(1)}, u32[]{:S(2)}, u32[]{:S(2)}) collective-permute-start(bf16[4,2,32,384]{3,2,1,0:T(8,128)(2,1)S(1)} %get-tuple-element.22), channel_id=1, source_target_pairs={{0,16},{2,18},{4,20},{6,22},{8,24},{10,26},{12,28},{14,30},{16,96}... | collective-permute-start | bytes 589832 | tf_op jit(solution)/shard_map/ppermute | solution.py:371
  65.3 24.2 %collective-permute-start.21 = (bf16[4,2,32,384]{3,2,1,0:T(8,128)(2,1)S(1)}, bf16[4,2,32,384]{3,2,1,0:T(8,128)(2,1)S(1)}, u32[]{:S(2)}, u32[]{:S(2)}) collective-permute-start(bf16[4,2,32,384]{3,2,1,0:T(8,128)(2,1)S(1)} %get-tuple-element.23), channel_id=1, source_target_pairs={{0,32},{2,34},{4,36},{6,38},{8,40},{10,42},{12,44},{14,46},{16,112... | collective-permute-start | bytes 589832 | tf_op jit(solution)/shard_map/ppermute | solution.py:371
  68.0 22.8 %collective-permute-start.22 = (bf16[4,2,32,384]{3,2,1,0:T(8,128)(2,1)S(1)}, bf16[4,2,32,384]{3,2,1,0:T(8,128)(2,1)S(1)}, u32[]{:S(2)}, u32[]{:S(2)}) collective-permute-start(bf16[4,2,32,384]{3,2,1,0:T(8,128)(2,1)S(1)} %get-tuple-element.24), channel_id=1, source_target_pairs={{0,48},{2,50},{4,52},{6,54},{8,56},{10,58},{12,60},{14,62},{16,64}... | collective-permute-start | bytes 589832 | tf_op jit(solution)/shard_map/ppermute | solution.py:371
  78.8 25.9 %collective-permute-start.23 = (bf16[4,2,32,384]{3,2,1,0:T(8,128)(2,1)S(1)}, bf16[4,2,32,384]{3,2,1,0:T(8,128)(2,1)S(1)}, u32[]{:S(2)}, u32[]{:S(2)}) collective-permute-start(bf16[4,2,32,384]{3,2,1,0:T(8,128)(2,1)S(1)} %get-tuple-element.25), channel_id=1, source_target_pairs={{0,8},{2,10},{4,12},{6,14},{8,0},{10,2},{12,4},{14,6},{16,88},{18,... | collective-permute-start | bytes 589832 | tf_op jit(solution)/shard_map/ppermute | solution.py:371
  80.7 58.0 %copy-start.4 = (bf16[4,2,32,384]{3,2,1,0:T(8,128)(2,1)}, bf16[4,2,32,384]{3,2,1,0:T(8,128)(2,1)S(1)}, u32[]{:S(2)}) copy-start(bf16[4,2,32,384]{3,2,1,0:T(8,128)(2,1)S(1)} %collective-permute-done.19.refs_8_) | copy-start | bytes 589828
  80.7 28.5 %collective-permute-start.24 = (bf16[4,2,32,384]{3,2,1,0:T(8,128)(2,1)S(1)}, bf16[4,2,32,384]{3,2,1,0:T(8,128)(2,1)S(1)}, u32[]{:S(2)}, u32[]{:S(2)}) collective-permute-start(bf16[4,2,32,384]{3,2,1,0:T(8,128)(2,1)S(1)} %get-tuple-element.26), channel_id=1, source_target_pairs={{0,24},{2,26},{4,28},{6,30},{8,16},{10,18},{12,20},{14,22},{16,104... | collective-permute-start | bytes 589832 | tf_op jit(solution)/shard_map/ppermute | solution.py:371
  89.5 50.5 %copy-start.6 = (bf16[4,2,32,384]{3,2,1,0:T(8,128)(2,1)}, bf16[4,2,32,384]{3,2,1,0:T(8,128)(2,1)S(1)}, u32[]{:S(2)}) copy-start(bf16[4,2,32,384]{3,2,1,0:T(8,128)(2,1)S(1)} %collective-permute-done.20.refs_9_) | copy-start | bytes 589828
  89.5 20.2 %collective-permute-start.25 = (bf16[4,2,32,384]{3,2,1,0:T(8,128)(2,1)S(1)}, bf16[4,2,32,384]{3,2,1,0:T(8,128)(2,1)S(1)}, u32[]{:S(2)}, u32[]{:S(2)}) collective-permute-start(bf16[4,2,32,384]{3,2,1,0:T(8,128)(2,1)S(1)} %get-tuple-element.27), channel_id=1, source_target_pairs={{0,40},{2,42},{4,44},{6,46},{8,32},{10,34},{12,36},{14,38},{16,120... | collective-permute-start | bytes 589832 | tf_op jit(solution)/shard_map/ppermute | solution.py:371
  89.5 50.5 %copy-start.8 = (bf16[4,2,32,384]{3,2,1,0:T(8,128)(2,1)}, bf16[4,2,32,384]{3,2,1,0:T(8,128)(2,1)S(1)}, u32[]{:S(2)}) copy-start(bf16[4,2,32,384]{3,2,1,0:T(8,128)(2,1)S(1)} %collective-permute-done.21.refs_10_) | copy-start | bytes 589828
  89.5 23.9 %collective-permute-start.26 = (bf16[4,2,32,384]{3,2,1,0:T(8,128)(2,1)S(1)}, bf16[4,2,32,384]{3,2,1,0:T(8,128)(2,1)}, u32[]{:S(2)}, u32[]{:S(2)}) collective-permute-start(bf16[4,2,32,384]{3,2,1,0:T(8,128)(2,1)S(1)} %get-tuple-element.28), channel_id=1, source_target_pairs={{0,56},{2,58},{4,60},{6,62},{8,48},{10,50},{12,52},{14,54},{16,72}... | collective-permute-start | bytes 589832 | tf_op jit(solution)/shard_map/ppermute | solution.py:371
  90.8 49.2 %copy-start.10 = (bf16[4,2,32,384]{3,2,1,0:T(8,128)(2,1)}, bf16[4,2,32,384]{3,2,1,0:T(8,128)(2,1)S(1)}, u32[]{:S(2)}) copy-start(bf16[4,2,32,384]{3,2,1,0:T(8,128)(2,1)S(1)} %collective-permute-done.22.refs_11_) | copy-start | bytes 589828
  90.8 27.9 %collective-permute-start.27 = (bf16[4,2,32,384]{3,2,1,0:T(8,128)(2,1)S(1)}, bf16[4,2,32,384]{3,2,1,0:T(8,128)(2,1)S(1)}, u32[]{:S(2)}, u32[]{:S(2)}) collective-permute-start(bf16[4,2,32,384]{3,2,1,0:T(8,128)(2,1)S(1)} %collective-permute-done.19.refs_8_), channel_id=1, source_target_pairs={{0,1},{1,0},{2,3},{3,2},{4,5},{5,4},{6,7},{7,6},{8,9},{9,8},{10,11... | collective-permute-start | bytes 589832 | tf_op jit(solution)/shard_map/ppermute | solution.py:324
  104.7 35.4 %copy-start.12 = (bf16[4,2,32,384]{3,2,1,0:T(8,128)(2,1)}, bf16[4,2,32,384]{3,2,1,0:T(8,128)(2,1)S(1)}, u32[]{:S(2)}) copy-start(bf16[4,2,32,384]{3,2,1,0:T(8,128)(2,1)S(1)} %collective-permute-done.23.refs_12_) | copy-start | bytes 589828
  104.7 14.7 %collective-permute-start.28 = (bf16[4,2,32,384]{3,2,1,0:T(8,128)(2,1)S(1)}, bf16[4,2,32,384]{3,2,1,0:T(8,128)(2,1)S(1)}, u32[]{:S(2)}, u32[]{:S(2)}) collective-permute-start(bf16[4,2,32,384]{3,2,1,0:T(8,128)(2,1)S(1)} %collective-permute-done.20.refs_9_), channel_id=1, source_target_pairs={{0,1},{1,0},{2,3},{3,2},{4,5},{5,4},{6,7},{7,6},{8,9},{9,8},{10,11... | collective-permute-start | bytes 589832 | tf_op jit(solution)/shard_map/ppermute | solution.py:324
  109.2 12.7 %collective-permute-start.29 = (bf16[4,2,32,384]{3,2,1,0:T(8,128)(2,1)S(1)}, bf16[4,2,32,384]{3,2,1,0:T(8,128)(2,1)S(1)}, u32[]{:S(2)}, u32[]{:S(2)}) collective-permute-start(bf16[4,2,32,384]{3,2,1,0:T(8,128)(2,1)S(1)} %collective-permute-done.21.refs_10_), channel_id=1, source_target_pairs={{0,1},{1,0},{2,3},{3,2},{4,5},{5,4},{6,7},{7,6},{8,9},{9,8},{10,11... | collective-permute-start | bytes 589832 | tf_op jit(solution)/shard_map/ppermute | solution.py:324
  109.7 13.8 %collective-permute-start.30 = (bf16[4,2,32,384]{3,2,1,0:T(8,128)(2,1)S(1)}, bf16[4,2,32,384]{3,2,1,0:T(8,128)(2,1)S(1)}, u32[]{:S(2)}, u32[]{:S(2)}) collective-permute-start(bf16[4,2,32,384]{3,2,1,0:T(8,128)(2,1)S(1)} %collective-permute-done.22.refs_11_), channel_id=1, source_target_pairs={{0,1},{1,0},{2,3},{3,2},{4,5},{5,4},{6,7},{7,6},{8,9},{9,8},{10,11... | collective-permute-start | bytes 589832 | tf_op jit(solution)/shard_map/ppermute | solution.py:324
  113.4 21.7 %collective-permute-start.9 = (bf16[8,2,32,384]{3,2,1,0:T(8,128)(2,1)S(1)}, bf16[8,2,32,384]{3,2,1,0:T(8,128)(2,1)S(1)}, u32[]{:S(2)}, u32[]{:S(2)}) collective-permute-start(bf16[8,2,32,384]{3,2,1,0:T(8,128)(2,1)S(1)} %get-tuple-element.18), channel_id=1, source_target_pairs={{0,2},{2,4},{4,6},{6,0},{8,10},{10,12},{12,14},{14,8},{16,18},{18,... | collective-permute-start | bytes 1179656 | tf_op jit(solution)/shard_map/ppermute | solution.py:383
  119.4 17.1 %collective-permute-start.10 = (bf16[8,2,32,384]{3,2,1,0:T(8,128)(2,1)S(1)}, bf16[8,2,32,384]{3,2,1,0:T(8,128)(2,1)S(1)}, u32[]{:S(2)}, u32[]{:S(2)}) collective-permute-start(bf16[8,2,32,384]{3,2,1,0:T(8,128)(2,1)S(1)} %get-tuple-element.19), channel_id=1, source_target_pairs={{0,4},{2,6},{4,0},{6,2},{8,12},{10,14},{12,8},{14,10},{16,20},{18,... | collective-permute-start | bytes 1179656 | tf_op jit(solution)/shard_map/ppermute | solution.py:383
  120.1 18.6 %collective-permute-start.11 = (bf16[8,2,32,384]{3,2,1,0:T(8,128)(2,1)S(1)}, bf16[8,2,32,384]{3,2,1,0:T(8,128)(2,1)S(1)}, u32[]{:S(2)}, u32[]{:S(2)}) collective-permute-start(bf16[8,2,32,384]{3,2,1,0:T(8,128)(2,1)S(1)} %get-tuple-element.20), channel_id=1, source_target_pairs={{0,6},{2,0},{4,2},{6,4},{8,14},{10,8},{12,10},{14,12},{16,22},{18,... | collective-permute-start | bytes 1179656 | tf_op jit(solution)/shard_map/ppermute | solution.py:383
  122.5 2.3 %collective-permute-start.31 = (bf16[4,2,32,384]{3,2,1,0:T(8,128)(2,1)S(1)}, bf16[4,2,32,384]{3,2,1,0:T(8,128)(2,1)S(1)}, u32[]{:S(2)}, u32[]{:S(2)}) collective-permute-start(bf16[4,2,32,384]{3,2,1,0:T(8,128)(2,1)S(1)} %collective-permute-done.23.refs_12_), channel_id=1, source_target_pairs={{0,1},{1,0},{2,3},{3,2},{4,5},{5,4},{6,7},{7,6},{8,9},{9,8},{10,11... | collective-permute-start | bytes 589832 | tf_op jit(solution)/shard_map/ppermute | solution.py:324
  124.2 1.9 %collective-permute-start.32 = (bf16[4,2,32,384]{3,2,1,0:T(8,128)(2,1)S(1)}, bf16[4,2,32,384]{3,2,1,0:T(8,128)(2,1)S(1)}, u32[]{:S(2)}, u32[]{:S(2)}) collective-permute-start(bf16[4,2,32,384]{3,2,1,0:T(8,128)(2,1)S(1)} %collective-permute-done.24.refs_13_), channel_id=1, source_target_pairs={{0,1},{1,0},{2,3},{3,2},{4,5},{5,4},{6,7},{7,6},{8,9},{9,8},{10,11... | collective-permute-start | bytes 589832 | tf_op jit(solution)/shard_map/ppermute | solution.py:324
  125.6 17.5 %collective-permute-start.12 = (bf16[8,2,32,384]{3,2,1,0:T(8,128)(2,1)S(1)}, bf16[8,2,32,384]{3,2,1,0:T(8,128)(2,1)S(1)}, u32[]{:S(2)}, u32[]{:S(2)}) collective-permute-start(bf16[8,2,32,384]{3,2,1,0:T(8,128)(2,1)S(1)} %get-tuple-element.17.refs_0_), channel_id=1, source_target_pairs={{0,1},{1,0},{2,3},{3,2},{4,5},{5,4},{6,7},{7,6},{8,9},{9,8},{10,11... | collective-permute-start | bytes 1179656 | tf_op jit(solution)/shard_map/ppermute | solution.py:324
  126.7 13.3 %collective-permute-start.33 = (bf16[4,2,32,384]{3,2,1,0:T(8,128)(2,1)S(1)}, bf16[4,2,32,384]{3,2,1,0:T(8,128)(2,1)S(1)}, u32[]{:S(2)}, u32[]{:S(2)}) collective-permute-start(bf16[4,2,32,384]{3,2,1,0:T(8,128)(2,1)S(1)} %collective-permute-done.25.refs_14_), channel_id=1, source_target_pairs={{0,1},{1,0},{2,3},{3,2},{4,5},{5,4},{6,7},{7,6},{8,9},{9,8},{10,11... | collective-permute-start | bytes 589832 | tf_op jit(solution)/shard_map/ppermute | solution.py:324
  135.2 7.9 %collective-permute-start.13 = (bf16[8,2,32,384]{3,2,1,0:T(8,128)(2,1)S(1)}, bf16[8,2,32,384]{3,2,1,0:T(8,128)(2,1)S(1)}, u32[]{:S(2)}, u32[]{:S(2)}) collective-permute-start(bf16[8,2,32,384]{3,2,1,0:T(8,128)(2,1)S(1)} %collective-permute-done.9.refs_1_), channel_id=1, source_target_pairs={{0,1},{1,0},{2,3},{3,2},{4,5},{5,4},{6,7},{7,6},{8,9},{9,8},{10,11... | collective-permute-start | bytes 1179656 | tf_op jit(solution)/shard_map/ppermute | solution.py:324
  136.4 6.6 %collective-permute-start.14 = (bf16[8,2,32,384]{3,2,1,0:T(8,128)(2,1)S(1)}, bf16[8,2,32,384]{3,2,1,0:T(8,128)(2,1)S(1)}, u32[]{:S(2)}, u32[]{:S(2)}) collective-permute-start(bf16[8,2,32,384]{3,2,1,0:T(8,128)(2,1)S(1)} %collective-permute-done.10.refs_2_), channel_id=1, source_target_pairs={{0,1},{1,0},{2,3},{3,2},{4,5},{5,4},{6,7},{7,6},{8,9},{9,8},{10,11... | collective-permute-start | bytes 1179656 | tf_op jit(solution)/shard_map/ppermute | solution.py:324
  138.7 4.4 %collective-permute-start.15 = (bf16[8,2,32,384]{3,2,1,0:T(8,128)(2,1)S(1)}, bf16[8,2,32,384]{3,2,1,0:T(8,128)(2,1)S(1)}, u32[]{:S(2)}, u32[]{:S(2)}) collective-permute-start(bf16[8,2,32,384]{3,2,1,0:T(8,128)(2,1)S(1)} %collective-permute-done.11.refs_3_), channel_id=1, source_target_pairs={{0,1},{1,0},{2,3},{3,2},{4,5},{5,4},{6,7},{7,6},{8,9},{9,8},{10,11... | collective-permute-start | bytes 1179656 | tf_op jit(solution)/shard_map/ppermute | solution.py:324
  140.7 1.7 collective-permute-start.34
  143.1 0.9 copy-start.5
  144.0 0.9 copy-start.7
  144.9 0.9 copy-start.9
  152.4 0.9 copy-start.25
  (23 other events, 18.7 us)

commit v2 on v1

--- a/solution.py
+++ b/solution.py
@@ -21,9 +21,7 @@
 HALF = 384
 TSLOT = 68
 TIMES = 4
-ROUNDS = 8
-SINGLE = 8
-PER_STEP = 4
+PER_STEP = 17
 STRIP = 16
 GROUP = 8
 
@@ -125,34 +123,41 @@
     )(*args)
 
 
-def correlate_body(tiles, sections, place_ref, *refs):
-    out_ref, raw_late, raw_soon, lanes, turned, held, in_sems, out_sems = refs[-8:]
+def correlate_body(chunk, tiles, sections, place_ref, *refs):
+    out_ref, raw, lanes, turned, held, in_sems, add_sems, out_sems = refs[-8:]
     blocks = HALF // PANEL
-    frames = BLOCKS * raw_late.shape[4]
+    frames = lanes.shape[1]
     turn, group = place_ref[0], place_ref[1]
 
-    copies = [[], []]
-    for index, source in enumerate(refs[: 2 * TIMES]):
-        which, step = index // TIMES, index % TIMES
-        half = group if which == 0 else 1 - group
-        copies[0].append(
-            pltpu.make_async_copy(source, raw_late.at[half, step], in_sems.at[0, which, step])
+    copies = [
+        pltpu.make_async_copy(
+            refs[index], raw.at[index // TIMES, index % TIMES], in_sems.at[index]
         )
-    for index, source in enumerate(refs[2 * TIMES : 2 * TIMES + 2 * ROUNDS]):
-        which, step = index // ROUNDS, index % ROUNDS
-        half = group if which == 0 else 1 - group
-        if step >= SINGLE:
-            source = source.at[pl.ds(TIMES, TIMES)]
-        copies[1].append(
-            pltpu.make_async_copy(
-                source, raw_soon.at[half, step % N_SITE, step // N_SITE], in_sems.at[1, which, step]
-            )
+        for index in range(2 * TIMES)
+    ]
+    for copy in copies:
+        copy.start()
+
+    def earlier(index):
+        span = pl.ds(index * PER_STEP, PER_STEP)
+        return pltpu.make_async_copy(
+            refs[2 * TIMES].at[0, 0, span], held.at[span], add_sems.at[index]
         )
-    for copy in copies[1] + copies[0]:
-        copy.start()
-
-    counts = [sections[2 * s] for s in range(N_SITE)]
-    starts = [sections[2 * s + 1] for s in range(N_SITE)]
+
+    def repeat(count, action):
+        def step(index, carry):
+            action(index)
+            return carry
+
+        lax.fori_loop(0, count, step, 0)
+
+    if chunk == 1:
+        repeat(TSLOT // PER_STEP, lambda index: earlier(index).start())
+    for copy in copies:
+        copy.wait()
+
+    counts = [sections[0, s] for s in range(N_SITE)]
+    starts = [sections[1, s] for s in range(N_SITE)]
     offsets = [jnp.int32(0)]
     for s in range(N_SITE - 1):
         offsets.append(offsets[-1] + counts[s])
@@ -163,7 +168,7 @@
             got = jnp.where(s == index, values[index], got)
         return got
 
-    def fill(chunk, panel):
+    def fill(panel):
         low = panel * PANEL
         high = low + PANEL - 1
         s_low = jnp.int32(0)
@@ -179,11 +184,15 @@
             half = block // blocks
             at = pl.multiple_of((block - half * blocks) * PANEL, PANEL)
             slot = (turn - s + N_SITE) % N_SITE
-            if chunk == 0:
-                value = raw_late[half, :, pl.ds(2 * slot, 2), part, :, pl.ds(at, PANEL)]
-            else:
-                value = raw_soon[half, slot, :, :, part, :, pl.ds(at, PANEL)]
-            return value.reshape(frames, PANEL)
+            values = []
+            for which in range(2):
+                far = (half + group + which) % 2
+                if chunk == 0:
+                    value = raw[which, :, 2 * slot + far, part, :, pl.ds(at, PANEL)]
+                else:
+                    value = raw[which, slot, far, :, part, :, pl.ds(at, PANEL)]
+                values.append(value.reshape(frames // 2, PANEL))
+            return jnp.concatenate(values, axis=0)
 
         def window(s, part):
             at = low + pick(starts, s) - pick(offsets, s)
@@ -192,9 +201,8 @@
             return pltpu.roll(mixed, (PANEL - shift) & 127, 1)
 
         def put(part, value):
-            span = slice(chunk * frames, (chunk + 1) * frames)
-            lanes[panel, span, part * PANEL : (part + 1) * PANEL] = value
-            turned[panel, part * PANEL : (part + 1) * PANEL, span] = value.T
+            lanes[panel, :, part * PANEL : (part + 1) * PANEL] = value
+            turned[panel, part * PANEL : (part + 1) * PANEL, :] = value.T
 
         @pl.when(s_low == s_high)
         def _():
@@ -206,32 +214,24 @@
             for part in range(2):
                 put(part, jnp.where(lane < bound, window(s_low, part), window(s_high, part)))
 
-    def repeat(count, action):
-        def step(index, carry):
-            action(index)
-            return carry
-
-        lax.fori_loop(0, count, step, 0)
-
-    for chunk in (1, 0):
-        for copy in copies[chunk]:
-            copy.wait()
-        repeat(PANELS, functools.partial(fill, chunk))
-
+    repeat(PANELS, fill)
     scale = 1.0 / FB
 
     def result(at):
         return pltpu.make_async_copy(held.at[at], out_ref.at[0, 0, at], out_sems.at[at])
 
     def multiply(index):
-        base = (group * TSLOT + index * PER_STEP) * 2
+        if chunk == 1:
+            earlier(index).wait()
         for slot in range(PER_STEP):
-            left = turned[tiles[base + 2 * slot]]
-            right = lanes[tiles[base + 2 * slot + 1]]
+            at = index * PER_STEP + slot
+            left = turned[tiles[group, 0, at]]
+            right = lanes[tiles[group, 1, at]]
             gram = jnp.dot(left, right, preferred_element_type=jnp.float32)
-            at = index * PER_STEP + slot
-            held[at, 0] = (gram[:PANEL, :PANEL] + gram[PANEL:, PANEL:]) * scale
-            held[at, 1] = (gram[PANEL:, :PANEL] - gram[:PANEL, PANEL:]) * scale
+            real = (gram[:PANEL, :PANEL] + gram[PANEL:, PANEL:]) * scale
+            imag = (gram[PANEL:, :PANEL] - gram[:PANEL, PANEL:]) * scale
+            held[at, 0] = real + held[at, 0] if chunk == 1 else real
+            held[at, 1] = imag + held[at, 1] if chunk == 1 else imag
         for slot in range(PER_STEP):
             result(index * PER_STEP + slot).start()
 
@@ -239,35 +239,36 @@
     repeat(TSLOT, lambda at: result(at).wait())
 
 
-def correlate_call(tiles, sections, place, pieces):
-    count = pieces[0].shape[2]
+def correlate_call(tiles, sections, place, pieces, sums):
+    chunk, count = len(sums), pieces[0].shape[-2]
+    frames = BLOCKS * count
     resident = pl.BlockSpec(memory_space=pltpu.HBM)
     return pl.pallas_call(
-        correlate_body,
-        name="correlate",
+        functools.partial(correlate_body, chunk),
         out_shape=jax.ShapeDtypeStruct((1, 1, TSLOT, 2, PANEL, PANEL), jnp.float32),
         grid_spec=pltpu.PrefetchScalarGridSpec(
             num_scalar_prefetch=3,
             grid=(),
-            in_specs=[resident] * len(pieces),
+            in_specs=[resident] * (2 * TIMES + chunk),
             out_specs=resident,
             scratch_shapes=[
-                pltpu.VMEM((2, TIMES, ROUNDS, 2, count, HALF), jnp.bfloat16),
-                pltpu.VMEM((2, N_SITE, 2, TIMES, 2, count, HALF), jnp.bfloat16),
-                pltpu.VMEM((PANELS, FB, 2 * PANEL), jnp.bfloat16),
-                pltpu.VMEM((PANELS, 2 * PANEL, FB), jnp.bfloat16),
+                pltpu.VMEM((2, TIMES) + pieces[0].shape, jnp.bfloat16),
+                pltpu.VMEM((PANELS, frames, 2 * PANEL), jnp.bfloat16),
+                pltpu.VMEM((PANELS, 2 * PANEL, frames), jnp.bfloat16),
                 pltpu.VMEM((TSLOT, 2, PANEL, PANEL), jnp.float32),
-                pltpu.SemaphoreType.DMA((2, 2, ROUNDS)),
+                pltpu.SemaphoreType.DMA((2 * TIMES,)),
+                pltpu.SemaphoreType.DMA((TSLOT // PER_STEP,)),
                 pltpu.SemaphoreType.DMA((TSLOT,)),
             ],
         ),
-        compiler_params=pltpu.CompilerParams(vmem_limit_bytes=32 << 20),
+        input_output_aliases={3 + 2 * TIMES: 0} if chunk else {},
+        compiler_params=pltpu.CompilerParams(vmem_limit_bytes=24 << 20),
         cost_estimate=pl.CostEstimate(
-            flops=TSLOT * 2 * 256 * 256 * FB,
-            bytes_accessed=TSLOT * 2 * PANEL * PANEL * 4 + 4 * FB * N_SITE * CAP,
+            flops=TSLOT * 2 * 256 * 256 * frames,
+            bytes_accessed=(1 + chunk) * TSLOT * 2 * PANEL * PANEL * 4 + 4 * frames * N_SITE * CAP,
             transcendentals=0,
         ),
-    )(tiles, sections, place, *pieces)
+    )(tiles, sections, place, *pieces, *sums)
 
 
 def move_blocks(keys, sources, shapes, moves):
@@ -306,13 +307,15 @@
     return lax.ppermute(value, axis, [(source, source + 1) for source in range(count - 1)])
 
 
-def across(turn, flip):
+def across(turn):
     pairs = []
     for site in range(N_SITE):
         for z in range(8):
-            goal = 2 * ((z // 2 + site + turn) % N_SITE) + ((z % 2) ^ flip)
             for y in range(TIMES):
-                pairs.append((site * NCHAN + z * TIMES + y, z // 2 * NCHAN + goal * TIMES + y))
+                for core in range(2):
+                    goal = 2 * ((z // 2 + site + turn) % N_SITE) + ((z + core) % 2)
+                    source = (site * NCHAN + z * TIMES + y) * 2 + core
+                    pairs.append((source, (z // 2 * NCHAN + goal * TIMES + y) * 2 + core))
     return pairs
 
 
@@ -331,61 +334,70 @@
     site, chan, group = (lax.axis_index(name) for name in ("site", "chan", "grp"))
     z, y = chan // TIMES, chan % TIMES
     place = jnp.stack([(z // 2 - site) % N_SITE, group])
-    tiles, section_list = tile_list.reshape(-1), sections.reshape(-1)
+    tiles, section_list = jnp.swapaxes(tile_list, 1, 2), sections.T
     strips = LOCAL // STRIP // 2
-    rounds = [(turn, flip) for flip in range(2) for turn in range(N_SITE)]
-    goals = [2 * ((z // 2 + site + turn) % N_SITE) + ((z % 2) ^ flip) for turn, flip in rounds]
-    keys = jnp.stack(goals + [(y + step) % TIMES for step in range(TIMES)])
-    joint = ("site", "chan")
+    even = [2 * ((z // 2 + site + turn) % N_SITE) for turn in range(N_SITE)]
+    mine = [goal + (z + group) % 2 for goal in even]
+    theirs = [goal + (z + group + 1) % 2 for goal in even]
+    keys = jnp.stack(mine + theirs + [(y + step) % TIMES for step in range(TIMES)])
+    everyone = ("site", "chan", "grp")
     block = (2, STRIP * strips, HALF)
-
-    soon = filter_call(
-        trig, tap_table, voltages, None, strips, strips, lambda m: m % TIMES * 8 + m // TIMES
+    turns, steps = range(N_SITE), range(TIMES)
+
+    def far(payload):
+        moved = []
+        for turn in turns:
+            moved.append(lax.ppermute(payload[turn], everyone, across(turn)))
+        return moved
+
+    def near(payload):
+        moved = list(payload)
+        for step in range(1, TIMES):
+            moved[step] = lax.ppermute(payload[step], "chan", along(step))
+        return moved
+
+    def blocks(sources, shapes, moves):
+        return move_blocks(keys, sources, shapes, moves)
+
+    one = filter_call(trig, tap_table, voltages, None, strips, strips, lambda m: m)
+    one = one.reshape((8, TIMES) + block)
+    moves = [(0, ((N_SITE + turn,),), 0, (turn,)) for turn in turns]
+    given = blocks([one], [(N_SITE, TIMES) + block], moves)[0]
+    back = swap(given)
+    moves = [(0, ((turn,),), turn, (0,)) for turn in turns]
+    moves += [(1, (turn,), turn, (1,)) for turn in turns]
+    got = far(blocks([one, back], [(2, TIMES) + block] * N_SITE, moves))
+    moves = [
+        (turn, (side, (2 * N_SITE + step,)), step, (2 * turn + side,))
+        for step in steps
+        for turn in turns
+        for side in range(2)
+    ]
+    own_one = near(blocks(got, [(2 * N_SITE,) + block] * TIMES, moves))
+
+    two = filter_call(
+        trig, tap_table, voltages, halo, 0, strips, lambda m: m % TIMES * 8 + m // TIMES
     ).reshape((TIMES, 8) + block)
-    held = []
-    for step in range(TIMES):
-        piece = lax.dynamic_index_in_dim(soon, (y + step) % TIMES, 0, keepdims=False)
-        if step:
-            piece = lax.ppermute(piece, "chan", along(step))
-        held.append(piece)
-
-    late = filter_call(trig, tap_table, voltages, halo, 0, strips, lambda m: m)
-    late = late.reshape((8, TIMES) + block)
-    late_got, soon_own = [None] * ROUNDS, [None] * ROUNDS
-    for index in range(SINGLE):
-        piece = lax.dynamic_index_in_dim(late, goals[index], 0, keepdims=False)
-        late_got[index] = lax.ppermute(piece, joint, across(*rounds[index]))
-
-    moves, shapes = [], []
-    for index in list(range(SINGLE, ROUNDS)) + list(range(SINGLE)):
-        both = index >= SINGLE
-        if both:
-            moves += [(TIMES, ((index,), part), len(shapes), (part,)) for part in range(TIMES)]
-        moves += [
-            (step, ((index,),), len(shapes), (TIMES * both + step,)) for step in range(TIMES)
-        ]
-        shapes.append((TIMES * (1 + both),) + block)
-    ready = move_blocks(keys, held, shapes, moves)
-    for number, piece in enumerate(ready):
-        index = (number + SINGLE) % ROUNDS
-        soon_own[index] = lax.ppermute(piece, joint, across(*rounds[index]))
-        if index >= SINGLE:
-            late_got[index] = soon_own[index]
-
+    held = near(
+        [
+            lax.dynamic_index_in_dim(two, (y + step) % TIMES, 0, keepdims=False)
+            for step in steps
+        ],
+    )
     moves = [
-        (index, ((ROUNDS + step,),), step, (index % N_SITE * 2 + index // N_SITE,))
-        for step in range(TIMES)
-        for index in range(ROUNDS)
+        (step, ((N_SITE + turn,),), 0, (turn, step)) for turn in turns for step in steps
     ]
-    shapes = [(ROUNDS,) + block] * TIMES
-    late_own = list(move_blocks(keys, late_got, shapes, moves))
-    for step in range(1, TIMES):
-        late_own[step] = lax.ppermute(late_own[step], "chan", along(step))
-
-    pieces = []
-    for own in (late_own, soon_own):
-        pieces += own + [swap(piece) for piece in own]
-    return correlate_call(tiles, section_list, place, pieces)
+    given = blocks(held, [(N_SITE, TIMES) + block], moves)[0]
+    back = swap(given)
+    moves = [(step, ((turn,),), turn, (0, step)) for turn in turns for step in steps]
+    moves += [(TIMES, (turn,), turn, (1,)) for turn in turns]
+    own_two = far(blocks(held + [back], [(2, TIMES) + block] * N_SITE, moves))
+
+    sums = []
+    for own in (own_one, own_two):
+        pieces = own + [swap(piece) for piece in own]
+        sums = [correlate_call(tiles, section_list, place, pieces, sums)]
+    return sums[0]
 
 
 def solution(mesh):

time: 181 us -> 186 us (1.028)
  the two profiles are of different devices: /device:TPU:13 before, /device:TPU:1 now
where the time goes in v2:
time: 186 us; the launch traced here: 185 us
  waiting for transfers between devices  89.9 us (48%)
  starting transfers between devices  45.2 us (24%)
  Pallas kernels  40 us (22%)
  local copies, waits for them, and re-layouts  8.68 us (5%)
    ppermute x8, waiting for transfers between devices, far(): moved.append(lax.ppermute(payload[turn], everyone, across(turn)))  59.2 us
    ppermute x6, waiting for transfers between devices, near(): moved[step] = lax.ppermute(payload[step], 'chan', along(step))  30.7 us
    ppermute x8, starting transfers between devices, far(): moved.append(lax.ppermute(payload[turn], everyone, across(turn)))  30.1 us
    pallas_call x2, Pallas kernels, correlate_call(): pl.pallas_call(functools.partial(correlate_body, chunk), out_shape=jax.Sh...  22.1 us
    pallas_call x5, Pallas kernels, move_blocks(): pl.pallas_call(body, out_shape=[jax.ShapeDtypeStruct(shape, jnp.bfloat16)...  11.7 us
    ppermute x6, starting transfers between devices, near(): moved[step] = lax.ppermute(payload[step], 'chan', along(step))  6.29 us
    pallas_call x2, Pallas kernels, filter_call(): pl.pallas_call(functools.partial(filter_body, slot_of, halo is not None),...  6.15 us
    unnamed x20, local copies, waits for them, and re-layouts  4.74 us
  transfers between devices with their start and end apart: 25, of which 8 were waited for; matrix products, arithmetic and copies ran while one was open for 1% of the time, Pallas kernels for 16%

profile of v2, /device:TPU:1, one launch (start us, length us, event | category | flops | bytes accessed | tf_op | source)
XLA Modules:
  0.0 184.6 jit_solution(15913753535389346459)
XLA Ops:
  0.0 1.8 slice.3
  1.8 4.0 %collective-permute-start = (bf16[2,256,384]{2,1,0:T(8,128)(2,1)}, bf16[2,256,384]{2,1,0:T(8,128)(2,1)S(1)}, u32[]{:S(2)}, u32[]{:S(2)}) collective-permute-start(bf16[2,256,384]{2,1,0:T(8,128)(2,1)} %slice.3), channel_id=1, source_target_pairs={{0,2},{2,4},{4,6},{6,8},{8,10},{10,12},{12,14},{14,16},{16,18},{18... | collective-permute-start | bytes 1179656 | tf_op jit(solution)/shard_map/ppermute | solution.py:307
  6.0 0.7 rev.3
  6.7 0.1 stack.98
  7.4 0.6 stack.90.key_ref
  8.0 1.9 %copy-done = bf16[2,2048,384]{2,1,0:T(8,128)(2,1)S(1)} copy-done((bf16[2,2048,384]{2,1,0:T(8,128)(2,1)S(1)}, bf16[2,2048,384]{2,1,0:T(8,128)(2,1)}, u32[]{:S(2)}) %copy-start) | copy-done | bytes 3145752
  9.9 0.8 copy-done.4
  10.7 3.1 %shard_map.58 = bf16[32,2,32,384]{3,2,1,0:T(8,128)(2,1)S(1)} custom-call(f32[32,512]{1,0:T(8,128)S(1)} %copy-done.4, f32[8,512]{1,0:T(8,128)S(1)} %stack.99.tap_ref, bf16[2,2048,384]{2,1,0:T(8,128)(2,1)S(1)} %copy-done, bf16[2,2048,384]{2,1,0:T(8,128)(2,1)S(1)} %copy-done), custom_call_target="tpu_custom_call" | custom-call | flops 1610612736 | bytes 3145728 | tf_op jit(solution)/shard_map/pallas_call | solution.py:104
  13.8 1.5 shard_map.59
  15.3 1.1 copy-done.2
  16.5 1.0 collective-permute-start.13
  17.4 0.8 copy-done.5
  18.3 3.1 %shard_map.55 = bf16[32,2,32,384]{3,2,1,0:T(8,128)(2,1)S(1)} custom-call(f32[32,512]{1,0:T(8,128)S(1)} %copy-done.5, f32[8,512]{1,0:T(8,128)S(1)} %stack.99.tap_ref, bf16[2,2048,384]{2,1,0:T(8,128)(2,1)S(1)} %copy-done.1, bf16[2,2048,384]{2,1,0:T(8,128)(2,1)S(1)} %copy-done.1, bf16[2,256,384]{2,1,0:T(8,128)(2,1)S(1)} %collective-permute-done.rest_0_), custom_call_target="tpu_custom_call" | custom-call | flops 1610612736 | bytes 3145728 | tf_op jit(solution)/shard_map/pallas_call | solution.py:104
  21.4 0.2 dynamic-slice_bitcast_fusion
  21.6 2.8 %collective-permute-start.3 = (bf16[8,2,32,384]{3,2,1,0:T(8,128)(2,1)S(1)}, bf16[8,2,32,384]{3,2,1,0:T(8,128)(2,1)S(1)}, u32[]{:S(2)}, u32[]{:S(2)}) collective-permute-start(bf16[8,2,32,384]{3,2,1,0:T(8,128)(2,1)S(1)} %get-tuple-element.29), channel_id=1, source_target_pairs={{0,6},{2,0},{4,2},{6,4},{8,14},{10,8},{12,10},{14,12},{16,22},{18,... | collective-permute-start | bytes 1179656 | tf_op jit(solution)/shard_map/ppermute | solution.py:356
  24.4 0.3 collective-permute-start.2
  24.7 0.4 collective-permute-start.1
  25.1 16.0 %collective-permute-done.3.refs_3_ = bf16[8,2,32,384]{3,2,1,0:T(8,128)(2,1)S(1)} collective-permute-done((bf16[8,2,32,384]{3,2,1,0:T(8,128)(2,1)S(1)}, bf16[8,2,32,384]{3,2,1,0:T(8,128)(2,1)S(1)}, u32[]{:S(2)}, u32[]{:S(2)}) %collective-permute-start.3) | collective-permute-done | bytes 393248 | tf_op jit(solution)/shard_map/ppermute | solution.py:356
  41.1 4.2 %collective-permute-done.1.refs_1_ = bf16[8,2,32,384]{3,2,1,0:T(8,128)(2,1)S(1)} collective-permute-done((bf16[8,2,32,384]{3,2,1,0:T(8,128)(2,1)S(1)}, bf16[8,2,32,384]{3,2,1,0:T(8,128)(2,1)S(1)}, u32[]{:S(2)}, u32[]{:S(2)}) %collective-permute-start.1) | collective-permute-done | bytes 393248 | tf_op jit(solution)/shard_map/ppermute | solution.py:356
  45.3 1.7 shard_map.56
  47.1 0.6 collective-permute-start.4
  47.7 2.8 %shard_map.60 = (bf16[2,4,2,32,384]{4,3,2,1,0:T(8,128)(2,1)S(1)}, bf16[2,4,2,32,384]{4,3,2,1,0:T(8,128)(2,1)S(1)}, bf16[2,4,2,32,384]{4,3,2,1,0:T(8,128)(2,1)S(1)}, bf16[2,4,2,32,384]{4,3,2,1,0:T(8,128)(2,1)S(1)}) custom-call(s32[12]{0:T(128)S(1)} %copy-done.7, bf16[8,4,2,32,384]{4,3,2,1,0:T(8,128)(2,1)S(1)} %bitcast.27, ...), custom_call_target="tpu_custom_call" | custom-call | tf_op jit(solution)/shard_map/pallas_call | solution.py:291
  50.5 3.5 %collective-permute-start.14 = (bf16[2,4,2,32,384]{4,3,2,1,0:T(8,128)(2,1)S(1)}, bf16[2,4,2,32,384]{4,3,2,1,0:T(8,128)(2,1)S(1)}, u32[]{:S(2)}, u32[]{:S(2)}) collective-permute-start(bf16[2,4,2,32,384]{4,3,2,1,0:T(8,128)(2,1)S(1)} %get-tuple-element.21), channel_id=1, source_target_pairs={{0,0},{1,9},{2,2},{3,11},{4,4},{5,13},{6,6},{7,15},{8,8},{9,1},{10... | collective-permute-start | bytes 1179656 | tf_op jit(solution)/shard_map/ppermute | solution.py:350
  54.1 5.6 %collective-permute-start.15 = (bf16[2,4,2,32,384]{4,3,2,1,0:T(8,128)(2,1)S(1)}, bf16[2,4,2,32,384]{4,3,2,1,0:T(8,128)(2,1)S(1)}, u32[]{:S(2)}, u32[]{:S(2)}) collective-permute-start(bf16[2,4,2,32,384]{4,3,2,1,0:T(8,128)(2,1)S(1)} %get-tuple-element.22), channel_id=1, source_target_pairs={{0,16},{1,25},{2,18},{3,27},{4,20},{5,29},{6,22},{7,31},{8,24},{9,... | collective-permute-start | bytes 1179656 | tf_op jit(solution)/shard_map/ppermute | solution.py:350
  59.6 8.6 %collective-permute-start.16 = (bf16[2,4,2,32,384]{4,3,2,1,0:T(8,128)(2,1)S(1)}, bf16[2,4,2,32,384]{4,3,2,1,0:T(8,128)(2,1)S(1)}, u32[]{:S(2)}, u32[]{:S(2)}) collective-permute-start(bf16[2,4,2,32,384]{4,3,2,1,0:T(8,128)(2,1)S(1)} %get-tuple-element.23), channel_id=1, source_target_pairs={{0,32},{1,41},{2,34},{3,43},{4,36},{5,45},{6,38},{7,47},{8,40},{9,... | collective-permute-start | bytes 1179656 | tf_op jit(solution)/shard_map/ppermute | solution.py:350
  68.2 2.0 %collective-permute-start.17 = (bf16[2,4,2,32,384]{4,3,2,1,0:T(8,128)(2,1)S(1)}, bf16[2,4,2,32,384]{4,3,2,1,0:T(8,128)(2,1)S(1)}, u32[]{:S(2)}, u32[]{:S(2)}) collective-permute-start(bf16[2,4,2,32,384]{4,3,2,1,0:T(8,128)(2,1)S(1)} %get-tuple-element.24), channel_id=1, source_target_pairs={{0,48},{1,57},{2,50},{3,59},{4,52},{5,61},{6,54},{7,63},{8,56},{9,... | collective-permute-start | bytes 1179656 | tf_op jit(solution)/shard_map/ppermute | solution.py:350
  70.2 23.9 %collective-permute-done.15.refs_1_ = bf16[2,4,2,32,384]{4,3,2,1,0:T(8,128)(2,1)S(1)} collective-permute-done((bf16[2,4,2,32,384]{4,3,2,1,0:T(8,128)(2,1)S(1)}, bf16[2,4,2,32,384]{4,3,2,1,0:T(8,128)(2,1)S(1)}, u32[]{:S(2)}, u32[]{:S(2)}) %collective-permute-start.15) | collective-permute-done | bytes 393248 | tf_op jit(solution)/shard_map/ppermute | solution.py:350
  94.1 3.8 %collective-permute-done.16.refs_2_ = bf16[2,4,2,32,384]{4,3,2,1,0:T(8,128)(2,1)S(1)} collective-permute-done((bf16[2,4,2,32,384]{4,3,2,1,0:T(8,128)(2,1)S(1)}, bf16[2,4,2,32,384]{4,3,2,1,0:T(8,128)(2,1)S(1)}, u32[]{:S(2)}, u32[]{:S(2)}) %collective-permute-start.16) | collective-permute-done | bytes 393248 | tf_op jit(solution)/shard_map/ppermute | solution.py:350
  97.9 2.9 %collective-permute-done.17.refs_3_ = bf16[2,4,2,32,384]{4,3,2,1,0:T(8,128)(2,1)S(1)} collective-permute-done((bf16[2,4,2,32,384]{4,3,2,1,0:T(8,128)(2,1)S(1)}, bf16[2,4,2,32,384]{4,3,2,1,0:T(8,128)(2,1)S(1)}, u32[]{:S(2)}, u32[]{:S(2)}) %collective-permute-start.17) | collective-permute-done | bytes 393248 | tf_op jit(solution)/shard_map/ppermute | solution.py:350
  100.8 2.9 %shard_map.61 = (bf16[8,2,32,384]{3,2,1,0:T(8,128)(2,1)S(1)}, bf16[8,2,32,384]{3,2,1,0:T(8,128)(2,1)S(1)}, bf16[8,2,32,384]{3,2,1,0:T(8,128)(2,1)S(1)}, bf16[8,2,32,384]{3,2,1,0:T(8,128)(2,1)S(1)}) custom-call(s32[12]{0:T(128)S(1)} %copy-done.7, bf16[2,4,2,32,384]{4,3,2,1,0:T(8,128)(2,1)S(1)} %collective-permute-done.14.refs_0_, ...), custom_call_target="tpu_custom_call" | custom-call | tf_op jit(solution)/shard_map/pallas_call | solution.py:291
  103.7 0.1 collective-permute-start.18
  103.8 1.5 collective-permute-start.19
  105.3 1.2 collective-permute-start.20
  106.5 2.8 %shard_map.57 = (bf16[2,4,2,32,384]{4,3,2,1,0:T(8,128)(2,1)S(1)}, bf16[2,4,2,32,384]{4,3,2,1,0:T(8,128)(2,1)S(1)}, bf16[2,4,2,32,384]{4,3,2,1,0:T(8,128)(2,1)S(1)}, bf16[2,4,2,32,384]{4,3,2,1,0:T(8,128)(2,1)S(1)}) custom-call(s32[12]{0:T(128)S(1)} %copy-done.7, bf16[8,2,32,384]{3,2,1,0:T(8,128)(2,1)S(1)} %get-tuple-element.32.refs_0_, ...), custom_call_target="tpu_custom_call" | custom-call | tf_op jit(solution)/shard_map/pallas_call | solution.py:291
  109.3 1.9 %collective-permute-start.5 = (bf16[2,4,2,32,384]{4,3,2,1,0:T(8,128)(2,1)S(1)}, bf16[2,4,2,32,384]{4,3,2,1,0:T(8,128)(2,1)S(1)}, u32[]{:S(2)}, u32[]{:S(2)}) collective-permute-start(bf16[2,4,2,32,384]{4,3,2,1,0:T(8,128)(2,1)S(1)} %get-tuple-element.17), channel_id=1, source_target_pairs={{0,0},{1,9},{2,2},{3,11},{4,4},{5,13},{6,6},{7,15},{8,8},{9,1},{10... | collective-permute-start | bytes 1179656 | tf_op jit(solution)/shard_map/ppermute | solution.py:350
  111.2 10.5 %collective-permute-done.18.refs_1_ = bf16[8,2,32,384]{3,2,1,0:T(8,128)(2,1)S(1)} collective-permute-done((bf16[8,2,32,384]{3,2,1,0:T(8,128)(2,1)S(1)}, bf16[8,2,32,384]{3,2,1,0:T(8,128)(2,1)S(1)}, u32[]{:S(2)}, u32[]{:S(2)}) %collective-permute-start.18) | collective-permute-done | bytes 393248 | tf_op jit(solution)/shard_map/ppermute | solution.py:356
  121.7 1.9 %collective-permute-start.6 = (bf16[2,4,2,32,384]{4,3,2,1,0:T(8,128)(2,1)S(1)}, bf16[2,4,2,32,384]{4,3,2,1,0:T(8,128)(2,1)}, u32[]{:S(2)}, u32[]{:S(2)}) collective-permute-start(bf16[2,4,2,32,384]{4,3,2,1,0:T(8,128)(2,1)S(1)} %get-tuple-element.18), channel_id=1, source_target_pairs={{0,16},{1,25},{2,18},{3,27},{4,20},{5,29},{6,22},{7,31},{8,24},{9,... | collective-permute-start | bytes 1179656 | tf_op jit(solution)/shard_map/ppermute | solution.py:350
  123.7 3.7 %collective-permute-start.7 = (bf16[2,4,2,32,384]{4,3,2,1,0:T(8,128)(2,1)S(1)}, bf16[2,4,2,32,384]{4,3,2,1,0:T(8,128)(2,1)}, u32[]{:S(2)}, u32[]{:S(2)}) collective-permute-start(bf16[2,4,2,32,384]{4,3,2,1,0:T(8,128)(2,1)S(1)} %get-tuple-element.19), channel_id=1, source_target_pairs={{0,32},{1,41},{2,34},{3,43},{4,36},{5,45},{6,38},{7,47},{8,40},{9,... | collective-permute-start | bytes 1179656 | tf_op jit(solution)/shard_map/ppermute | solution.py:350
  127.3 3.0 %collective-permute-start.8 = (bf16[2,4,2,32,384]{4,3,2,1,0:T(8,128)(2,1)S(1)}, bf16[2,4,2,32,384]{4,3,2,1,0:T(8,128)(2,1)}, u32[]{:S(2)}, u32[]{:S(2)}) collective-permute-start(bf16[2,4,2,32,384]{4,3,2,1,0:T(8,128)(2,1)S(1)} %get-tuple-element.20), channel_id=1, source_target_pairs={{0,48},{1,57},{2,50},{3,59},{4,52},{5,61},{6,54},{7,63},{8,56},{9,... | collective-permute-start | bytes 1179656 | tf_op jit(solution)/shard_map/ppermute | solution.py:350
  130.4 1.8 collective-permute-start.22
  132.2 0.3 collective-permute-start.23
  132.5 24.1 %collective-permute-done.6.refs_1_ = bf16[2,4,2,32,384]{4,3,2,1,0:T(8,128)(2,1)} collective-permute-done((bf16[2,4,2,32,384]{4,3,2,1,0:T(8,128)(2,1)S(1)}, bf16[2,4,2,32,384]{4,3,2,1,0:T(8,128)(2,1)}, u32[]{:S(2)}, u32[]{:S(2)}) %collective-permute-start.6) | collective-permute-done | bytes 393248 | tf_op jit(solution)/shard_map/ppermute | solution.py:350
  156.6 0.5 collective-permute-start.9
  157.1 4.5 %collective-permute-done.8.refs_3_ = bf16[2,4,2,32,384]{4,3,2,1,0:T(8,128)(2,1)} collective-permute-done((bf16[2,4,2,32,384]{4,3,2,1,0:T(8,128)(2,1)S(1)}, bf16[2,4,2,32,384]{4,3,2,1,0:T(8,128)(2,1)}, u32[]{:S(2)}, u32[]{:S(2)}) %collective-permute-start.8) | collective-permute-done | bytes 393248 | tf_op jit(solution)/shard_map/ppermute | solution.py:350
  161.5 0.5 collective-permute-start.11
  162.0 0.1 collective-permute-start.12
  162.2 10.9 %shard_map.62.refs_8_ = f32[1,1,68,2,128,128]{5,4,3,2,1,0:T(8,128)} custom-call(s32[2,2,68]{2,1,0:T(2,128)S(1)} %bitcast.29, s32[2,4]{1,0:T(2,128)S(1)} %bitcast.31, s32[2]{0:T(128)S(1)} %pad_add_fusion.place_ref, bf16[8,2,32,384]{3,2,1,0:T(8,128)(2,1)S(1)} %get-tuple-element.25.refs_0_, bf16[8,2,32,384]{3,2,1,0:T(8,128)(2,1)S(1)} %collective-permute-done.18.refs_1_, ...), custom_call_target="tpu_custom_call" | custom-call | flops 2281701376 | bytes 12058624 | tf_op jit(solution)/shard_map/pallas_call | solution.py:246
  173.2 11.3 %shard_map.63 = f32[1,1,68,2,128,128]{5,4,3,2,1,0:T(8,128)} custom-call(s32[2,2,68]{2,1,0:T(2,128)S(1)} %bitcast.30, s32[2,4]{1,0:T(2,128)S(1)} %bitcast.32, s32[2]{0:T(128)S(1)} %pad_add_fusion.place_ref, bf16[2,4,2,32,384]{4,3,2,1,0:T(8,128)(2,1)S(1)} %collective-permute-done.5.refs_0_, ...), custom_call_target="tpu_custom_call", output_to_operand_aliasing={{}: (11, {})} | custom-call | flops 2281701376 | bytes 20971520 | tf_op jit(solution)/shard_map/pallas_call | solution.py:246
  (46 shorter events, 0.8 us)
Async XLA Ops:
  1.8 15.6 %collective-permute-start = (bf16[2,256,384]{2,1,0:T(8,128)(2,1)}, bf16[2,256,384]{2,1,0:T(8,128)(2,1)S(1)}, u32[]{:S(2)}, u32[]{:S(2)}) collective-permute-start(bf16[2,256,384]{2,1,0:T(8,128)(2,1)} %slice.3), channel_id=1, source_target_pairs={{0,2},{2,4},{4,6},{6,8},{8,10},{10,12},{12,14},{14,16},{16,18},{18... | collective-permute-start | bytes 1179656 | tf_op jit(solution)/shard_map/ppermute | solution.py:307
  8.0 1.9 %copy-start = (bf16[2,2048,384]{2,1,0:T(8,128)(2,1)S(1)}, bf16[2,2048,384]{2,1,0:T(8,128)(2,1)}, u32[]{:S(2)}) copy-start(bf16[2,2048,384]{2,1,0:T(8,128)(2,1)} %now_ref.3) | copy-start | bytes 9437188
  9.9 0.8 copy-start.4
  10.7 3.1 %copy-start.6 = (s32[12]{0:T(128)S(1)}, s32[12]{0:T(128)}, u32[]{:S(2)}) copy-start(s32[12]{0:T(128)} %stack.90.key_ref) | copy-start | bytes 148
  10.7 6.7 %copy-start.1 = (bf16[2,2048,384]{2,1,0:T(8,128)(2,1)S(1)}, bf16[2,2048,384]{2,1,0:T(8,128)(2,1)}, u32[]{:S(2)}) copy-start(bf16[2,2048,384]{2,1,0:T(8,128)(2,1)} %now_ref.3) | copy-start | bytes 9437188
  15.3 1.1 copy-start.2
  16.5 31.2 %collective-permute-start.13 = (bf16[4,4,2,32,384]{4,3,2,1,0:T(8,128)(2,1)}, bf16[4,4,2,32,384]{4,3,2,1,0:T(8,128)(2,1)}, u32[]{:S(2)}, u32[]{:S(2)}) collective-permute-start(bf16[4,4,2,32,384]{4,3,2,1,0:T(8,128)(2,1)} %shard_map.59), channel_id=1, source_target_pairs={{0,1},{1,0},{2,3},{3,2},{4,5},{5,4},{6,7},{7,6},{8,9},{9,8},{10,11... | collective-permute-start | bytes 2359304 | tf_op jit(solution)/shard_map/ppermute | solution.py:327
  17.4 0.8 copy-start.5
  21.3 24.0 %copy-start.7 = (s32[12]{0:T(128)S(1)}, s32[12]{0:T(128)}, u32[]{:S(2)}) copy-start(s32[12]{0:T(128)} %stack.90.key_ref) | copy-start | bytes 148
  21.4 26.3 %copy-start.3 = (bf16[32,2,32,384]{3,2,1,0:T(8,128)(2,1)S(1)}, bf16[32,2,32,384]{3,2,1,0:T(8,128)(2,1)}, u32[]{:S(2)}) copy-start(bf16[32,2,32,384]{3,2,1,0:T(8,128)(2,1)} %copy-done.2) | copy-start | bytes 4718596
  21.6 19.5 %collective-permute-start.3 = (bf16[8,2,32,384]{3,2,1,0:T(8,128)(2,1)S(1)}, bf16[8,2,32,384]{3,2,1,0:T(8,128)(2,1)S(1)}, u32[]{:S(2)}, u32[]{:S(2)}) collective-permute-start(bf16[8,2,32,384]{3,2,1,0:T(8,128)(2,1)S(1)} %get-tuple-element.29), channel_id=1, source_target_pairs={{0,6},{2,0},{4,2},{6,4},{8,14},{10,8},{12,10},{14,12},{16,22},{18,... | collective-permute-start | bytes 1179656 | tf_op jit(solution)/shard_map/ppermute | solution.py:356
  24.4 16.8 %collective-permute-start.2 = (bf16[8,2,32,384]{3,2,1,0:T(8,128)(2,1)S(1)}, bf16[8,2,32,384]{3,2,1,0:T(8,128)(2,1)S(1)}, u32[]{:S(2)}, u32[]{:S(2)}) collective-permute-start(bf16[8,2,32,384]{3,2,1,0:T(8,128)(2,1)S(1)} %get-tuple-element.30), channel_id=1, source_target_pairs={{0,4},{2,6},{4,0},{6,2},{8,12},{10,14},{12,8},{14,10},{16,20},{18,... | collective-permute-start | bytes 1179656 | tf_op jit(solution)/shard_map/ppermute | solution.py:356
  24.7 20.6 %collective-permute-start.1 = (bf16[8,2,32,384]{3,2,1,0:T(8,128)(2,1)S(1)}, bf16[8,2,32,384]{3,2,1,0:T(8,128)(2,1)S(1)}, u32[]{:S(2)}, u32[]{:S(2)}) collective-permute-start(bf16[8,2,32,384]{3,2,1,0:T(8,128)(2,1)S(1)} %get-tuple-element.31), channel_id=1, source_target_pairs={{0,2},{2,4},{4,6},{6,0},{8,10},{10,12},{12,14},{14,8},{16,18},{18,... | collective-permute-start | bytes 1179656 | tf_op jit(solution)/shard_map/ppermute | solution.py:356
  47.1 115.2 %copy-start.8 = (s32[2,68,2]{1,2,0:T(2,128)S(1)}, s32[2,68,2]{1,2,0:T(2,128)}, u32[]{:S(2)}) copy-start(s32[2,68,2]{1,2,0:T(2,128)} %param.8) | copy-start | bytes 3268
  47.1 115.1 %copy-start.9 = (s32[4,2]{0,1:T(2,128)S(1)}, s32[4,2]{0,1:T(2,128)}, u32[]{:S(2)}) copy-start(s32[4,2]{0,1:T(2,128)} %param.7) | copy-start | bytes 100
  47.1 59.4 %collective-permute-start.4 = (bf16[4,4,2,32,384]{4,3,2,1,0:T(8,128)(2,1)S(1)}, bf16[4,4,2,32,384]{4,3,2,1,0:T(8,128)(2,1)S(1)}, u32[]{:S(2)}, u32[]{:S(2)}) collective-permute-start(bf16[4,4,2,32,384]{4,3,2,1,0:T(8,128)(2,1)S(1)} %shard_map.56), channel_id=1, source_target_pairs={{0,1},{1,0},{2,3},{3,2},{4,5},{5,4},{6,7},{7,6},{8,9},{9,8},{10,11... | collective-permute-start | bytes 2359304 | tf_op jit(solution)/shard_map/ppermute | solution.py:327
  50.5 19.7 %collective-permute-start.14 = (bf16[2,4,2,32,384]{4,3,2,1,0:T(8,128)(2,1)S(1)}, bf16[2,4,2,32,384]{4,3,2,1,0:T(8,128)(2,1)S(1)}, u32[]{:S(2)}, u32[]{:S(2)}) collective-permute-start(bf16[2,4,2,32,384]{4,3,2,1,0:T(8,128)(2,1)S(1)} %get-tuple-element.21), channel_id=1, source_target_pairs={{0,0},{1,9},{2,2},{3,11},{4,4},{5,13},{6,6},{7,15},{8,8},{9,1},{10... | collective-permute-start | bytes 1179656 | tf_op jit(solution)/shard_map/ppermute | solution.py:350
  54.1 40.0 %collective-permute-start.15 = (bf16[2,4,2,32,384]{4,3,2,1,0:T(8,128)(2,1)S(1)}, bf16[2,4,2,32,384]{4,3,2,1,0:T(8,128)(2,1)S(1)}, u32[]{:S(2)}, u32[]{:S(2)}) collective-permute-start(bf16[2,4,2,32,384]{4,3,2,1,0:T(8,128)(2,1)S(1)} %get-tuple-element.22), channel_id=1, source_target_pairs={{0,16},{1,25},{2,18},{3,27},{4,20},{5,29},{6,22},{7,31},{8,24},{9,... | collective-permute-start | bytes 1179656 | tf_op jit(solution)/shard_map/ppermute | solution.py:350
  59.6 38.3 %collective-permute-start.16 = (bf16[2,4,2,32,384]{4,3,2,1,0:T(8,128)(2,1)S(1)}, bf16[2,4,2,32,384]{4,3,2,1,0:T(8,128)(2,1)S(1)}, u32[]{:S(2)}, u32[]{:S(2)}) collective-permute-start(bf16[2,4,2,32,384]{4,3,2,1,0:T(8,128)(2,1)S(1)} %get-tuple-element.23), channel_id=1, source_target_pairs={{0,32},{1,41},{2,34},{3,43},{4,36},{5,45},{6,38},{7,47},{8,40},{9,... | collective-permute-start | bytes 1179656 | tf_op jit(solution)/shard_map/ppermute | solution.py:350
  68.2 32.6 %collective-permute-start.17 = (bf16[2,4,2,32,384]{4,3,2,1,0:T(8,128)(2,1)S(1)}, bf16[2,4,2,32,384]{4,3,2,1,0:T(8,128)(2,1)S(1)}, u32[]{:S(2)}, u32[]{:S(2)}) collective-permute-start(bf16[2,4,2,32,384]{4,3,2,1,0:T(8,128)(2,1)S(1)} %get-tuple-element.24), channel_id=1, source_target_pairs={{0,48},{1,57},{2,50},{3,59},{4,52},{5,61},{6,54},{7,63},{8,56},{9,... | collective-permute-start | bytes 1179656 | tf_op jit(solution)/shard_map/ppermute | solution.py:350
  103.7 18.0 %collective-permute-start.18 = (bf16[8,2,32,384]{3,2,1,0:T(8,128)(2,1)S(1)}, bf16[8,2,32,384]{3,2,1,0:T(8,128)(2,1)S(1)}, u32[]{:S(2)}, u32[]{:S(2)}) collective-permute-start(bf16[8,2,32,384]{3,2,1,0:T(8,128)(2,1)S(1)} %get-tuple-element.26), channel_id=1, source_target_pairs={{0,2},{2,4},{4,6},{6,0},{8,10},{10,12},{12,14},{14,8},{16,18},{18,... | collective-permute-start | bytes 1179656 | tf_op jit(solution)/shard_map/ppermute | solution.py:356
  103.8 19.8 %collective-permute-start.19 = (bf16[8,2,32,384]{3,2,1,0:T(8,128)(2,1)S(1)}, bf16[8,2,32,384]{3,2,1,0:T(8,128)(2,1)S(1)}, u32[]{:S(2)}, u32[]{:S(2)}) collective-permute-start(bf16[8,2,32,384]{3,2,1,0:T(8,128)(2,1)S(1)} %get-tuple-element.27), channel_id=1, source_target_pairs={{0,4},{2,6},{4,0},{6,2},{8,12},{10,14},{12,8},{14,10},{16,20},{18,... | collective-permute-start | bytes 1179656 | tf_op jit(solution)/shard_map/ppermute | solution.py:356
  105.3 22.0 %collective-permute-start.20 = (bf16[8,2,32,384]{3,2,1,0:T(8,128)(2,1)S(1)}, bf16[8,2,32,384]{3,2,1,0:T(8,128)(2,1)S(1)}, u32[]{:S(2)}, u32[]{:S(2)}) collective-permute-start(bf16[8,2,32,384]{3,2,1,0:T(8,128)(2,1)S(1)} %get-tuple-element.28), channel_id=1, source_target_pairs={{0,6},{2,0},{4,2},{6,4},{8,14},{10,8},{12,10},{14,12},{16,22},{18,... | collective-permute-start | bytes 1179656 | tf_op jit(solution)/shard_map/ppermute | solution.py:356
  106.5 23.9 %collective-permute-start.21 = (bf16[8,2,32,384]{3,2,1,0:T(8,128)(2,1)S(1)}, bf16[8,2,32,384]{3,2,1,0:T(8,128)(2,1)S(1)}, u32[]{:S(2)}, u32[]{:S(2)}) collective-permute-start(bf16[8,2,32,384]{3,2,1,0:T(8,128)(2,1)S(1)} %get-tuple-element.25.refs_0_), channel_id=1, source_target_pairs={{0,1},{1,0},{2,3},{3,2},{4,5},{5,4},{6,7},{7,6},{8,9},{9,8},{10,11... | collective-permute-start | bytes 1179656 | tf_op jit(solution)/shard_map/ppermute | solution.py:327
  109.3 22.9 %collective-permute-start.5 = (bf16[2,4,2,32,384]{4,3,2,1,0:T(8,128)(2,1)S(1)}, bf16[2,4,2,32,384]{4,3,2,1,0:T(8,128)(2,1)S(1)}, u32[]{:S(2)}, u32[]{:S(2)}) collective-permute-start(bf16[2,4,2,32,384]{4,3,2,1,0:T(8,128)(2,1)S(1)} %get-tuple-element.17), channel_id=1, source_target_pairs={{0,0},{1,9},{2,2},{3,11},{4,4},{5,13},{6,6},{7,15},{8,8},{9,1},{10... | collective-permute-start | bytes 1179656 | tf_op jit(solution)/shard_map/ppermute | solution.py:350
  121.7 34.8 %collective-permute-start.6 = (bf16[2,4,2,32,384]{4,3,2,1,0:T(8,128)(2,1)S(1)}, bf16[2,4,2,32,384]{4,3,2,1,0:T(8,128)(2,1)}, u32[]{:S(2)}, u32[]{:S(2)}) collective-permute-start(bf16[2,4,2,32,384]{4,3,2,1,0:T(8,128)(2,1)S(1)} %get-tuple-element.18), channel_id=1, source_target_pairs={{0,16},{1,25},{2,18},{3,27},{4,20},{5,29},{6,22},{7,31},{8,24},{9,... | collective-permute-start | bytes 1179656 | tf_op jit(solution)/shard_map/ppermute | solution.py:350
  123.7 32.9 %collective-permute-start.7 = (bf16[2,4,2,32,384]{4,3,2,1,0:T(8,128)(2,1)S(1)}, bf16[2,4,2,32,384]{4,3,2,1,0:T(8,128)(2,1)}, u32[]{:S(2)}, u32[]{:S(2)}) collective-permute-start(bf16[2,4,2,32,384]{4,3,2,1,0:T(8,128)(2,1)S(1)} %get-tuple-element.19), channel_id=1, source_target_pairs={{0,32},{1,41},{2,34},{3,43},{4,36},{5,45},{6,38},{7,47},{8,40},{9,... | collective-permute-start | bytes 1179656 | tf_op jit(solution)/shard_map/ppermute | solution.py:350
  127.3 34.2 %collective-permute-start.8 = (bf16[2,4,2,32,384]{4,3,2,1,0:T(8,128)(2,1)S(1)}, bf16[2,4,2,32,384]{4,3,2,1,0:T(8,128)(2,1)}, u32[]{:S(2)}, u32[]{:S(2)}) collective-permute-start(bf16[2,4,2,32,384]{4,3,2,1,0:T(8,128)(2,1)S(1)} %get-tuple-element.20), channel_id=1, source_target_pairs={{0,48},{1,57},{2,50},{3,59},{4,52},{5,61},{6,54},{7,63},{8,56},{9,... | collective-permute-start | bytes 1179656 | tf_op jit(solution)/shard_map/ppermute | solution.py:350
  130.4 31.2 %collective-permute-start.22 = (bf16[8,2,32,384]{3,2,1,0:T(8,128)(2,1)S(1)}, bf16[8,2,32,384]{3,2,1,0:T(8,128)(2,1)S(1)}, u32[]{:S(2)}, u32[]{:S(2)}) collective-permute-start(bf16[8,2,32,384]{3,2,1,0:T(8,128)(2,1)S(1)} %collective-permute-done.18.refs_1_), channel_id=1, source_target_pairs={{0,1},{1,0},{2,3},{3,2},{4,5},{5,4},{6,7},{7,6},{8,9},{9,8},{10,11... | collective-permute-start | bytes 1179656 | tf_op jit(solution)/shard_map/ppermute | solution.py:327
  132.2 29.9 %collective-permute-start.23 = (bf16[8,2,32,384]{3,2,1,0:T(8,128)(2,1)S(1)}, bf16[8,2,32,384]{3,2,1,0:T(8,128)(2,1)S(1)}, u32[]{:S(2)}, u32[]{:S(2)}) collective-permute-start(bf16[8,2,32,384]{3,2,1,0:T(8,128)(2,1)S(1)} %collective-permute-done.19.refs_2_), channel_id=1, source_target_pairs={{0,1},{1,0},{2,3},{3,2},{4,5},{5,4},{6,7},{7,6},{8,9},{9,8},{10,11... | collective-permute-start | bytes 1179656 | tf_op jit(solution)/shard_map/ppermute | solution.py:327
  156.6 5.7 %collective-permute-start.24 = (bf16[8,2,32,384]{3,2,1,0:T(8,128)(2,1)S(1)}, bf16[8,2,32,384]{3,2,1,0:T(8,128)(2,1)S(1)}, u32[]{:S(2)}, u32[]{:S(2)}) collective-permute-start(bf16[8,2,32,384]{3,2,1,0:T(8,128)(2,1)S(1)} %collective-permute-done.20.refs_3_), channel_id=1, source_target_pairs={{0,1},{1,0},{2,3},{3,2},{4,5},{5,4},{6,7},{7,6},{8,9},{9,8},{10,11... | collective-permute-start | bytes 1179656 | tf_op jit(solution)/shard_map/ppermute | solution.py:327
  156.6 16.6 %collective-permute-start.9 = (bf16[2,4,2,32,384]{4,3,2,1,0:T(8,128)(2,1)S(1)}, bf16[2,4,2,32,384]{4,3,2,1,0:T(8,128)(2,1)}, u32[]{:S(2)}, u32[]{:S(2)}) collective-permute-start(bf16[2,4,2,32,384]{4,3,2,1,0:T(8,128)(2,1)S(1)} %collective-permute-done.5.refs_0_), channel_id=1, source_target_pairs={{0,1},{1,0},{2,3},{3,2},{4,5},{5,4},{6,7},{7,6},{8,9},{9,8},{10,11... | collective-permute-start | bytes 1179656 | tf_op jit(solution)/shard_map/ppermute | solution.py:327
  161.5 11.6 %collective-permute-start.10 = (bf16[2,4,2,32,384]{4,3,2,1,0:T(8,128)(2,1)}, bf16[2,4,2,32,384]{4,3,2,1,0:T(8,128)(2,1)}, u32[]{:S(2)}, u32[]{:S(2)}) collective-permute-start(bf16[2,4,2,32,384]{4,3,2,1,0:T(8,128)(2,1)} %collective-permute-done.6.refs_1_), channel_id=1, source_target_pairs={{0,1},{1,0},{2,3},{3,2},{4,5},{5,4},{6,7},{7,6},{8,9},{9,8},{10,11... | collective-permute-start | bytes 1179656 | tf_op jit(solution)/shard_map/ppermute | solution.py:327
  161.5 11.6 %collective-permute-start.11 = (bf16[2,4,2,32,384]{4,3,2,1,0:T(8,128)(2,1)}, bf16[2,4,2,32,384]{4,3,2,1,0:T(8,128)(2,1)}, u32[]{:S(2)}, u32[]{:S(2)}) collective-permute-start(bf16[2,4,2,32,384]{4,3,2,1,0:T(8,128)(2,1)} %collective-permute-done.7.refs_2_), channel_id=1, source_target_pairs={{0,1},{1,0},{2,3},{3,2},{4,5},{5,4},{6,7},{7,6},{8,9},{9,8},{10,11... | collective-permute-start | bytes 1179656 | tf_op jit(solution)/shard_map/ppermute | solution.py:327
  162.0 11.1 %collective-permute-start.12 = (bf16[2,4,2,32,384]{4,3,2,1,0:T(8,128)(2,1)}, bf16[2,4,2,32,384]{4,3,2,1,0:T(8,128)(2,1)}, u32[]{:S(2)}, u32[]{:S(2)}) collective-permute-start(bf16[2,4,2,32,384]{4,3,2,1,0:T(8,128)(2,1)} %collective-permute-done.8.refs_3_), channel_id=1, source_target_pairs={{0,1},{1,0},{2,3},{3,2},{4,5},{5,4},{6,7},{7,6},{8,9},{9,8},{10,11... | collective-permute-start | bytes 1179656 | tf_op jit(solution)/shard_map/ppermute | solution.py:327

commit v3 on v2

--- a/solution.py
+++ b/solution.py
@@ -114,7 +114,7 @@
                 pltpu.VMEM((NCHAN * GROUP, 2 * GROUP * NCHAN), jnp.bfloat16),
             ],
         ),
-        compiler_params=pltpu.CompilerParams(vmem_limit_bytes=16 << 20),
+        compiler_params=pltpu.CompilerParams(vmem_limit_bytes=(16 if halo is not None else 60) << 20),
         cost_estimate=pl.CostEstimate(
             flops=strips * 2 * 2 * 2 * 2 * 256 * 512 * HALF,
             bytes_accessed=strips * 4 * rows * HALF * 2,
@@ -124,7 +124,7 @@
 
 
 def correlate_body(chunk, tiles, sections, place_ref, *refs):
-    out_ref, raw, lanes, turned, held, in_sems, add_sems, out_sems = refs[-8:]
+    out_ref, raw, lanes, held, in_sems, add_sems, out_sems = refs[-7:]
     blocks = HALF // PANEL
     frames = lanes.shape[1]
     turn, group = place_ref[0], place_ref[1]
@@ -202,7 +202,6 @@
 
         def put(part, value):
             lanes[panel, :, part * PANEL : (part + 1) * PANEL] = value
-            turned[panel, part * PANEL : (part + 1) * PANEL, :] = value.T
 
         @pl.when(s_low == s_high)
         def _():
@@ -225,9 +224,11 @@
             earlier(index).wait()
         for slot in range(PER_STEP):
             at = index * PER_STEP + slot
-            left = turned[tiles[group, 0, at]]
+            left = lanes[tiles[group, 0, at]]
             right = lanes[tiles[group, 1, at]]
-            gram = jnp.dot(left, right, preferred_element_type=jnp.float32)
+            gram = lax.dot_general(
+                left, right, (((0,), (0,)), ((), ())), preferred_element_type=jnp.float32
+            )
             real = (gram[:PANEL, :PANEL] + gram[PANEL:, PANEL:]) * scale
             imag = (gram[PANEL:, :PANEL] - gram[:PANEL, PANEL:]) * scale
             held[at, 0] = real + held[at, 0] if chunk == 1 else real
@@ -254,7 +255,6 @@
             scratch_shapes=[
                 pltpu.VMEM((2, TIMES) + pieces[0].shape, jnp.bfloat16),
                 pltpu.VMEM((PANELS, frames, 2 * PANEL), jnp.bfloat16),
-                pltpu.VMEM((PANELS, 2 * PANEL, frames), jnp.bfloat16),
                 pltpu.VMEM((TSLOT, 2, PANEL, PANEL), jnp.float32),
                 pltpu.SemaphoreType.DMA((2 * TIMES,)),
                 pltpu.SemaphoreType.DMA((TSLOT // PER_STEP,)),

time: 186 us -> 184 us (0.989)
    unnamed x20 -> x18, local copies, waits for them, and re-layouts: 4.74 us -> 2.27 us
    pallas_call x2, Pallas kernels: 6.15 us -> 8.05 us  [filter_call(): pl.pallas_call(functools.partial(filter_body, slot_of, halo is not None),...]
    pallas_call x2, Pallas kernels: 22.1 us -> 20.3 us  [correlate_call(): pl.pallas_call(functools.partial(correlate_body, chunk), out_shape=jax.Sh...]
  transfers between devices with their start and end apart: 25 -> 25, of which waited for: 8 -> 8; matrix products, arithmetic and copies ran while one was open for 1% -> 2% of each run, Pallas kernels for 16% -> 16%
where the time goes in v3:
time: 184 us; the launch traced here: 183 us
  waiting for transfers between devices  89.9 us (49%)
  starting transfers between devices  45.3 us (25%)
  Pallas kernels  40.1 us (22%)
  local copies, waits for them, and re-layouts  6.82 us (4%)
    ppermute x8, waiting for transfers between devices, far(): moved.append(lax.ppermute(payload[turn], everyone, across(turn)))  59.2 us
    ppermute x6, waiting for transfers between devices, near(): moved[step] = lax.ppermute(payload[step], 'chan', along(step))  30.7 us
    ppermute x8, starting transfers between devices, far(): moved.append(lax.ppermute(payload[turn], everyone, across(turn)))  30.2 us
    pallas_call x2, Pallas kernels, correlate_call(): pl.pallas_call(functools.partial(correlate_body, chunk), out_shape=jax.Sh...  20.3 us
    pallas_call x5, Pallas kernels, move_blocks(): pl.pallas_call(body, out_shape=[jax.ShapeDtypeStruct(shape, jnp.bfloat16)...  11.7 us
    pallas_call x2, Pallas kernels, filter_call(): pl.pallas_call(functools.partial(filter_body, slot_of, halo is not None),...  8.05 us
    ppermute x6, starting transfers between devices, near(): moved[step] = lax.ppermute(payload[step], 'chan', along(step))  6.29 us
    ppermute x10, starting transfers between devices, swap(): return lax.ppermute(piece, 'grp', [(0, 1), (1, 0)])  4.81 us
  transfers between devices with their start and end apart: 25, of which 8 were waited for; matrix products, arithmetic and copies ran while one was open for 2% of the time, Pallas kernels for 16%

profile of v3, /device:TPU:1, one launch (start us, length us, event | category | flops | bytes accessed | tf_op | source)
XLA Modules:
  0.0 182.8 jit_solution(3875623541707456590)
XLA Ops:
  0.0 1.8 slice.3
  1.8 4.0 %collective-permute-start = (bf16[2,256,384]{2,1,0:T(8,128)(2,1)}, bf16[2,256,384]{2,1,0:T(8,128)(2,1)S(1)}, u32[]{:S(2)}, u32[]{:S(2)}) collective-permute-start(bf16[2,256,384]{2,1,0:T(8,128)(2,1)} %slice.3), channel_id=1, source_target_pairs={{0,2},{2,4},{4,6},{6,8},{8,10},{10,12},{12,14},{14,16},{16,18},{18... | collective-permute-start | bytes 1179656 | tf_op jit(solution)/shard_map/ppermute | solution.py:307
  6.0 0.7 rev.3
  6.7 0.1 stack.98
  6.8 0.1 stack.97
  7.4 0.6 stack.99.tap_ref
  8.0 0.6 stack.90.key_ref
  8.6 5.0 %shard_map.58 = bf16[32,2,32,384]{3,2,1,0:T(8,128)(2,1)} custom-call(f32[32,512]{1,0:T(8,128)} %constant.141.clone.trig_ref, f32[8,512]{1,0:T(8,128)} %stack.99.tap_ref, bf16[2,2048,384]{2,1,0:T(8,128)(2,1)} %now_ref.3, bf16[2,2048,384]{2,1,0:T(8,128)(2,1)} %now_ref.3), custom_call_target="tpu_custom_call" | custom-call | flops 1610612736 | bytes 3145728 | tf_op jit(solution)/shard_map/pallas_call | solution.py:104
  13.6 1.4 copy-done.1
  15.0 1.5 shard_map.59
  16.5 1.0 collective-permute-start.13
  17.5 0.8 copy-done.3
  18.4 3.1 %shard_map.55 = bf16[32,2,32,384]{3,2,1,0:T(8,128)(2,1)S(1)} custom-call(f32[32,512]{1,0:T(8,128)S(1)} %copy-done.3, f32[8,512]{1,0:T(8,128)S(1)} %copy-done.4, bf16[2,2048,384]{2,1,0:T(8,128)(2,1)S(1)} %copy-done, bf16[2,2048,384]{2,1,0:T(8,128)(2,1)S(1)} %copy-done, bf16[2,256,384]{2,1,0:T(8,128)(2,1)S(1)} %collective-permute-done.rest_0_), custom_call_target="tpu_custom_call" | custom-call | flops 1610612736 | bytes 3145728 | tf_op jit(solution)/shard_map/pallas_call | solution.py:104
  21.5 0.2 dynamic-slice_bitcast_fusion
  21.7 2.8 %collective-permute-start.3 = (bf16[8,2,32,384]{3,2,1,0:T(8,128)(2,1)S(1)}, bf16[8,2,32,384]{3,2,1,0:T(8,128)(2,1)S(1)}, u32[]{:S(2)}, u32[]{:S(2)}) collective-permute-start(bf16[8,2,32,384]{3,2,1,0:T(8,128)(2,1)S(1)} %get-tuple-element.29), channel_id=1, source_target_pairs={{0,6},{2,0},{4,2},{6,4},{8,14},{10,8},{12,10},{14,12},{16,22},{18,... | collective-permute-start | bytes 1179656 | tf_op jit(solution)/shard_map/ppermute | solution.py:356
  24.5 0.3 collective-permute-start.2
  24.8 0.4 collective-permute-start.1
  25.2 15.9 %collective-permute-done.3.refs_3_ = bf16[8,2,32,384]{3,2,1,0:T(8,128)(2,1)S(1)} collective-permute-done((bf16[8,2,32,384]{3,2,1,0:T(8,128)(2,1)S(1)}, bf16[8,2,32,384]{3,2,1,0:T(8,128)(2,1)S(1)}, u32[]{:S(2)}, u32[]{:S(2)}) %collective-permute-start.3) | collective-permute-done | bytes 393248 | tf_op jit(solution)/shard_map/ppermute | solution.py:356
  41.2 4.3 %collective-permute-done.1.refs_1_ = bf16[8,2,32,384]{3,2,1,0:T(8,128)(2,1)S(1)} collective-permute-done((bf16[8,2,32,384]{3,2,1,0:T(8,128)(2,1)S(1)}, bf16[8,2,32,384]{3,2,1,0:T(8,128)(2,1)S(1)}, u32[]{:S(2)}, u32[]{:S(2)}) %collective-permute-start.1) | collective-permute-done | bytes 393248 | tf_op jit(solution)/shard_map/ppermute | solution.py:356
  45.4 1.7 shard_map.56
  47.2 0.6 collective-permute-start.4
  47.8 2.8 %shard_map.60 = (bf16[2,4,2,32,384]{4,3,2,1,0:T(8,128)(2,1)S(1)}, bf16[2,4,2,32,384]{4,3,2,1,0:T(8,128)(2,1)S(1)}, bf16[2,4,2,32,384]{4,3,2,1,0:T(8,128)(2,1)S(1)}, bf16[2,4,2,32,384]{4,3,2,1,0:T(8,128)(2,1)S(1)}) custom-call(s32[12]{0:T(128)S(1)} %copy-done.6, bf16[8,4,2,32,384]{4,3,2,1,0:T(8,128)(2,1)S(1)} %bitcast.27, ...), custom_call_target="tpu_custom_call" | custom-call | tf_op jit(solution)/shard_map/pallas_call | solution.py:291
  50.6 3.5 %collective-permute-start.14 = (bf16[2,4,2,32,384]{4,3,2,1,0:T(8,128)(2,1)S(1)}, bf16[2,4,2,32,384]{4,3,2,1,0:T(8,128)(2,1)S(1)}, u32[]{:S(2)}, u32[]{:S(2)}) collective-permute-start(bf16[2,4,2,32,384]{4,3,2,1,0:T(8,128)(2,1)S(1)} %get-tuple-element.21), channel_id=1, source_target_pairs={{0,0},{1,9},{2,2},{3,11},{4,4},{5,13},{6,6},{7,15},{8,8},{9,1},{10... | collective-permute-start | bytes 1179656 | tf_op jit(solution)/shard_map/ppermute | solution.py:350
  54.2 5.5 %collective-permute-start.15 = (bf16[2,4,2,32,384]{4,3,2,1,0:T(8,128)(2,1)S(1)}, bf16[2,4,2,32,384]{4,3,2,1,0:T(8,128)(2,1)S(1)}, u32[]{:S(2)}, u32[]{:S(2)}) collective-permute-start(bf16[2,4,2,32,384]{4,3,2,1,0:T(8,128)(2,1)S(1)} %get-tuple-element.22), channel_id=1, source_target_pairs={{0,16},{1,25},{2,18},{3,27},{4,20},{5,29},{6,22},{7,31},{8,24},{9,... | collective-permute-start | bytes 1179656 | tf_op jit(solution)/shard_map/ppermute | solution.py:350
  59.7 8.6 %collective-permute-start.16 = (bf16[2,4,2,32,384]{4,3,2,1,0:T(8,128)(2,1)S(1)}, bf16[2,4,2,32,384]{4,3,2,1,0:T(8,128)(2,1)S(1)}, u32[]{:S(2)}, u32[]{:S(2)}) collective-permute-start(bf16[2,4,2,32,384]{4,3,2,1,0:T(8,128)(2,1)S(1)} %get-tuple-element.23), channel_id=1, source_target_pairs={{0,32},{1,41},{2,34},{3,43},{4,36},{5,45},{6,38},{7,47},{8,40},{9,... | collective-permute-start | bytes 1179656 | tf_op jit(solution)/shard_map/ppermute | solution.py:350
  68.3 2.0 %collective-permute-start.17 = (bf16[2,4,2,32,384]{4,3,2,1,0:T(8,128)(2,1)S(1)}, bf16[2,4,2,32,384]{4,3,2,1,0:T(8,128)(2,1)S(1)}, u32[]{:S(2)}, u32[]{:S(2)}) collective-permute-start(bf16[2,4,2,32,384]{4,3,2,1,0:T(8,128)(2,1)S(1)} %get-tuple-element.24), channel_id=1, source_target_pairs={{0,48},{1,57},{2,50},{3,59},{4,52},{5,61},{6,54},{7,63},{8,56},{9,... | collective-permute-start | bytes 1179656 | tf_op jit(solution)/shard_map/ppermute | solution.py:350
  70.3 23.9 %collective-permute-done.15.refs_1_ = bf16[2,4,2,32,384]{4,3,2,1,0:T(8,128)(2,1)S(1)} collective-permute-done((bf16[2,4,2,32,384]{4,3,2,1,0:T(8,128)(2,1)S(1)}, bf16[2,4,2,32,384]{4,3,2,1,0:T(8,128)(2,1)S(1)}, u32[]{:S(2)}, u32[]{:S(2)}) %collective-permute-start.15) | collective-permute-done | bytes 393248 | tf_op jit(solution)/shard_map/ppermute | solution.py:350
  94.2 3.8 %collective-permute-done.16.refs_2_ = bf16[2,4,2,32,384]{4,3,2,1,0:T(8,128)(2,1)S(1)} collective-permute-done((bf16[2,4,2,32,384]{4,3,2,1,0:T(8,128)(2,1)S(1)}, bf16[2,4,2,32,384]{4,3,2,1,0:T(8,128)(2,1)S(1)}, u32[]{:S(2)}, u32[]{:S(2)}) %collective-permute-start.16) | collective-permute-done | bytes 393248 | tf_op jit(solution)/shard_map/ppermute | solution.py:350
  98.0 2.9 %collective-permute-done.17.refs_3_ = bf16[2,4,2,32,384]{4,3,2,1,0:T(8,128)(2,1)S(1)} collective-permute-done((bf16[2,4,2,32,384]{4,3,2,1,0:T(8,128)(2,1)S(1)}, bf16[2,4,2,32,384]{4,3,2,1,0:T(8,128)(2,1)S(1)}, u32[]{:S(2)}, u32[]{:S(2)}) %collective-permute-start.17) | collective-permute-done | bytes 393248 | tf_op jit(solution)/shard_map/ppermute | solution.py:350
  100.9 2.9 %shard_map.61 = (bf16[8,2,32,384]{3,2,1,0:T(8,128)(2,1)S(1)}, bf16[8,2,32,384]{3,2,1,0:T(8,128)(2,1)S(1)}, bf16[8,2,32,384]{3,2,1,0:T(8,128)(2,1)S(1)}, bf16[8,2,32,384]{3,2,1,0:T(8,128)(2,1)S(1)}) custom-call(s32[12]{0:T(128)S(1)} %copy-done.6, bf16[2,4,2,32,384]{4,3,2,1,0:T(8,128)(2,1)S(1)} %collective-permute-done.14.refs_0_, ...), custom_call_target="tpu_custom_call" | custom-call | tf_op jit(solution)/shard_map/pallas_call | solution.py:291
  103.8 0.1 collective-permute-start.18
  103.9 1.5 collective-permute-start.19
  105.4 1.2 collective-permute-start.20
  106.6 2.8 %shard_map.57 = (bf16[2,4,2,32,384]{4,3,2,1,0:T(8,128)(2,1)S(1)}, bf16[2,4,2,32,384]{4,3,2,1,0:T(8,128)(2,1)S(1)}, bf16[2,4,2,32,384]{4,3,2,1,0:T(8,128)(2,1)S(1)}, bf16[2,4,2,32,384]{4,3,2,1,0:T(8,128)(2,1)S(1)}) custom-call(s32[12]{0:T(128)S(1)} %copy-done.6, bf16[8,2,32,384]{3,2,1,0:T(8,128)(2,1)S(1)} %get-tuple-element.32.refs_0_, ...), custom_call_target="tpu_custom_call" | custom-call | tf_op jit(solution)/shard_map/pallas_call | solution.py:291
  109.4 1.9 %collective-permute-start.5 = (bf16[2,4,2,32,384]{4,3,2,1,0:T(8,128)(2,1)S(1)}, bf16[2,4,2,32,384]{4,3,2,1,0:T(8,128)(2,1)S(1)}, u32[]{:S(2)}, u32[]{:S(2)}) collective-permute-start(bf16[2,4,2,32,384]{4,3,2,1,0:T(8,128)(2,1)S(1)} %get-tuple-element.17), channel_id=1, source_target_pairs={{0,0},{1,9},{2,2},{3,11},{4,4},{5,13},{6,6},{7,15},{8,8},{9,1},{10... | collective-permute-start | bytes 1179656 | tf_op jit(solution)/shard_map/ppermute | solution.py:350
  111.3 10.5 %collective-permute-done.18.refs_1_ = bf16[8,2,32,384]{3,2,1,0:T(8,128)(2,1)S(1)} collective-permute-done((bf16[8,2,32,384]{3,2,1,0:T(8,128)(2,1)S(1)}, bf16[8,2,32,384]{3,2,1,0:T(8,128)(2,1)S(1)}, u32[]{:S(2)}, u32[]{:S(2)}) %collective-permute-start.18) | collective-permute-done | bytes 393248 | tf_op jit(solution)/shard_map/ppermute | solution.py:356
  121.8 1.9 %collective-permute-start.6 = (bf16[2,4,2,32,384]{4,3,2,1,0:T(8,128)(2,1)S(1)}, bf16[2,4,2,32,384]{4,3,2,1,0:T(8,128)(2,1)}, u32[]{:S(2)}, u32[]{:S(2)}) collective-permute-start(bf16[2,4,2,32,384]{4,3,2,1,0:T(8,128)(2,1)S(1)} %get-tuple-element.18), channel_id=1, source_target_pairs={{0,16},{1,25},{2,18},{3,27},{4,20},{5,29},{6,22},{7,31},{8,24},{9,... | collective-permute-start | bytes 1179656 | tf_op jit(solution)/shard_map/ppermute | solution.py:350
  123.8 3.7 %collective-permute-start.7 = (bf16[2,4,2,32,384]{4,3,2,1,0:T(8,128)(2,1)S(1)}, bf16[2,4,2,32,384]{4,3,2,1,0:T(8,128)(2,1)}, u32[]{:S(2)}, u32[]{:S(2)}) collective-permute-start(bf16[2,4,2,32,384]{4,3,2,1,0:T(8,128)(2,1)S(1)} %get-tuple-element.19), channel_id=1, source_target_pairs={{0,32},{1,41},{2,34},{3,43},{4,36},{5,45},{6,38},{7,47},{8,40},{9,... | collective-permute-start | bytes 1179656 | tf_op jit(solution)/shard_map/ppermute | solution.py:350
  127.5 3.0 %collective-permute-start.8 = (bf16[2,4,2,32,384]{4,3,2,1,0:T(8,128)(2,1)S(1)}, bf16[2,4,2,32,384]{4,3,2,1,0:T(8,128)(2,1)}, u32[]{:S(2)}, u32[]{:S(2)}) collective-permute-start(bf16[2,4,2,32,384]{4,3,2,1,0:T(8,128)(2,1)S(1)} %get-tuple-element.20), channel_id=1, source_target_pairs={{0,48},{1,57},{2,50},{3,59},{4,52},{5,61},{6,54},{7,63},{8,56},{9,... | collective-permute-start | bytes 1179656 | tf_op jit(solution)/shard_map/ppermute | solution.py:350
  130.5 1.8 collective-permute-start.22
  132.3 0.3 collective-permute-start.23
  132.6 24.1 %collective-permute-done.6.refs_1_ = bf16[2,4,2,32,384]{4,3,2,1,0:T(8,128)(2,1)} collective-permute-done((bf16[2,4,2,32,384]{4,3,2,1,0:T(8,128)(2,1)S(1)}, bf16[2,4,2,32,384]{4,3,2,1,0:T(8,128)(2,1)}, u32[]{:S(2)}, u32[]{:S(2)}) %collective-permute-start.6) | collective-permute-done | bytes 393248 | tf_op jit(solution)/shard_map/ppermute | solution.py:350
  156.7 0.5 collective-permute-start.9
  157.2 4.5 %collective-permute-done.8.refs_3_ = bf16[2,4,2,32,384]{4,3,2,1,0:T(8,128)(2,1)} collective-permute-done((bf16[2,4,2,32,384]{4,3,2,1,0:T(8,128)(2,1)S(1)}, bf16[2,4,2,32,384]{4,3,2,1,0:T(8,128)(2,1)}, u32[]{:S(2)}, u32[]{:S(2)}) %collective-permute-start.8) | collective-permute-done | bytes 393248 | tf_op jit(solution)/shard_map/ppermute | solution.py:350
  161.6 0.5 collective-permute-start.11
  162.2 0.1 collective-permute-start.12
  162.3 9.9 %shard_map.62.refs_8_ = f32[1,1,68,2,128,128]{5,4,3,2,1,0:T(8,128)} custom-call(s32[2,2,68]{2,1,0:T(2,128)S(1)} %bitcast.29, s32[2,4]{1,0:T(2,128)S(1)} %bitcast.31, s32[2]{0:T(128)S(1)} %pad_add_fusion.place_ref, bf16[8,2,32,384]{3,2,1,0:T(8,128)(2,1)S(1)} %get-tuple-element.25.refs_0_, bf16[8,2,32,384]{3,2,1,0:T(8,128)(2,1)S(1)} %collective-permute-done.18.refs_1_, ...), custom_call_target="tpu_custom_call" | custom-call | flops 2281701376 | bytes 12058624 | tf_op jit(solution)/shard_map/pallas_call | solution.py:247
  172.3 10.4 %shard_map.63 = f32[1,1,68,2,128,128]{5,4,3,2,1,0:T(8,128)} custom-call(s32[2,2,68]{2,1,0:T(2,128)S(1)} %bitcast.30, s32[2,4]{1,0:T(2,128)S(1)} %bitcast.32, s32[2]{0:T(128)S(1)} %pad_add_fusion.place_ref, bf16[2,4,2,32,384]{4,3,2,1,0:T(8,128)(2,1)S(1)} %collective-permute-done.5.refs_0_, ...), custom_call_target="tpu_custom_call", output_to_operand_aliasing={{}: (11, {})} | custom-call | flops 2281701376 | bytes 20971520 | tf_op jit(solution)/shard_map/pallas_call | solution.py:247
  (44 shorter events, 0.6 us)
Async XLA Ops:
  1.8 15.7 %collective-permute-start = (bf16[2,256,384]{2,1,0:T(8,128)(2,1)}, bf16[2,256,384]{2,1,0:T(8,128)(2,1)S(1)}, u32[]{:S(2)}, u32[]{:S(2)}) collective-permute-start(bf16[2,256,384]{2,1,0:T(8,128)(2,1)} %slice.3), channel_id=1, source_target_pairs={{0,2},{2,4},{4,6},{6,8},{8,10},{10,12},{12,14},{14,16},{16,18},{18... | collective-permute-start | bytes 1179656 | tf_op jit(solution)/shard_map/ppermute | solution.py:307
  8.6 5.0 %copy-start.5 = (s32[12]{0:T(128)S(1)}, s32[12]{0:T(128)}, u32[]{:S(2)}) copy-start(s32[12]{0:T(128)} %stack.90.key_ref) | copy-start | bytes 148
  8.6 8.9 %copy-start = (bf16[2,2048,384]{2,1,0:T(8,128)(2,1)S(1)}, bf16[2,2048,384]{2,1,0:T(8,128)(2,1)}, u32[]{:S(2)}) copy-start(bf16[2,2048,384]{2,1,0:T(8,128)(2,1)} %now_ref.3) | copy-start | bytes 9437188
  8.6 8.9 %copy-start.4 = (f32[8,512]{1,0:T(8,128)S(1)}, f32[8,512]{1,0:T(8,128)}, u32[]{:S(2)}) copy-start(f32[8,512]{1,0:T(8,128)} %stack.99.tap_ref) | copy-start | bytes 49156
  13.6 1.4 copy-start.1
  16.5 31.3 %collective-permute-start.13 = (bf16[4,4,2,32,384]{4,3,2,1,0:T(8,128)(2,1)}, bf16[4,4,2,32,384]{4,3,2,1,0:T(8,128)(2,1)}, u32[]{:S(2)}, u32[]{:S(2)}) collective-permute-start(bf16[4,4,2,32,384]{4,3,2,1,0:T(8,128)(2,1)} %shard_map.59), channel_id=1, source_target_pairs={{0,1},{1,0},{2,3},{3,2},{4,5},{5,4},{6,7},{7,6},{8,9},{9,8},{10,11... | collective-permute-start | bytes 2359304 | tf_op jit(solution)/shard_map/ppermute | solution.py:327
  17.5 0.8 copy-start.3
  21.5 24.0 %copy-start.6 = (s32[12]{0:T(128)S(1)}, s32[12]{0:T(128)}, u32[]{:S(2)}) copy-start(s32[12]{0:T(128)} %stack.90.key_ref) | copy-start | bytes 148
  21.5 26.3 %copy-start.2 = (bf16[32,2,32,384]{3,2,1,0:T(8,128)(2,1)S(1)}, bf16[32,2,32,384]{3,2,1,0:T(8,128)(2,1)}, u32[]{:S(2)}) copy-start(bf16[32,2,32,384]{3,2,1,0:T(8,128)(2,1)} %shard_map.58) | copy-start | bytes 4718596
  21.7 19.5 %collective-permute-start.3 = (bf16[8,2,32,384]{3,2,1,0:T(8,128)(2,1)S(1)}, bf16[8,2,32,384]{3,2,1,0:T(8,128)(2,1)S(1)}, u32[]{:S(2)}, u32[]{:S(2)}) collective-permute-start(bf16[8,2,32,384]{3,2,1,0:T(8,128)(2,1)S(1)} %get-tuple-element.29), channel_id=1, source_target_pairs={{0,6},{2,0},{4,2},{6,4},{8,14},{10,8},{12,10},{14,12},{16,22},{18,... | collective-permute-start | bytes 1179656 | tf_op jit(solution)/shard_map/ppermute | solution.py:356
  24.5 16.7 %collective-permute-start.2 = (bf16[8,2,32,384]{3,2,1,0:T(8,128)(2,1)S(1)}, bf16[8,2,32,384]{3,2,1,0:T(8,128)(2,1)S(1)}, u32[]{:S(2)}, u32[]{:S(2)}) collective-permute-start(bf16[8,2,32,384]{3,2,1,0:T(8,128)(2,1)S(1)} %get-tuple-element.30), channel_id=1, source_target_pairs={{0,4},{2,6},{4,0},{6,2},{8,12},{10,14},{12,8},{14,10},{16,20},{18,... | collective-permute-start | bytes 1179656 | tf_op jit(solution)/shard_map/ppermute | solution.py:356
  24.8 20.6 %collective-permute-start.1 = (bf16[8,2,32,384]{3,2,1,0:T(8,128)(2,1)S(1)}, bf16[8,2,32,384]{3,2,1,0:T(8,128)(2,1)S(1)}, u32[]{:S(2)}, u32[]{:S(2)}) collective-permute-start(bf16[8,2,32,384]{3,2,1,0:T(8,128)(2,1)S(1)} %get-tuple-element.31), channel_id=1, source_target_pairs={{0,2},{2,4},{4,6},{6,0},{8,10},{10,12},{12,14},{14,8},{16,18},{18,... | collective-permute-start | bytes 1179656 | tf_op jit(solution)/shard_map/ppermute | solution.py:356
  47.2 115.2 %copy-start.7 = (s32[2,68,2]{1,2,0:T(2,128)S(1)}, s32[2,68,2]{1,2,0:T(2,128)}, u32[]{:S(2)}) copy-start(s32[2,68,2]{1,2,0:T(2,128)} %param.8) | copy-start | bytes 3268
  47.2 115.1 %copy-start.8 = (s32[4,2]{0,1:T(2,128)S(1)}, s32[4,2]{0,1:T(2,128)}, u32[]{:S(2)}) copy-start(s32[4,2]{0,1:T(2,128)} %param.7) | copy-start | bytes 100
  47.2 59.4 %collective-permute-start.4 = (bf16[4,4,2,32,384]{4,3,2,1,0:T(8,128)(2,1)S(1)}, bf16[4,4,2,32,384]{4,3,2,1,0:T(8,128)(2,1)S(1)}, u32[]{:S(2)}, u32[]{:S(2)}) collective-permute-start(bf16[4,4,2,32,384]{4,3,2,1,0:T(8,128)(2,1)S(1)} %shard_map.56), channel_id=1, source_target_pairs={{0,1},{1,0},{2,3},{3,2},{4,5},{5,4},{6,7},{7,6},{8,9},{9,8},{10,11... | collective-permute-start | bytes 2359304 | tf_op jit(solution)/shard_map/ppermute | solution.py:327
  50.6 19.7 %collective-permute-start.14 = (bf16[2,4,2,32,384]{4,3,2,1,0:T(8,128)(2,1)S(1)}, bf16[2,4,2,32,384]{4,3,2,1,0:T(8,128)(2,1)S(1)}, u32[]{:S(2)}, u32[]{:S(2)}) collective-permute-start(bf16[2,4,2,32,384]{4,3,2,1,0:T(8,128)(2,1)S(1)} %get-tuple-element.21), channel_id=1, source_target_pairs={{0,0},{1,9},{2,2},{3,11},{4,4},{5,13},{6,6},{7,15},{8,8},{9,1},{10... | collective-permute-start | bytes 1179656 | tf_op jit(solution)/shard_map/ppermute | solution.py:350
  54.2 40.0 %collective-permute-start.15 = (bf16[2,4,2,32,384]{4,3,2,1,0:T(8,128)(2,1)S(1)}, bf16[2,4,2,32,384]{4,3,2,1,0:T(8,128)(2,1)S(1)}, u32[]{:S(2)}, u32[]{:S(2)}) collective-permute-start(bf16[2,4,2,32,384]{4,3,2,1,0:T(8,128)(2,1)S(1)} %get-tuple-element.22), channel_id=1, source_target_pairs={{0,16},{1,25},{2,18},{3,27},{4,20},{5,29},{6,22},{7,31},{8,24},{9,... | collective-permute-start | bytes 1179656 | tf_op jit(solution)/shard_map/ppermute | solution.py:350
  59.7 38.3 %collective-permute-start.16 = (bf16[2,4,2,32,384]{4,3,2,1,0:T(8,128)(2,1)S(1)}, bf16[2,4,2,32,384]{4,3,2,1,0:T(8,128)(2,1)S(1)}, u32[]{:S(2)}, u32[]{:S(2)}) collective-permute-start(bf16[2,4,2,32,384]{4,3,2,1,0:T(8,128)(2,1)S(1)} %get-tuple-element.23), channel_id=1, source_target_pairs={{0,32},{1,41},{2,34},{3,43},{4,36},{5,45},{6,38},{7,47},{8,40},{9,... | collective-permute-start | bytes 1179656 | tf_op jit(solution)/shard_map/ppermute | solution.py:350
  68.3 32.6 %collective-permute-start.17 = (bf16[2,4,2,32,384]{4,3,2,1,0:T(8,128)(2,1)S(1)}, bf16[2,4,2,32,384]{4,3,2,1,0:T(8,128)(2,1)S(1)}, u32[]{:S(2)}, u32[]{:S(2)}) collective-permute-start(bf16[2,4,2,32,384]{4,3,2,1,0:T(8,128)(2,1)S(1)} %get-tuple-element.24), channel_id=1, source_target_pairs={{0,48},{1,57},{2,50},{3,59},{4,52},{5,61},{6,54},{7,63},{8,56},{9,... | collective-permute-start | bytes 1179656 | tf_op jit(solution)/shard_map/ppermute | solution.py:350
  103.8 18.0 %collective-permute-start.18 = (bf16[8,2,32,384]{3,2,1,0:T(8,128)(2,1)S(1)}, bf16[8,2,32,384]{3,2,1,0:T(8,128)(2,1)S(1)}, u32[]{:S(2)}, u32[]{:S(2)}) collective-permute-start(bf16[8,2,32,384]{3,2,1,0:T(8,128)(2,1)S(1)} %get-tuple-element.26), channel_id=1, source_target_pairs={{0,2},{2,4},{4,6},{6,0},{8,10},{10,12},{12,14},{14,8},{16,18},{18,... | collective-permute-start | bytes 1179656 | tf_op jit(solution)/shard_map/ppermute | solution.py:356
  103.9 19.8 %collective-permute-start.19 = (bf16[8,2,32,384]{3,2,1,0:T(8,128)(2,1)S(1)}, bf16[8,2,32,384]{3,2,1,0:T(8,128)(2,1)S(1)}, u32[]{:S(2)}, u32[]{:S(2)}) collective-permute-start(bf16[8,2,32,384]{3,2,1,0:T(8,128)(2,1)S(1)} %get-tuple-element.27), channel_id=1, source_target_pairs={{0,4},{2,6},{4,0},{6,2},{8,12},{10,14},{12,8},{14,10},{16,20},{18,... | collective-permute-start | bytes 1179656 | tf_op jit(solution)/shard_map/ppermute | solution.py:356
  105.4 22.0 %collective-permute-start.20 = (bf16[8,2,32,384]{3,2,1,0:T(8,128)(2,1)S(1)}, bf16[8,2,32,384]{3,2,1,0:T(8,128)(2,1)S(1)}, u32[]{:S(2)}, u32[]{:S(2)}) collective-permute-start(bf16[8,2,32,384]{3,2,1,0:T(8,128)(2,1)S(1)} %get-tuple-element.28), channel_id=1, source_target_pairs={{0,6},{2,0},{4,2},{6,4},{8,14},{10,8},{12,10},{14,12},{16,22},{18,... | collective-permute-start | bytes 1179656 | tf_op jit(solution)/shard_map/ppermute | solution.py:356
  106.6 23.9 %collective-permute-start.21 = (bf16[8,2,32,384]{3,2,1,0:T(8,128)(2,1)S(1)}, bf16[8,2,32,384]{3,2,1,0:T(8,128)(2,1)S(1)}, u32[]{:S(2)}, u32[]{:S(2)}) collective-permute-start(bf16[8,2,32,384]{3,2,1,0:T(8,128)(2,1)S(1)} %get-tuple-element.25.refs_0_), channel_id=1, source_target_pairs={{0,1},{1,0},{2,3},{3,2},{4,5},{5,4},{6,7},{7,6},{8,9},{9,8},{10,11... | collective-permute-start | bytes 1179656 | tf_op jit(solution)/shard_map/ppermute | solution.py:327
  109.4 22.9 %collective-permute-start.5 = (bf16[2,4,2,32,384]{4,3,2,1,0:T(8,128)(2,1)S(1)}, bf16[2,4,2,32,384]{4,3,2,1,0:T(8,128)(2,1)S(1)}, u32[]{:S(2)}, u32[]{:S(2)}) collective-permute-start(bf16[2,4,2,32,384]{4,3,2,1,0:T(8,128)(2,1)S(1)} %get-tuple-element.17), channel_id=1, source_target_pairs={{0,0},{1,9},{2,2},{3,11},{4,4},{5,13},{6,6},{7,15},{8,8},{9,1},{10... | collective-permute-start | bytes 1179656 | tf_op jit(solution)/shard_map/ppermute | solution.py:350
  121.8 34.8 %collective-permute-start.6 = (bf16[2,4,2,32,384]{4,3,2,1,0:T(8,128)(2,1)S(1)}, bf16[2,4,2,32,384]{4,3,2,1,0:T(8,128)(2,1)}, u32[]{:S(2)}, u32[]{:S(2)}) collective-permute-start(bf16[2,4,2,32,384]{4,3,2,1,0:T(8,128)(2,1)S(1)} %get-tuple-element.18), channel_id=1, source_target_pairs={{0,16},{1,25},{2,18},{3,27},{4,20},{5,29},{6,22},{7,31},{8,24},{9,... | collective-permute-start | bytes 1179656 | tf_op jit(solution)/shard_map/ppermute | solution.py:350
  123.8 32.9 %collective-permute-start.7 = (bf16[2,4,2,32,384]{4,3,2,1,0:T(8,128)(2,1)S(1)}, bf16[2,4,2,32,384]{4,3,2,1,0:T(8,128)(2,1)}, u32[]{:S(2)}, u32[]{:S(2)}) collective-permute-start(bf16[2,4,2,32,384]{4,3,2,1,0:T(8,128)(2,1)S(1)} %get-tuple-element.19), channel_id=1, source_target_pairs={{0,32},{1,41},{2,34},{3,43},{4,36},{5,45},{6,38},{7,47},{8,40},{9,... | collective-permute-start | bytes 1179656 | tf_op jit(solution)/shard_map/ppermute | solution.py:350
  127.5 34.2 %collective-permute-start.8 = (bf16[2,4,2,32,384]{4,3,2,1,0:T(8,128)(2,1)S(1)}, bf16[2,4,2,32,384]{4,3,2,1,0:T(8,128)(2,1)}, u32[]{:S(2)}, u32[]{:S(2)}) collective-permute-start(bf16[2,4,2,32,384]{4,3,2,1,0:T(8,128)(2,1)S(1)} %get-tuple-element.20), channel_id=1, source_target_pairs={{0,48},{1,57},{2,50},{3,59},{4,52},{5,61},{6,54},{7,63},{8,56},{9,... | collective-permute-start | bytes 1179656 | tf_op jit(solution)/shard_map/ppermute | solution.py:350
  130.5 31.2 %collective-permute-start.22 = (bf16[8,2,32,384]{3,2,1,0:T(8,128)(2,1)S(1)}, bf16[8,2,32,384]{3,2,1,0:T(8,128)(2,1)S(1)}, u32[]{:S(2)}, u32[]{:S(2)}) collective-permute-start(bf16[8,2,32,384]{3,2,1,0:T(8,128)(2,1)S(1)} %collective-permute-done.18.refs_1_), channel_id=1, source_target_pairs={{0,1},{1,0},{2,3},{3,2},{4,5},{5,4},{6,7},{7,6},{8,9},{9,8},{10,11... | collective-permute-start | bytes 1179656 | tf_op jit(solution)/shard_map/ppermute | solution.py:327
  132.3 29.9 %collective-permute-start.23 = (bf16[8,2,32,384]{3,2,1,0:T(8,128)(2,1)S(1)}, bf16[8,2,32,384]{3,2,1,0:T(8,128)(2,1)S(1)}, u32[]{:S(2)}, u32[]{:S(2)}) collective-permute-start(bf16[8,2,32,384]{3,2,1,0:T(8,128)(2,1)S(1)} %collective-permute-done.19.refs_2_), channel_id=1, source_target_pairs={{0,1},{1,0},{2,3},{3,2},{4,5},{5,4},{6,7},{7,6},{8,9},{9,8},{10,11... | collective-permute-start | bytes 1179656 | tf_op jit(solution)/shard_map/ppermute | solution.py:327
  156.7 5.7 %collective-permute-start.24 = (bf16[8,2,32,384]{3,2,1,0:T(8,128)(2,1)S(1)}, bf16[8,2,32,384]{3,2,1,0:T(8,128)(2,1)S(1)}, u32[]{:S(2)}, u32[]{:S(2)}) collective-permute-start(bf16[8,2,32,384]{3,2,1,0:T(8,128)(2,1)S(1)} %collective-permute-done.20.refs_3_), channel_id=1, source_target_pairs={{0,1},{1,0},{2,3},{3,2},{4,5},{5,4},{6,7},{7,6},{8,9},{9,8},{10,11... | collective-permute-start | bytes 1179656 | tf_op jit(solution)/shard_map/ppermute | solution.py:327
  156.7 15.6 %collective-permute-start.9 = (bf16[2,4,2,32,384]{4,3,2,1,0:T(8,128)(2,1)S(1)}, bf16[2,4,2,32,384]{4,3,2,1,0:T(8,128)(2,1)}, u32[]{:S(2)}, u32[]{:S(2)}) collective-permute-start(bf16[2,4,2,32,384]{4,3,2,1,0:T(8,128)(2,1)S(1)} %collective-permute-done.5.refs_0_), channel_id=1, source_target_pairs={{0,1},{1,0},{2,3},{3,2},{4,5},{5,4},{6,7},{7,6},{8,9},{9,8},{10,11... | collective-permute-start | bytes 1179656 | tf_op jit(solution)/shard_map/ppermute | solution.py:327
  161.6 10.7 %collective-permute-start.10 = (bf16[2,4,2,32,384]{4,3,2,1,0:T(8,128)(2,1)}, bf16[2,4,2,32,384]{4,3,2,1,0:T(8,128)(2,1)}, u32[]{:S(2)}, u32[]{:S(2)}) collective-permute-start(bf16[2,4,2,32,384]{4,3,2,1,0:T(8,128)(2,1)} %collective-permute-done.6.refs_1_), channel_id=1, source_target_pairs={{0,1},{1,0},{2,3},{3,2},{4,5},{5,4},{6,7},{7,6},{8,9},{9,8},{10,11... | collective-permute-start | bytes 1179656 | tf_op jit(solution)/shard_map/ppermute | solution.py:327
  161.6 10.7 %collective-permute-start.11 = (bf16[2,4,2,32,384]{4,3,2,1,0:T(8,128)(2,1)}, bf16[2,4,2,32,384]{4,3,2,1,0:T(8,128)(2,1)}, u32[]{:S(2)}, u32[]{:S(2)}) collective-permute-start(bf16[2,4,2,32,384]{4,3,2,1,0:T(8,128)(2,1)} %collective-permute-done.7.refs_2_), channel_id=1, source_target_pairs={{0,1},{1,0},{2,3},{3,2},{4,5},{5,4},{6,7},{7,6},{8,9},{9,8},{10,11... | collective-permute-start | bytes 1179656 | tf_op jit(solution)/shard_map/ppermute | solution.py:327
  162.2 10.2 %collective-permute-start.12 = (bf16[2,4,2,32,384]{4,3,2,1,0:T(8,128)(2,1)}, bf16[2,4,2,32,384]{4,3,2,1,0:T(8,128)(2,1)}, u32[]{:S(2)}, u32[]{:S(2)}) collective-permute-start(bf16[2,4,2,32,384]{4,3,2,1,0:T(8,128)(2,1)} %collective-permute-done.8.refs_3_), channel_id=1, source_target_pairs={{0,1},{1,0},{2,3},{3,2},{4,5},{5,4},{6,7},{7,6},{8,9},{9,8},{10,11... | collective-permute-start | bytes 1179656 | tf_op jit(solution)/shard_map/ppermute | solution.py:327

commit v4 on v3

--- a/solution.py
+++ b/solution.py
@@ -233,8 +233,10 @@
             imag = (gram[PANEL:, :PANEL] - gram[:PANEL, PANEL:]) * scale
             held[at, 0] = real + held[at, 0] if chunk == 1 else real
             held[at, 1] = imag + held[at, 1] if chunk == 1 else imag
-        for slot in range(PER_STEP):
-            result(index * PER_STEP + slot).start()
+            if slot in (PER_STEP // 2, PER_STEP - 1):
+                first = 0 if slot < PER_STEP - 1 else PER_STEP // 2 + 1
+                for done in range(first, slot + 1):
+                    result(index * PER_STEP + done).start()
 
     repeat(TSLOT // PER_STEP, multiply)
     repeat(TSLOT, lambda at: result(at).wait())

time: 184 us -> 184 us (level)
  no operation moved by 1% of the time
where the time goes in v4:
time: 184 us; the launch traced here: 182 us
  waiting for transfers between devices  89.9 us (49%)
  starting transfers between devices  45.3 us (25%)
  Pallas kernels  39.5 us (21%)
  local copies, waits for them, and re-layouts  6.82 us (4%)
    ppermute x8, waiting for transfers between devices, far(): moved.append(lax.ppermute(payload[turn], everyone, across(turn)))  59.2 us
    ppermute x6, waiting for transfers between devices, near(): moved[step] = lax.ppermute(payload[step], 'chan', along(step))  30.7 us
    ppermute x8, starting transfers between devices, far(): moved.append(lax.ppermute(payload[turn], everyone, across(turn)))  30.2 us
    pallas_call x2, Pallas kernels, correlate_call(): pl.pallas_call(functools.partial(correlate_body, chunk), out_shape=jax.Sh...  19.7 us
    pallas_call x5, Pallas kernels, move_blocks(): pl.pallas_call(body, out_shape=[jax.ShapeDtypeStruct(shape, jnp.bfloat16)...  11.7 us
    pallas_call x2, Pallas kernels, filter_call(): pl.pallas_call(functools.partial(filter_body, slot_of, halo is not None),...  8.05 us
    ppermute x6, starting transfers between devices, near(): moved[step] = lax.ppermute(payload[step], 'chan', along(step))  6.29 us
    ppermute x10, starting transfers between devices, swap(): return lax.ppermute(piece, 'grp', [(0, 1), (1, 0)])  4.81 us
  transfers between devices with their start and end apart: 25, of which 8 were waited for; matrix products, arithmetic and copies ran while one was open for 2% of the time, Pallas kernels for 16%

profile of v4, /device:TPU:1, one launch (start us, length us, event | category | flops | bytes accessed | tf_op | source)
XLA Modules:
  0.0 182.2 jit_solution(6569074810915529324)
XLA Ops:
  0.0 1.8 slice.3
  1.8 4.0 %collective-permute-start = (bf16[2,256,384]{2,1,0:T(8,128)(2,1)}, bf16[2,256,384]{2,1,0:T(8,128)(2,1)S(1)}, u32[]{:S(2)}, u32[]{:S(2)}) collective-permute-start(bf16[2,256,384]{2,1,0:T(8,128)(2,1)} %slice.3), channel_id=1, source_target_pairs={{0,2},{2,4},{4,6},{6,8},{8,10},{10,12},{12,14},{14,16},{16,18},{18... | collective-permute-start | bytes 1179656 | tf_op jit(solution)/shard_map/ppermute | solution.py:309
  6.0 0.7 rev.3
  6.7 0.1 stack.98
  6.8 0.1 stack.97
  7.4 0.6 stack.99.tap_ref
  8.0 0.6 stack.90.key_ref
  8.6 5.0 %shard_map.58 = bf16[32,2,32,384]{3,2,1,0:T(8,128)(2,1)} custom-call(f32[32,512]{1,0:T(8,128)} %constant.141.clone.trig_ref, f32[8,512]{1,0:T(8,128)} %stack.99.tap_ref, bf16[2,2048,384]{2,1,0:T(8,128)(2,1)} %now_ref.3, bf16[2,2048,384]{2,1,0:T(8,128)(2,1)} %now_ref.3), custom_call_target="tpu_custom_call" | custom-call | flops 1610612736 | bytes 3145728 | tf_op jit(solution)/shard_map/pallas_call | solution.py:104
  13.6 1.4 copy-done.1
  15.0 1.5 shard_map.59
  16.5 1.0 collective-permute-start.13
  17.5 0.8 copy-done.3
  18.4 3.1 %shard_map.55 = bf16[32,2,32,384]{3,2,1,0:T(8,128)(2,1)S(1)} custom-call(f32[32,512]{1,0:T(8,128)S(1)} %copy-done.3, f32[8,512]{1,0:T(8,128)S(1)} %copy-done.4, bf16[2,2048,384]{2,1,0:T(8,128)(2,1)S(1)} %copy-done, bf16[2,2048,384]{2,1,0:T(8,128)(2,1)S(1)} %copy-done, bf16[2,256,384]{2,1,0:T(8,128)(2,1)S(1)} %collective-permute-done.rest_0_), custom_call_target="tpu_custom_call" | custom-call | flops 1610612736 | bytes 3145728 | tf_op jit(solution)/shard_map/pallas_call | solution.py:104
  21.5 0.2 dynamic-slice_bitcast_fusion
  21.7 2.8 %collective-permute-start.3 = (bf16[8,2,32,384]{3,2,1,0:T(8,128)(2,1)S(1)}, bf16[8,2,32,384]{3,2,1,0:T(8,128)(2,1)S(1)}, u32[]{:S(2)}, u32[]{:S(2)}) collective-permute-start(bf16[8,2,32,384]{3,2,1,0:T(8,128)(2,1)S(1)} %get-tuple-element.29), channel_id=1, source_target_pairs={{0,6},{2,0},{4,2},{6,4},{8,14},{10,8},{12,10},{14,12},{16,22},{18,... | collective-permute-start | bytes 1179656 | tf_op jit(solution)/shard_map/ppermute | solution.py:358
  24.5 0.3 collective-permute-start.2
  24.8 0.4 collective-permute-start.1
  25.2 15.9 %collective-permute-done.3.refs_3_ = bf16[8,2,32,384]{3,2,1,0:T(8,128)(2,1)S(1)} collective-permute-done((bf16[8,2,32,384]{3,2,1,0:T(8,128)(2,1)S(1)}, bf16[8,2,32,384]{3,2,1,0:T(8,128)(2,1)S(1)}, u32[]{:S(2)}, u32[]{:S(2)}) %collective-permute-start.3) | collective-permute-done | bytes 393248 | tf_op jit(solution)/shard_map/ppermute | solution.py:358
  41.2 4.3 %collective-permute-done.1.refs_1_ = bf16[8,2,32,384]{3,2,1,0:T(8,128)(2,1)S(1)} collective-permute-done((bf16[8,2,32,384]{3,2,1,0:T(8,128)(2,1)S(1)}, bf16[8,2,32,384]{3,2,1,0:T(8,128)(2,1)S(1)}, u32[]{:S(2)}, u32[]{:S(2)}) %collective-permute-start.1) | collective-permute-done | bytes 393248 | tf_op jit(solution)/shard_map/ppermute | solution.py:358
  45.4 1.7 shard_map.56
  47.2 0.6 collective-permute-start.4
  47.8 2.8 %shard_map.60 = (bf16[2,4,2,32,384]{4,3,2,1,0:T(8,128)(2,1)S(1)}, bf16[2,4,2,32,384]{4,3,2,1,0:T(8,128)(2,1)S(1)}, bf16[2,4,2,32,384]{4,3,2,1,0:T(8,128)(2,1)S(1)}, bf16[2,4,2,32,384]{4,3,2,1,0:T(8,128)(2,1)S(1)}) custom-call(s32[12]{0:T(128)S(1)} %copy-done.6, bf16[8,4,2,32,384]{4,3,2,1,0:T(8,128)(2,1)S(1)} %bitcast.27, ...), custom_call_target="tpu_custom_call" | custom-call | tf_op jit(solution)/shard_map/pallas_call | solution.py:293
  50.6 3.5 %collective-permute-start.14 = (bf16[2,4,2,32,384]{4,3,2,1,0:T(8,128)(2,1)S(1)}, bf16[2,4,2,32,384]{4,3,2,1,0:T(8,128)(2,1)S(1)}, u32[]{:S(2)}, u32[]{:S(2)}) collective-permute-start(bf16[2,4,2,32,384]{4,3,2,1,0:T(8,128)(2,1)S(1)} %get-tuple-element.21), channel_id=1, source_target_pairs={{0,0},{1,9},{2,2},{3,11},{4,4},{5,13},{6,6},{7,15},{8,8},{9,1},{10... | collective-permute-start | bytes 1179656 | tf_op jit(solution)/shard_map/ppermute | solution.py:352
  54.2 5.5 %collective-permute-start.15 = (bf16[2,4,2,32,384]{4,3,2,1,0:T(8,128)(2,1)S(1)}, bf16[2,4,2,32,384]{4,3,2,1,0:T(8,128)(2,1)S(1)}, u32[]{:S(2)}, u32[]{:S(2)}) collective-permute-start(bf16[2,4,2,32,384]{4,3,2,1,0:T(8,128)(2,1)S(1)} %get-tuple-element.22), channel_id=1, source_target_pairs={{0,16},{1,25},{2,18},{3,27},{4,20},{5,29},{6,22},{7,31},{8,24},{9,... | collective-permute-start | bytes 1179656 | tf_op jit(solution)/shard_map/ppermute | solution.py:352
  59.7 8.6 %collective-permute-start.16 = (bf16[2,4,2,32,384]{4,3,2,1,0:T(8,128)(2,1)S(1)}, bf16[2,4,2,32,384]{4,3,2,1,0:T(8,128)(2,1)S(1)}, u32[]{:S(2)}, u32[]{:S(2)}) collective-permute-start(bf16[2,4,2,32,384]{4,3,2,1,0:T(8,128)(2,1)S(1)} %get-tuple-element.23), channel_id=1, source_target_pairs={{0,32},{1,41},{2,34},{3,43},{4,36},{5,45},{6,38},{7,47},{8,40},{9,... | collective-permute-start | bytes 1179656 | tf_op jit(solution)/shard_map/ppermute | solution.py:352
  68.3 2.0 %collective-permute-start.17 = (bf16[2,4,2,32,384]{4,3,2,1,0:T(8,128)(2,1)S(1)}, bf16[2,4,2,32,384]{4,3,2,1,0:T(8,128)(2,1)S(1)}, u32[]{:S(2)}, u32[]{:S(2)}) collective-permute-start(bf16[2,4,2,32,384]{4,3,2,1,0:T(8,128)(2,1)S(1)} %get-tuple-element.24), channel_id=1, source_target_pairs={{0,48},{1,57},{2,50},{3,59},{4,52},{5,61},{6,54},{7,63},{8,56},{9,... | collective-permute-start | bytes 1179656 | tf_op jit(solution)/shard_map/ppermute | solution.py:352
  70.3 23.9 %collective-permute-done.15.refs_1_ = bf16[2,4,2,32,384]{4,3,2,1,0:T(8,128)(2,1)S(1)} collective-permute-done((bf16[2,4,2,32,384]{4,3,2,1,0:T(8,128)(2,1)S(1)}, bf16[2,4,2,32,384]{4,3,2,1,0:T(8,128)(2,1)S(1)}, u32[]{:S(2)}, u32[]{:S(2)}) %collective-permute-start.15) | collective-permute-done | bytes 393248 | tf_op jit(solution)/shard_map/ppermute | solution.py:352
  94.2 3.8 %collective-permute-done.16.refs_2_ = bf16[2,4,2,32,384]{4,3,2,1,0:T(8,128)(2,1)S(1)} collective-permute-done((bf16[2,4,2,32,384]{4,3,2,1,0:T(8,128)(2,1)S(1)}, bf16[2,4,2,32,384]{4,3,2,1,0:T(8,128)(2,1)S(1)}, u32[]{:S(2)}, u32[]{:S(2)}) %collective-permute-start.16) | collective-permute-done | bytes 393248 | tf_op jit(solution)/shard_map/ppermute | solution.py:352
  98.0 2.9 %collective-permute-done.17.refs_3_ = bf16[2,4,2,32,384]{4,3,2,1,0:T(8,128)(2,1)S(1)} collective-permute-done((bf16[2,4,2,32,384]{4,3,2,1,0:T(8,128)(2,1)S(1)}, bf16[2,4,2,32,384]{4,3,2,1,0:T(8,128)(2,1)S(1)}, u32[]{:S(2)}, u32[]{:S(2)}) %collective-permute-start.17) | collective-permute-done | bytes 393248 | tf_op jit(solution)/shard_map/ppermute | solution.py:352
  100.9 2.9 %shard_map.61 = (bf16[8,2,32,384]{3,2,1,0:T(8,128)(2,1)S(1)}, bf16[8,2,32,384]{3,2,1,0:T(8,128)(2,1)S(1)}, bf16[8,2,32,384]{3,2,1,0:T(8,128)(2,1)S(1)}, bf16[8,2,32,384]{3,2,1,0:T(8,128)(2,1)S(1)}) custom-call(s32[12]{0:T(128)S(1)} %copy-done.6, bf16[2,4,2,32,384]{4,3,2,1,0:T(8,128)(2,1)S(1)} %collective-permute-done.14.refs_0_, ...), custom_call_target="tpu_custom_call" | custom-call | tf_op jit(solution)/shard_map/pallas_call | solution.py:293
  103.8 0.1 collective-permute-start.18
  103.9 1.5 collective-permute-start.19
  105.4 1.2 collective-permute-start.20
  106.6 2.8 %shard_map.57 = (bf16[2,4,2,32,384]{4,3,2,1,0:T(8,128)(2,1)S(1)}, bf16[2,4,2,32,384]{4,3,2,1,0:T(8,128)(2,1)S(1)}, bf16[2,4,2,32,384]{4,3,2,1,0:T(8,128)(2,1)S(1)}, bf16[2,4,2,32,384]{4,3,2,1,0:T(8,128)(2,1)S(1)}) custom-call(s32[12]{0:T(128)S(1)} %copy-done.6, bf16[8,2,32,384]{3,2,1,0:T(8,128)(2,1)S(1)} %get-tuple-element.32.refs_0_, ...), custom_call_target="tpu_custom_call" | custom-call | tf_op jit(solution)/shard_map/pallas_call | solution.py:293
  109.4 1.9 %collective-permute-start.5 = (bf16[2,4,2,32,384]{4,3,2,1,0:T(8,128)(2,1)S(1)}, bf16[2,4,2,32,384]{4,3,2,1,0:T(8,128)(2,1)S(1)}, u32[]{:S(2)}, u32[]{:S(2)}) collective-permute-start(bf16[2,4,2,32,384]{4,3,2,1,0:T(8,128)(2,1)S(1)} %get-tuple-element.17), channel_id=1, source_target_pairs={{0,0},{1,9},{2,2},{3,11},{4,4},{5,13},{6,6},{7,15},{8,8},{9,1},{10... | collective-permute-start | bytes 1179656 | tf_op jit(solution)/shard_map/ppermute | solution.py:352
  111.3 10.5 %collective-permute-done.18.refs_1_ = bf16[8,2,32,384]{3,2,1,0:T(8,128)(2,1)S(1)} collective-permute-done((bf16[8,2,32,384]{3,2,1,0:T(8,128)(2,1)S(1)}, bf16[8,2,32,384]{3,2,1,0:T(8,128)(2,1)S(1)}, u32[]{:S(2)}, u32[]{:S(2)}) %collective-permute-start.18) | collective-permute-done | bytes 393248 | tf_op jit(solution)/shard_map/ppermute | solution.py:358
  121.8 1.9 %collective-permute-start.6 = (bf16[2,4,2,32,384]{4,3,2,1,0:T(8,128)(2,1)S(1)}, bf16[2,4,2,32,384]{4,3,2,1,0:T(8,128)(2,1)}, u32[]{:S(2)}, u32[]{:S(2)}) collective-permute-start(bf16[2,4,2,32,384]{4,3,2,1,0:T(8,128)(2,1)S(1)} %get-tuple-element.18), channel_id=1, source_target_pairs={{0,16},{1,25},{2,18},{3,27},{4,20},{5,29},{6,22},{7,31},{8,24},{9,... | collective-permute-start | bytes 1179656 | tf_op jit(solution)/shard_map/ppermute | solution.py:352
  123.8 3.7 %collective-permute-start.7 = (bf16[2,4,2,32,384]{4,3,2,1,0:T(8,128)(2,1)S(1)}, bf16[2,4,2,32,384]{4,3,2,1,0:T(8,128)(2,1)}, u32[]{:S(2)}, u32[]{:S(2)}) collective-permute-start(bf16[2,4,2,32,384]{4,3,2,1,0:T(8,128)(2,1)S(1)} %get-tuple-element.19), channel_id=1, source_target_pairs={{0,32},{1,41},{2,34},{3,43},{4,36},{5,45},{6,38},{7,47},{8,40},{9,... | collective-permute-start | bytes 1179656 | tf_op jit(solution)/shard_map/ppermute | solution.py:352
  127.5 3.0 %collective-permute-start.8 = (bf16[2,4,2,32,384]{4,3,2,1,0:T(8,128)(2,1)S(1)}, bf16[2,4,2,32,384]{4,3,2,1,0:T(8,128)(2,1)}, u32[]{:S(2)}, u32[]{:S(2)}) collective-permute-start(bf16[2,4,2,32,384]{4,3,2,1,0:T(8,128)(2,1)S(1)} %get-tuple-element.20), channel_id=1, source_target_pairs={{0,48},{1,57},{2,50},{3,59},{4,52},{5,61},{6,54},{7,63},{8,56},{9,... | collective-permute-start | bytes 1179656 | tf_op jit(solution)/shard_map/ppermute | solution.py:352
  130.5 1.8 collective-permute-start.22
  132.3 0.3 collective-permute-start.23
  132.6 24.1 %collective-permute-done.6.refs_1_ = bf16[2,4,2,32,384]{4,3,2,1,0:T(8,128)(2,1)} collective-permute-done((bf16[2,4,2,32,384]{4,3,2,1,0:T(8,128)(2,1)S(1)}, bf16[2,4,2,32,384]{4,3,2,1,0:T(8,128)(2,1)}, u32[]{:S(2)}, u32[]{:S(2)}) %collective-permute-start.6) | collective-permute-done | bytes 393248 | tf_op jit(solution)/shard_map/ppermute | solution.py:352
  156.7 0.5 collective-permute-start.9
  157.2 4.5 %collective-permute-done.8.refs_3_ = bf16[2,4,2,32,384]{4,3,2,1,0:T(8,128)(2,1)} collective-permute-done((bf16[2,4,2,32,384]{4,3,2,1,0:T(8,128)(2,1)S(1)}, bf16[2,4,2,32,384]{4,3,2,1,0:T(8,128)(2,1)}, u32[]{:S(2)}, u32[]{:S(2)}) %collective-permute-start.8) | collective-permute-done | bytes 393248 | tf_op jit(solution)/shard_map/ppermute | solution.py:352
  161.6 0.5 collective-permute-start.11
  162.2 0.1 collective-permute-start.12
  162.3 9.6 %shard_map.62.refs_8_ = f32[1,1,68,2,128,128]{5,4,3,2,1,0:T(8,128)} custom-call(s32[2,2,68]{2,1,0:T(2,128)S(1)} %bitcast.29, s32[2,4]{1,0:T(2,128)S(1)} %bitcast.31, s32[2]{0:T(128)S(1)} %pad_add_fusion.place_ref, bf16[8,2,32,384]{3,2,1,0:T(8,128)(2,1)S(1)} %get-tuple-element.25.refs_0_, bf16[8,2,32,384]{3,2,1,0:T(8,128)(2,1)S(1)} %collective-permute-done.18.refs_1_, ...), custom_call_target="tpu_custom_call" | custom-call | flops 2281701376 | bytes 12058624 | tf_op jit(solution)/shard_map/pallas_call | solution.py:249
  172.0 10.0 %shard_map.63 = f32[1,1,68,2,128,128]{5,4,3,2,1,0:T(8,128)} custom-call(s32[2,2,68]{2,1,0:T(2,128)S(1)} %bitcast.30, s32[2,4]{1,0:T(2,128)S(1)} %bitcast.32, s32[2]{0:T(128)S(1)} %pad_add_fusion.place_ref, bf16[2,4,2,32,384]{4,3,2,1,0:T(8,128)(2,1)S(1)} %collective-permute-done.5.refs_0_, ...), custom_call_target="tpu_custom_call", output_to_operand_aliasing={{}: (11, {})} | custom-call | flops 2281701376 | bytes 20971520 | tf_op jit(solution)/shard_map/pallas_call | solution.py:249
  (44 shorter events, 0.6 us)
Async XLA Ops:
  1.8 15.7 %collective-permute-start = (bf16[2,256,384]{2,1,0:T(8,128)(2,1)}, bf16[2,256,384]{2,1,0:T(8,128)(2,1)S(1)}, u32[]{:S(2)}, u32[]{:S(2)}) collective-permute-start(bf16[2,256,384]{2,1,0:T(8,128)(2,1)} %slice.3), channel_id=1, source_target_pairs={{0,2},{2,4},{4,6},{6,8},{8,10},{10,12},{12,14},{14,16},{16,18},{18... | collective-permute-start | bytes 1179656 | tf_op jit(solution)/shard_map/ppermute | solution.py:309
  8.6 5.0 %copy-start.5 = (s32[12]{0:T(128)S(1)}, s32[12]{0:T(128)}, u32[]{:S(2)}) copy-start(s32[12]{0:T(128)} %stack.90.key_ref) | copy-start | bytes 148
  8.6 8.9 %copy-start = (bf16[2,2048,384]{2,1,0:T(8,128)(2,1)S(1)}, bf16[2,2048,384]{2,1,0:T(8,128)(2,1)}, u32[]{:S(2)}) copy-start(bf16[2,2048,384]{2,1,0:T(8,128)(2,1)} %now_ref.3) | copy-start | bytes 9437188
  8.6 8.9 %copy-start.4 = (f32[8,512]{1,0:T(8,128)S(1)}, f32[8,512]{1,0:T(8,128)}, u32[]{:S(2)}) copy-start(f32[8,512]{1,0:T(8,128)} %stack.99.tap_ref) | copy-start | bytes 49156
  13.6 1.4 copy-start.1
  16.5 31.3 %collective-permute-start.13 = (bf16[4,4,2,32,384]{4,3,2,1,0:T(8,128)(2,1)}, bf16[4,4,2,32,384]{4,3,2,1,0:T(8,128)(2,1)}, u32[]{:S(2)}, u32[]{:S(2)}) collective-permute-start(bf16[4,4,2,32,384]{4,3,2,1,0:T(8,128)(2,1)} %shard_map.59), channel_id=1, source_target_pairs={{0,1},{1,0},{2,3},{3,2},{4,5},{5,4},{6,7},{7,6},{8,9},{9,8},{10,11... | collective-permute-start | bytes 2359304 | tf_op jit(solution)/shard_map/ppermute | solution.py:329
  17.5 0.8 copy-start.3
  21.5 24.0 %copy-start.6 = (s32[12]{0:T(128)S(1)}, s32[12]{0:T(128)}, u32[]{:S(2)}) copy-start(s32[12]{0:T(128)} %stack.90.key_ref) | copy-start | bytes 148
  21.5 26.3 %copy-start.2 = (bf16[32,2,32,384]{3,2,1,0:T(8,128)(2,1)S(1)}, bf16[32,2,32,384]{3,2,1,0:T(8,128)(2,1)}, u32[]{:S(2)}) copy-start(bf16[32,2,32,384]{3,2,1,0:T(8,128)(2,1)} %shard_map.58) | copy-start | bytes 4718596
  21.7 19.5 %collective-permute-start.3 = (bf16[8,2,32,384]{3,2,1,0:T(8,128)(2,1)S(1)}, bf16[8,2,32,384]{3,2,1,0:T(8,128)(2,1)S(1)}, u32[]{:S(2)}, u32[]{:S(2)}) collective-permute-start(bf16[8,2,32,384]{3,2,1,0:T(8,128)(2,1)S(1)} %get-tuple-element.29), channel_id=1, source_target_pairs={{0,6},{2,0},{4,2},{6,4},{8,14},{10,8},{12,10},{14,12},{16,22},{18,... | collective-permute-start | bytes 1179656 | tf_op jit(solution)/shard_map/ppermute | solution.py:358
  24.5 16.7 %collective-permute-start.2 = (bf16[8,2,32,384]{3,2,1,0:T(8,128)(2,1)S(1)}, bf16[8,2,32,384]{3,2,1,0:T(8,128)(2,1)S(1)}, u32[]{:S(2)}, u32[]{:S(2)}) collective-permute-start(bf16[8,2,32,384]{3,2,1,0:T(8,128)(2,1)S(1)} %get-tuple-element.30), channel_id=1, source_target_pairs={{0,4},{2,6},{4,0},{6,2},{8,12},{10,14},{12,8},{14,10},{16,20},{18,... | collective-permute-start | bytes 1179656 | tf_op jit(solution)/shard_map/ppermute | solution.py:358
  24.8 20.6 %collective-permute-start.1 = (bf16[8,2,32,384]{3,2,1,0:T(8,128)(2,1)S(1)}, bf16[8,2,32,384]{3,2,1,0:T(8,128)(2,1)S(1)}, u32[]{:S(2)}, u32[]{:S(2)}) collective-permute-start(bf16[8,2,32,384]{3,2,1,0:T(8,128)(2,1)S(1)} %get-tuple-element.31), channel_id=1, source_target_pairs={{0,2},{2,4},{4,6},{6,0},{8,10},{10,12},{12,14},{14,8},{16,18},{18,... | collective-permute-start | bytes 1179656 | tf_op jit(solution)/shard_map/ppermute | solution.py:358
  47.2 115.2 %copy-start.7 = (s32[2,68,2]{1,2,0:T(2,128)S(1)}, s32[2,68,2]{1,2,0:T(2,128)}, u32[]{:S(2)}) copy-start(s32[2,68,2]{1,2,0:T(2,128)} %param.8) | copy-start | bytes 3268
  47.2 115.1 %copy-start.8 = (s32[4,2]{0,1:T(2,128)S(1)}, s32[4,2]{0,1:T(2,128)}, u32[]{:S(2)}) copy-start(s32[4,2]{0,1:T(2,128)} %param.7) | copy-start | bytes 100
  47.2 59.4 %collective-permute-start.4 = (bf16[4,4,2,32,384]{4,3,2,1,0:T(8,128)(2,1)S(1)}, bf16[4,4,2,32,384]{4,3,2,1,0:T(8,128)(2,1)S(1)}, u32[]{:S(2)}, u32[]{:S(2)}) collective-permute-start(bf16[4,4,2,32,384]{4,3,2,1,0:T(8,128)(2,1)S(1)} %shard_map.56), channel_id=1, source_target_pairs={{0,1},{1,0},{2,3},{3,2},{4,5},{5,4},{6,7},{7,6},{8,9},{9,8},{10,11... | collective-permute-start | bytes 2359304 | tf_op jit(solution)/shard_map/ppermute | solution.py:329
  50.6 19.7 %collective-permute-start.14 = (bf16[2,4,2,32,384]{4,3,2,1,0:T(8,128)(2,1)S(1)}, bf16[2,4,2,32,384]{4,3,2,1,0:T(8,128)(2,1)S(1)}, u32[]{:S(2)}, u32[]{:S(2)}) collective-permute-start(bf16[2,4,2,32,384]{4,3,2,1,0:T(8,128)(2,1)S(1)} %get-tuple-element.21), channel_id=1, source_target_pairs={{0,0},{1,9},{2,2},{3,11},{4,4},{5,13},{6,6},{7,15},{8,8},{9,1},{10... | collective-permute-start | bytes 1179656 | tf_op jit(solution)/shard_map/ppermute | solution.py:352
  54.2 40.0 %collective-permute-start.15 = (bf16[2,4,2,32,384]{4,3,2,1,0:T(8,128)(2,1)S(1)}, bf16[2,4,2,32,384]{4,3,2,1,0:T(8,128)(2,1)S(1)}, u32[]{:S(2)}, u32[]{:S(2)}) collective-permute-start(bf16[2,4,2,32,384]{4,3,2,1,0:T(8,128)(2,1)S(1)} %get-tuple-element.22), channel_id=1, source_target_pairs={{0,16},{1,25},{2,18},{3,27},{4,20},{5,29},{6,22},{7,31},{8,24},{9,... | collective-permute-start | bytes 1179656 | tf_op jit(solution)/shard_map/ppermute | solution.py:352
  59.7 38.3 %collective-permute-start.16 = (bf16[2,4,2,32,384]{4,3,2,1,0:T(8,128)(2,1)S(1)}, bf16[2,4,2,32,384]{4,3,2,1,0:T(8,128)(2,1)S(1)}, u32[]{:S(2)}, u32[]{:S(2)}) collective-permute-start(bf16[2,4,2,32,384]{4,3,2,1,0:T(8,128)(2,1)S(1)} %get-tuple-element.23), channel_id=1, source_target_pairs={{0,32},{1,41},{2,34},{3,43},{4,36},{5,45},{6,38},{7,47},{8,40},{9,... | collective-permute-start | bytes 1179656 | tf_op jit(solution)/shard_map/ppermute | solution.py:352
  68.3 32.6 %collective-permute-start.17 = (bf16[2,4,2,32,384]{4,3,2,1,0:T(8,128)(2,1)S(1)}, bf16[2,4,2,32,384]{4,3,2,1,0:T(8,128)(2,1)S(1)}, u32[]{:S(2)}, u32[]{:S(2)}) collective-permute-start(bf16[2,4,2,32,384]{4,3,2,1,0:T(8,128)(2,1)S(1)} %get-tuple-element.24), channel_id=1, source_target_pairs={{0,48},{1,57},{2,50},{3,59},{4,52},{5,61},{6,54},{7,63},{8,56},{9,... | collective-permute-start | bytes 1179656 | tf_op jit(solution)/shard_map/ppermute | solution.py:352
  103.8 18.0 %collective-permute-start.18 = (bf16[8,2,32,384]{3,2,1,0:T(8,128)(2,1)S(1)}, bf16[8,2,32,384]{3,2,1,0:T(8,128)(2,1)S(1)}, u32[]{:S(2)}, u32[]{:S(2)}) collective-permute-start(bf16[8,2,32,384]{3,2,1,0:T(8,128)(2,1)S(1)} %get-tuple-element.26), channel_id=1, source_target_pairs={{0,2},{2,4},{4,6},{6,0},{8,10},{10,12},{12,14},{14,8},{16,18},{18,... | collective-permute-start | bytes 1179656 | tf_op jit(solution)/shard_map/ppermute | solution.py:358
  103.9 19.8 %collective-permute-start.19 = (bf16[8,2,32,384]{3,2,1,0:T(8,128)(2,1)S(1)}, bf16[8,2,32,384]{3,2,1,0:T(8,128)(2,1)S(1)}, u32[]{:S(2)}, u32[]{:S(2)}) collective-permute-start(bf16[8,2,32,384]{3,2,1,0:T(8,128)(2,1)S(1)} %get-tuple-element.27), channel_id=1, source_target_pairs={{0,4},{2,6},{4,0},{6,2},{8,12},{10,14},{12,8},{14,10},{16,20},{18,... | collective-permute-start | bytes 1179656 | tf_op jit(solution)/shard_map/ppermute | solution.py:358
  105.4 22.0 %collective-permute-start.20 = (bf16[8,2,32,384]{3,2,1,0:T(8,128)(2,1)S(1)}, bf16[8,2,32,384]{3,2,1,0:T(8,128)(2,1)S(1)}, u32[]{:S(2)}, u32[]{:S(2)}) collective-permute-start(bf16[8,2,32,384]{3,2,1,0:T(8,128)(2,1)S(1)} %get-tuple-element.28), channel_id=1, source_target_pairs={{0,6},{2,0},{4,2},{6,4},{8,14},{10,8},{12,10},{14,12},{16,22},{18,... | collective-permute-start | bytes 1179656 | tf_op jit(solution)/shard_map/ppermute | solution.py:358
  106.6 23.9 %collective-permute-start.21 = (bf16[8,2,32,384]{3,2,1,0:T(8,128)(2,1)S(1)}, bf16[8,2,32,384]{3,2,1,0:T(8,128)(2,1)S(1)}, u32[]{:S(2)}, u32[]{:S(2)}) collective-permute-start(bf16[8,2,32,384]{3,2,1,0:T(8,128)(2,1)S(1)} %get-tuple-element.25.refs_0_), channel_id=1, source_target_pairs={{0,1},{1,0},{2,3},{3,2},{4,5},{5,4},{6,7},{7,6},{8,9},{9,8},{10,11... | collective-permute-start | bytes 1179656 | tf_op jit(solution)/shard_map/ppermute | solution.py:329
  109.4 22.9 %collective-permute-start.5 = (bf16[2,4,2,32,384]{4,3,2,1,0:T(8,128)(2,1)S(1)}, bf16[2,4,2,32,384]{4,3,2,1,0:T(8,128)(2,1)S(1)}, u32[]{:S(2)}, u32[]{:S(2)}) collective-permute-start(bf16[2,4,2,32,384]{4,3,2,1,0:T(8,128)(2,1)S(1)} %get-tuple-element.17), channel_id=1, source_target_pairs={{0,0},{1,9},{2,2},{3,11},{4,4},{5,13},{6,6},{7,15},{8,8},{9,1},{10... | collective-permute-start | bytes 1179656 | tf_op jit(solution)/shard_map/ppermute | solution.py:352
  121.8 34.8 %collective-permute-start.6 = (bf16[2,4,2,32,384]{4,3,2,1,0:T(8,128)(2,1)S(1)}, bf16[2,4,2,32,384]{4,3,2,1,0:T(8,128)(2,1)}, u32[]{:S(2)}, u32[]{:S(2)}) collective-permute-start(bf16[2,4,2,32,384]{4,3,2,1,0:T(8,128)(2,1)S(1)} %get-tuple-element.18), channel_id=1, source_target_pairs={{0,16},{1,25},{2,18},{3,27},{4,20},{5,29},{6,22},{7,31},{8,24},{9,... | collective-permute-start | bytes 1179656 | tf_op jit(solution)/shard_map/ppermute | solution.py:352
  123.8 32.9 %collective-permute-start.7 = (bf16[2,4,2,32,384]{4,3,2,1,0:T(8,128)(2,1)S(1)}, bf16[2,4,2,32,384]{4,3,2,1,0:T(8,128)(2,1)}, u32[]{:S(2)}, u32[]{:S(2)}) collective-permute-start(bf16[2,4,2,32,384]{4,3,2,1,0:T(8,128)(2,1)S(1)} %get-tuple-element.19), channel_id=1, source_target_pairs={{0,32},{1,41},{2,34},{3,43},{4,36},{5,45},{6,38},{7,47},{8,40},{9,... | collective-permute-start | bytes 1179656 | tf_op jit(solution)/shard_map/ppermute | solution.py:352
  127.5 34.2 %collective-permute-start.8 = (bf16[2,4,2,32,384]{4,3,2,1,0:T(8,128)(2,1)S(1)}, bf16[2,4,2,32,384]{4,3,2,1,0:T(8,128)(2,1)}, u32[]{:S(2)}, u32[]{:S(2)}) collective-permute-start(bf16[2,4,2,32,384]{4,3,2,1,0:T(8,128)(2,1)S(1)} %get-tuple-element.20), channel_id=1, source_target_pairs={{0,48},{1,57},{2,50},{3,59},{4,52},{5,61},{6,54},{7,63},{8,56},{9,... | collective-permute-start | bytes 1179656 | tf_op jit(solution)/shard_map/ppermute | solution.py:352
  130.5 31.2 %collective-permute-start.22 = (bf16[8,2,32,384]{3,2,1,0:T(8,128)(2,1)S(1)}, bf16[8,2,32,384]{3,2,1,0:T(8,128)(2,1)S(1)}, u32[]{:S(2)}, u32[]{:S(2)}) collective-permute-start(bf16[8,2,32,384]{3,2,1,0:T(8,128)(2,1)S(1)} %collective-permute-done.18.refs_1_), channel_id=1, source_target_pairs={{0,1},{1,0},{2,3},{3,2},{4,5},{5,4},{6,7},{7,6},{8,9},{9,8},{10,11... | collective-permute-start | bytes 1179656 | tf_op jit(solution)/shard_map/ppermute | solution.py:329
  132.3 29.9 %collective-permute-start.23 = (bf16[8,2,32,384]{3,2,1,0:T(8,128)(2,1)S(1)}, bf16[8,2,32,384]{3,2,1,0:T(8,128)(2,1)S(1)}, u32[]{:S(2)}, u32[]{:S(2)}) collective-permute-start(bf16[8,2,32,384]{3,2,1,0:T(8,128)(2,1)S(1)} %collective-permute-done.19.refs_2_), channel_id=1, source_target_pairs={{0,1},{1,0},{2,3},{3,2},{4,5},{5,4},{6,7},{7,6},{8,9},{9,8},{10,11... | collective-permute-start | bytes 1179656 | tf_op jit(solution)/shard_map/ppermute | solution.py:329
  156.7 5.7 %collective-permute-start.24 = (bf16[8,2,32,384]{3,2,1,0:T(8,128)(2,1)S(1)}, bf16[8,2,32,384]{3,2,1,0:T(8,128)(2,1)S(1)}, u32[]{:S(2)}, u32[]{:S(2)}) collective-permute-start(bf16[8,2,32,384]{3,2,1,0:T(8,128)(2,1)S(1)} %collective-permute-done.20.refs_3_), channel_id=1, source_target_pairs={{0,1},{1,0},{2,3},{3,2},{4,5},{5,4},{6,7},{7,6},{8,9},{9,8},{10,11... | collective-permute-start | bytes 1179656 | tf_op jit(solution)/shard_map/ppermute | solution.py:329
  156.7 15.3 %collective-permute-start.9 = (bf16[2,4,2,32,384]{4,3,2,1,0:T(8,128)(2,1)S(1)}, bf16[2,4,2,32,384]{4,3,2,1,0:T(8,128)(2,1)}, u32[]{:S(2)}, u32[]{:S(2)}) collective-permute-start(bf16[2,4,2,32,384]{4,3,2,1,0:T(8,128)(2,1)S(1)} %collective-permute-done.5.refs_0_), channel_id=1, source_target_pairs={{0,1},{1,0},{2,3},{3,2},{4,5},{5,4},{6,7},{7,6},{8,9},{9,8},{10,11... | collective-permute-start | bytes 1179656 | tf_op jit(solution)/shard_map/ppermute | solution.py:329
  161.6 10.3 %collective-permute-start.10 = (bf16[2,4,2,32,384]{4,3,2,1,0:T(8,128)(2,1)}, bf16[2,4,2,32,384]{4,3,2,1,0:T(8,128)(2,1)}, u32[]{:S(2)}, u32[]{:S(2)}) collective-permute-start(bf16[2,4,2,32,384]{4,3,2,1,0:T(8,128)(2,1)} %collective-permute-done.6.refs_1_), channel_id=1, source_target_pairs={{0,1},{1,0},{2,3},{3,2},{4,5},{5,4},{6,7},{7,6},{8,9},{9,8},{10,11... | collective-permute-start | bytes 1179656 | tf_op jit(solution)/shard_map/ppermute | solution.py:329
  161.6 10.4 %collective-permute-start.11 = (bf16[2,4,2,32,384]{4,3,2,1,0:T(8,128)(2,1)}, bf16[2,4,2,32,384]{4,3,2,1,0:T(8,128)(2,1)}, u32[]{:S(2)}, u32[]{:S(2)}) collective-permute-start(bf16[2,4,2,32,384]{4,3,2,1,0:T(8,128)(2,1)} %collective-permute-done.7.refs_2_), channel_id=1, source_target_pairs={{0,1},{1,0},{2,3},{3,2},{4,5},{5,4},{6,7},{7,6},{8,9},{9,8},{10,11... | collective-permute-start | bytes 1179656 | tf_op jit(solution)/shard_map/ppermute | solution.py:329
  162.2 9.9 %collective-permute-start.12 = (bf16[2,4,2,32,384]{4,3,2,1,0:T(8,128)(2,1)}, bf16[2,4,2,32,384]{4,3,2,1,0:T(8,128)(2,1)}, u32[]{:S(2)}, u32[]{:S(2)}) collective-permute-start(bf16[2,4,2,32,384]{4,3,2,1,0:T(8,128)(2,1)} %collective-permute-done.8.refs_3_), channel_id=1, source_target_pairs={{0,1},{1,0},{2,3},{3,2},{4,5},{5,4},{6,7},{7,6},{8,9},{9,8},{10,11... | collective-permute-start | bytes 1179656 | tf_op jit(solution)/shard_map/ppermute | solution.py:329
